TPU v7x, 32 devices: a whole 2x2x4 slice. The times are simulated.
32 devices in a mesh: groups: 2 (over x), aa: 8 (over z, y), ba: 2 (over core).
Axes of the slice: x: 2, y: 2, z: 4, core: 2. Of those that a mesh axis runs over, the one named last changes fastest.
Arguments:
- video: bfloat16 [128, 8, 32, 512], P('groups', 'aa', 'ba'), parts along dimension 0, may hold values from -6 to 6
- norm_gain: float32 [3, 512], replicated, may hold values from 0.1 to 1.9
- qkv_weight: bfloat16 [3, 512, 1536], replicated, may hold values from -8 to 8
- out_weight: bfloat16 [3, 512, 512], replicated, may hold values from -0.25 to 0.25
Outputs:
- result: bfloat16 [128, 8, 32, 512], P('groups', 'aa', 'ba'), parts along dimension 0
There are 2 independent parts, one for each index of `groups`. A program takes and returns all parts, laid end to end along the dimension named above; an argument that names none is the same for every part. Nothing has to cross between parts.
All inputs are finite; a program needn't handle non-finite values.
Results may differ from a plain program's by a relative error of at most 0.014.
Values may be sent and summed in bfloat16 or wider, within the bound.
No kernel may reach another device: no remote copies, remote signals or barrier semaphores. Data moves between devices by JAX's collectives and lax.ppermute only.
A program may use at most 64 MiB of HBM per device.

v0:
```python
import functools
import math

import jax
import jax.numpy as jnp
from jax import lax
from jax.experimental import pallas as pl
from jax.experimental.pallas import tpu as pltpu
from jax.sharding import PartitionSpec as P


HEADS = 8
HEAD_DIM = 64
EPS = 1e-06
LANES = 128
HIDDEN = -1e30


score_forms = ("sbcnd,tbcnd->bcnst", "ascnd,atcnd->acnst", "absnd,abtnd->abnst")
mix_forms = ("bcnst,tbcnd->sbcnd", "acnst,atcnd->ascnd", "abnst,abtnd->absnd")


def attend(queries, key_rows, value_rows, line):
    shape = queries.shape
    split = shape[:3] + (HEADS, HEAD_DIM)
    scores = jnp.einsum(
        score_forms[line],
        queries.reshape(split),
        key_rows.reshape(split),
        preferred_element_type=jnp.float32,
    ) * (1.0 / math.sqrt(HEAD_DIM))
    weights = jax.nn.softmax(scores, axis=-1).astype(jnp.bfloat16)
    mixed = jnp.einsum(
        mix_forms[line], weights, value_rows.reshape(split), preferred_element_type=jnp.float32
    )
    return mixed.astype(jnp.bfloat16).reshape(shape)


def full_block(state, gain, weight_in, weight_out, line):
    floats = state.astype(jnp.float32)
    meansq = jnp.mean(floats * floats, axis=-1, keepdims=True)
    normed = (floats * lax.rsqrt(meansq + EPS) * gain).astype(jnp.bfloat16)
    packed = jnp.dot(normed, weight_in, preferred_element_type=jnp.float32).astype(jnp.bfloat16)
    width = state.shape[-1]
    mixed = attend(
        packed[..., :width], packed[..., width : 2 * width], packed[..., 2 * width :], line
    )
    update = jnp.dot(mixed, weight_out, preferred_element_type=jnp.float32)
    return (floats + update).astype(jnp.bfloat16)


def general_body(video, norm_gain, qkv_weight, out_weight):
    state = full_block(video, norm_gain[0], qkv_weight[0], out_weight[0], 0)
    state = lax.all_to_all(state, "aa", split_axis=0, concat_axis=1, tiled=True)
    state = full_block(state, norm_gain[1], qkv_weight[1], out_weight[1], 1)
    state = lax.all_to_all(state, "ba", split_axis=1, concat_axis=2, tiled=True)
    state = full_block(state, norm_gain[2], qkv_weight[2], out_weight[2], 2)
    state = lax.all_to_all(state, "ba", split_axis=2, concat_axis=1, tiled=True)
    return lax.all_to_all(state, "aa", split_axis=1, concat_axis=0, tiled=True)


def normalise(floats, gain):
    meansq = jnp.mean(floats * floats, axis=-1, keepdims=True)
    return (floats * lax.rsqrt(meansq + EPS) * gain).astype(jnp.bfloat16)


def lane_halves(tokens):
    left = lax.broadcasted_iota(jnp.int32, (tokens, LANES), 1) < HEAD_DIM
    left = left.astype(jnp.float32)
    return left.astype(jnp.bfloat16), (1 - left).astype(jnp.bfloat16)


def tile_attention(packed, same_line, halves):
    tokens, width = packed.shape[0], packed.shape[1] // 3
    left, right = halves
    pieces = []
    for at in range(0, width, LANES):
        q = packed[:, at : at + LANES]
        k = packed[:, width + at : width + at + LANES]
        v = packed[:, 2 * width + at : 2 * width + at + LANES]
        scores = lax.dot_general(
            q,
            jnp.concatenate([k * left, k * right], axis=0),
            (((1,), (1,)), ((), ())),
            preferred_element_type=jnp.float32,
        )
        weights = []
        for head in range(2):
            own = jnp.where(same_line, scores[:, head * tokens : (head + 1) * tokens], HIDDEN)
            top = jnp.max(own, axis=-1, keepdims=True)
            weights.append(jnp.exp2(own - top).astype(jnp.bfloat16))
        values = jnp.concatenate(
            [
                jnp.concatenate([v * left, left], axis=1),
                jnp.concatenate([v * right, right], axis=1),
            ],
            axis=0,
        )
        mixed = jnp.dot(
            jnp.concatenate(weights, axis=1), values, preferred_element_type=jnp.float32
        )
        pieces.append((mixed[:, :LANES] / mixed[:, LANES:]).astype(jnp.bfloat16))
    return jnp.concatenate(pieces, axis=1)


def line_mask(tokens, line_of):
    rows = lax.broadcasted_iota(jnp.int32, (tokens, tokens), 0)
    columns = lax.broadcasted_iota(jnp.int32, (tokens, tokens), 1)
    return line_of(rows) == line_of(columns)


def project(normed, weight_ref, packed_ref, at):
    rows, width = normed.shape
    result = jnp.dot(normed, weight_ref[...], preferred_element_type=jnp.float32)
    scale = math.log2(math.e) / math.sqrt(HEAD_DIM)
    packed_ref[at : at + rows, :width] = (result[:, :width] * scale).astype(jnp.bfloat16)
    packed_ref[at : at + rows, width:] = result[:, width:].astype(jnp.bfloat16)


def lanes_of(value):
    return [value[:, at : at + LANES] for at in range(0, value.shape[1], LANES)]


def strided(ref, start, size, stride):
    return jnp.concatenate(
        [ref[at, pl.ds(start, size, stride=stride), :] for at in range(ref.shape[0])], axis=1
    )


def first_kernel(block, me_ref, x_hbm, gain_hbm, win_hbm, wout_hbm, *rest):
    n = len(rest) - 9
    outs = rest[:n]
    win, wout, natural, lined, packed, mixed, sems, x_ref, gain_ref = rest[n:]
    frames, columns, width = x_ref.shape
    tokens = frames * columns
    loads = [
        pltpu.make_async_copy(source, target, sems.at[index])
        for index, (source, target) in enumerate(
            (
                (x_hbm, x_ref),
                (gain_hbm, gain_ref),
                (win_hbm.at[block], win),
                (wout_hbm.at[block], wout),
            )
        )
    ]
    for load in loads:
        load.start()
    loads[0].wait()
    loads[1].wait()
    for at, lanes in enumerate(lanes_of(x_ref[...].reshape(tokens, width).astype(jnp.float32))):
        natural[at] = lanes
    gain = gain_ref[block : block + 1]
    group = 256 // frames
    for column in range(0, columns, group):
        pieces = []
        for each in range(column, column + group):
            floats = strided(natural, each, frames, columns)
            for at, lanes in enumerate(lanes_of(floats)):
                lined[at, each * frames : (each + 1) * frames] = lanes
            pieces.append(normalise(floats, gain))
        if column == 0:
            loads[2].wait()
        project(jnp.concatenate(pieces, axis=0), win, packed, column * frames)
    mask = line_mask(LANES, lambda i: i // frames)
    halves = lane_halves(LANES)
    for at in range(0, tokens, LANES):
        mixed[at : at + LANES] = tile_attention(packed[at : at + LANES], mask, halves)
    loads[3].wait()
    for at in range(0, tokens, 256):
        update = jnp.dot(mixed[at : at + 256], wout[...], preferred_element_type=jnp.float32)
        for index, lanes in enumerate(lanes_of(update)):
            lined[index, at : at + 256] += lanes
    piece = frames // n
    for k in range(n):
        start = jnp.bitwise_xor(me_ref[0], k) * piece
        for frame in range(piece):
            outs[k][frame] = strided(lined, start + frame, columns, frames).astype(jnp.bfloat16)


def load_all(pairs, sems):
    loads = [
        pltpu.make_async_copy(source, target, sems.at[index])
        for index, (source, target) in enumerate(pairs)
    ]
    for load in loads:
        load.start()
    return loads


def prepare(refs, gain, win, packed_ref, at):
    pieces, start, count = [], at, 0
    for index, ref in enumerate(refs):
        floats = ref[...].reshape(-1, ref.shape[-1]).astype(jnp.float32)
        pieces.append(normalise(floats, gain))
        count += floats.shape[0]
        if count >= 256 or index == len(refs) - 1:
            normed = jnp.concatenate(pieces, axis=0) if len(pieces) > 1 else pieces[0]
            project(normed, win, packed_ref, start)
            pieces, start, count = [], start + count, 0


def early_kernel(block, count, *rest):
    ins, (gain_hbm, win_hbm, wout_hbm) = rest[:count], rest[count : count + 3]
    packed, win, wout, gain_ref, sems = rest[count + 3 :]
    loads = load_all(
        ((gain_hbm, gain_ref), (win_hbm.at[block], win), (wout_hbm.at[block], wout)), sems
    )
    loads[0].wait()
    loads[1].wait()
    prepare(ins, gain_ref[block : block + 1], win, packed, 0)
    loads[2].wait()


def late_kernel(block, count, *rest):
    ins, (gain_ref, win, win_hbm, wout_hbm, packed, next_win, next_wout, sems) = (
        rest[:count],
        rest[count:],
    )
    loads = load_all(
        ((win_hbm.at[block + 1], next_win), (wout_hbm.at[block + 1], next_wout)), sems
    )
    prepare(ins, gain_ref[block : block + 1], win, packed, 0)
    for load in loads:
        load.wait()


def share_rows(core_ref, update, ins, keep, give):
    frames, columns, width = ins[0].shape
    per = frames * columns
    totals = [
        (ins[each][...].reshape(per, width).astype(jnp.float32) + update[each * per : (each + 1) * per])
        .astype(jnp.bfloat16)
        .reshape(frames, columns, width)
        for each in range(2)
    ]
    second = core_ref[0]

    @pl.when(second == 0)
    def _():
        keep[...] = totals[0]
        give[...] = totals[1]

    @pl.when(second != 0)
    def _():
        keep[...] = totals[1]
        give[...] = totals[0]


def middle_kernel(block, counts, pair, core_ref, *rest):
    n = sum(counts)
    ins = rest[:n]
    groups = rest[n : n + len(counts) - 1]
    gain_ref, win, wout, mixed, keep_ref, give_ref, packed = rest[n + len(counts) - 1 :]
    frames, columns, _ = ins[0].shape
    per = columns * frames
    last = n - counts[-1]
    prepare(ins[last:], gain_ref[block : block + 1], win, packed, 0)
    homes = []
    for group, count in zip((*groups, packed), counts):
        homes += [(group, index * per) for index in range(count)]
    share = LANES // n
    mask = line_mask(LANES, lambda i: i % share)
    halves = lane_halves(LANES)
    for at in range(0, per, share):
        tile = jnp.concatenate(
            [group[start + at : start + at + share] for group, start in homes], axis=0
        )
        result = tile_attention(tile, mask, halves)
        for k in range(n):
            mixed[k * per + at : k * per + at + share] = result[k * share : (k + 1) * share]
    k = 2 * pair
    update = jnp.dot(mixed[k * per : (k + 2) * per], wout[...], preferred_element_type=jnp.float32)
    share_rows(core_ref, update, ins[k : k + 2], keep_ref.at[0], give_ref.at[0])


def middle_rest_kernel(pairs, core_ref, mixed, wout, *rest):
    ins = rest[: 2 * len(pairs)]
    keep_ref, give_ref = rest[2 * len(pairs) :]
    frames, columns, _ = ins[0].shape
    per = columns * frames
    for index, pair in enumerate(pairs):
        k = 2 * pair
        update = jnp.dot(
            mixed[k * per : (k + 2) * per], wout[...], preferred_element_type=jnp.float32
        )
        share_rows(
            core_ref,
            update,
            ins[2 * index : 2 * index + 2],
            keep_ref.at[index],
            give_ref.at[index],
        )


def kept_kernel(block, keep_ref, gain_ref, win, packed):
    prepare(
        [keep_ref.at[row] for row in range(keep_ref.shape[0])],
        gain_ref[block : block + 1],
        win,
        packed,
        0,
    )


def last_kernel(block, rows, keep_ref, got_ref, kept_packed, gain_ref, win, wout, *rest):
    outs = rest[: 2 * len(rows)]
    packed, mixed = rest[2 * len(rows) :]
    _, frames, columns, width = keep_ref.shape
    per = frames * columns
    tile = 2 * per
    gain = gain_ref[block : block + 1]
    prepare([got_ref.at[row] for row in rows], gain, win, packed, 0)
    mask = line_mask(LANES, lambda i: i // (2 * columns))
    halves = lane_halves(LANES)
    for index, row in enumerate(rows):
        for at in range(0, per, LANES // 2):
            strips = []
            for each in range(at, at + LANES // 2, columns):
                strips.append(kept_packed[row * per + each : row * per + each + columns])
                strips.append(packed[index * per + each : index * per + each + columns])
            start = index * tile + 2 * at
            mixed[start : start + LANES] = tile_attention(
                jnp.concatenate(strips, axis=0), mask, halves
            )
    for index, row in enumerate(rows):
        update = jnp.dot(
            mixed[index * tile : (index + 1) * tile],
            wout[...],
            preferred_element_type=jnp.float32,
        ).reshape(frames, 2 * columns, width)
        for half, ref in enumerate((keep_ref, got_ref)):
            outs[2 * index + half][...] = (
                ref[row].astype(jnp.float32) + update[:, half * columns : (half + 1) * columns]
            ).astype(jnp.bfloat16)


def join_kernel(count, starts_ref, *rest):
    pieces, out, sems = rest[:count], rest[-2], rest[-1]
    size = pieces[0].shape[0]
    copies = []
    for index, piece in enumerate(pieces):
        where = pl.ds(starts_ref[index] * size, size)
        copies.append(pltpu.make_async_copy(piece, out.at[where], sems.at[index]))
        copies[-1].start()
    for copy in copies:
        copy.wait()


SMEM = pl.BlockSpec(memory_space=pltpu.SMEM)
VMEM = pl.BlockSpec(memory_space=pltpu.VMEM)
HBM = pl.BlockSpec(memory_space=pltpu.HBM)


def call(kernel, outs, in_specs, scratch_shapes, limit=24):
    return pl.pallas_call(
        kernel,
        out_shape=outs,
        in_specs=in_specs,
        out_specs=[VMEM] * len(outs),
        scratch_shapes=scratch_shapes,
        compiler_params=pltpu.CompilerParams(vmem_limit_bytes=limit << 20),
    )


def fast_body(n, video, norm_gain, qkv_weight, out_weight):
    frames, _, columns, width = video.shape
    piece = frames // n
    per = piece * columns
    tokens = frames * columns
    spot = lax.axis_index("aa")
    core = lax.axis_index("ba")
    bf16, f32 = jnp.bfloat16, jnp.float32
    array = jax.ShapeDtypeStruct
    message = array((piece, columns, width), bf16)
    win_shape, wout_shape = (width, 3 * width), (width, width)
    gain_shape = norm_gain.shape
    local = pltpu.with_memory_space_constraint(
        video.reshape(frames, columns, width), pltpu.HBM
    )
    weights = tuple(
        pltpu.with_memory_space_constraint(w, pltpu.HBM)
        for w in (norm_gain, qkv_weight, out_weight)
    )

    sent = call(
        functools.partial(first_kernel, 0),
        [message] * n,
        [SMEM, HBM, HBM, HBM, HBM],
        [
            pltpu.VMEM(win_shape, bf16),
            pltpu.VMEM(wout_shape, bf16),
            pltpu.VMEM((width // LANES, tokens, LANES), f32),
            pltpu.VMEM((width // LANES, tokens, LANES), f32),
            pltpu.VMEM((tokens, 3 * width), bf16),
            pltpu.VMEM((tokens, width), bf16),
            pltpu.SemaphoreType.DMA((4,)),
            pltpu.VMEM((frames, columns, width), bf16),
            pltpu.VMEM(gain_shape, f32),
        ],
    )(spot[None], local, *weights)

    came = {0: sent[0]}
    for k in range(1, n):
        came[k] = lax.ppermute(sent[k], "aa", [(i, i ^ k) for i in range(n)])

    half, quarter = n // 2, n // 4
    final = n - half - quarter
    packed_early, win, wout, gain = call(
        functools.partial(early_kernel, 1, half),
        [
            array((half * per, 3 * width), bf16),
            array(win_shape, bf16),
            array(wout_shape, bf16),
            array(gain_shape, f32),
        ],
        [VMEM] * half + [HBM, HBM, HBM],
        [pltpu.SemaphoreType.DMA((3,))],
    )(*[came[k] for k in range(half)], *weights)
    packed_late, next_win, next_wout = call(
        functools.partial(late_kernel, 1, quarter),
        [array((quarter * per, 3 * width), bf16), array(win_shape, bf16), array(wout_shape, bf16)],
        [VMEM] * (quarter + 2) + [HBM, HBM],
        [pltpu.SemaphoreType.DMA((2,))],
    )(*[came[k] for k in range(half, half + quarter)], gain, win, *weights[1:])

    lead, *others = row_order(n)

    def kept(count):
        return array((count, piece, columns, width), bf16)

    mixed, keep, give = call(
        functools.partial(middle_kernel, 1, (half, quarter, final), lead),
        [array((tokens, width), bf16), kept(1), kept(1)],
        [SMEM] + [VMEM] * (n + 5),
        [pltpu.VMEM((final * per, 3 * width), bf16)],
    )(core[None], *[came[k] for k in range(n)], packed_early, packed_late, gain, win, wout)

    arrived, starts = [], []

    def swap(value):
        return lax.ppermute(value, "ba", [(0, 1), (1, 0)])

    def project_kept(value):
        count = value.shape[0]
        (packed,) = call(
            functools.partial(kept_kernel, 2),
            [array((count * per, 3 * width), bf16)],
            [VMEM] * 3,
            [],
        )(value, gain, next_win)
        return packed

    def finish(rows, pairs_of_rows, value, other, packed):
        results = call(
            functools.partial(last_kernel, 2, rows),
            [message] * (2 * len(rows)),
            [VMEM] * 6,
            [
                pltpu.VMEM((len(rows) * per, 3 * width), bf16),
                pltpu.VMEM((len(rows) * 2 * per, width), bf16),
            ],
        )(value, other, packed, gain, next_win, next_wout)
        for index, row in enumerate(pairs_of_rows):
            for flip in range(2):
                route = [
                    (2 * a + b, 2 * (a ^ (2 * row + b)) + (b ^ flip))
                    for a in range(n)
                    for b in range(2)
                ]
                arrived.append(lax.ppermute(results[2 * index + flip], ("aa", "ba"), route))
                starts.append(jnp.bitwise_xor(spot, 2 * row + jnp.bitwise_xor(core, flip)))

    got = swap(give)
    finish([0], [lead], keep, got, project_kept(keep))

    keep, give = call(
        functools.partial(middle_rest_kernel, others),
        [kept(len(others)), kept(len(others))],
        [SMEM] + [VMEM] * (2 + 2 * len(others)),
        [],
    )(
        core[None],
        mixed,
        wout,
        *[came[2 * pair + each] for pair in others for each in range(2)],
    )
    got = swap(give)
    packed = project_kept(keep)
    cut = n // 4 - 1
    for rows in ([*range(cut)], [*range(cut, len(others))]):
        finish(rows, [others[row] for row in rows], keep, got, packed)

    def join(values, offsets, base=None):
        count = len(values)
        given = [] if base is None else [base]
        return pl.pallas_call(
            functools.partial(join_kernel, count),
            out_shape=array((frames, columns, width), bf16),
            in_specs=[SMEM] + [VMEM] * count + [HBM] * len(given),
            out_specs=HBM,
            scratch_shapes=[pltpu.SemaphoreType.DMA((count,))],
            input_output_aliases={count + 1: 0} if given else {},
            name="join",
            compiler_params=pltpu.CompilerParams(vmem_limit_bytes=4 << 20),
        )(jnp.stack(offsets).astype(jnp.int32), *values, *given)

    out = join(arrived[:2], starts[:2])
    out = join(arrived[2:], starts[2:], out)
    return out.reshape(video.shape)


def body(n, cores, video, norm_gain, qkv_weight, out_weight):
    frames, rows, columns, width = video.shape
    piece = frames // n
    fast = (
        cores == 2
        and rows == 1
        and n % 4 == 0
        and n & (n - 1) == 0
        and LANES % n == 0
        and (LANES // n) % 16 == 0
        and frames % n == 0
        and LANES % frames == 0
        and frames % 8 == 0
        and columns % 16 == 0
        and LANES % (2 * columns) == 0
        and (columns * piece) % LANES == 0
        and (frames * columns) % 256 == 0
        and width == HEADS * HEAD_DIM
        and width % LANES == 0
    )
    if fast:
        return fast_body(n, video, norm_gain, qkv_weight, out_weight)
    return general_body(video, norm_gain, qkv_weight, out_weight)


def row_order(n):
    return [*range(n // 4, n // 2), *range(n // 4 - 1, -1, -1)]


def solution(mesh):
    n = mesh.shape["aa"]
    return jax.shard_map(
        functools.partial(body, n, mesh.shape["ba"]),
        mesh=mesh,
        in_specs=(P("groups", "aa", "ba", None), P(), P(), P()),
        out_specs=P("groups", "aa", "ba", None),
        check_vma=False,
    )
```

profile of v0, /device:TPU:0, one launch (start us, length us, event | category | flops | bytes accessed | tf_op | source)
XLA Modules:
  0.0 72.2 jit_solution(18020139598495546863)
XLA Ops:
  0.0 7.6 %shard_map.46 = (bf16[8,16,512]{2,1,0:T(8,128)(2,1)S(1)}, bf16[8,16,512]{2,1,0:T(8,128)(2,1)S(1)}, bf16[8,16,512]{2,1,0:T(8,128)(2,1)S(1)}, bf16[8,16,512]{2,1,0...) custom-call(s32[1]{0:T(128)} %bitcast.7.me_ref, ...), custom_call_target="tpu_custom_call" | custom-call | tf_op jit(solution)/shard_map/pallas_call | solution.py:386
  7.6 3.1 %collective-permute-start = (bf16[8,16,512]{2,1,0:T(8,128)(2,1)S(1)}, bf16[8,16,512]{2,1,0:T(8,128)(2,1)S(1)}, u32[]{:S(2)}, u32[]{:S(2)}) collective-permute-start(bf16[8,16,512]{2,1,0:T(8,128)(2,1)S(1)} %get-tuple-element.34), channel_id=1, source_target_pairs={{0,2},{2,0},{4,6},{6,4},{8,10},{10,8},{12,14},{14,12},{1,3},{3,1},... | collective-permute-start | bytes 393224 | tf_op jit(solution)/shard_map/ppermute | solution.py:405
  10.6 1.6 %collective-permute-start.1 = (bf16[8,16,512]{2,1,0:T(8,128)(2,1)S(1)}, bf16[8,16,512]{2,1,0:T(8,128)(2,1)S(1)}, u32[]{:S(2)}, u32[]{:S(2)}) collective-permute-start(bf16[8,16,512]{2,1,0:T(8,128)(2,1)S(1)} %get-tuple-element.35), channel_id=1, source_target_pairs={{0,4},{2,6},{4,0},{6,2},{8,12},{10,14},{12,8},{14,10},{1,5},{3,7},... | collective-permute-start | bytes 393224 | tf_op jit(solution)/shard_map/ppermute | solution.py:405
  12.2 0.0 collective-permute-start.2
  12.2 3.0 %collective-permute-start.3 = (bf16[8,16,512]{2,1,0:T(8,128)(2,1)S(1)}, bf16[8,16,512]{2,1,0:T(8,128)(2,1)S(1)}, u32[]{:S(2)}, u32[]{:S(2)}) collective-permute-start(bf16[8,16,512]{2,1,0:T(8,128)(2,1)S(1)} %get-tuple-element.37), channel_id=1, source_target_pairs={{0,8},{2,10},{4,12},{6,14},{8,0},{10,2},{12,4},{14,6},{1,9},{3,11}... | collective-permute-start | bytes 393224 | tf_op jit(solution)/shard_map/ppermute | solution.py:405
  15.2 1.3 %collective-permute-start.4 = (bf16[8,16,512]{2,1,0:T(8,128)(2,1)S(1)}, bf16[8,16,512]{2,1,0:T(8,128)(2,1)S(1)}, u32[]{:S(2)}, u32[]{:S(2)}) collective-permute-start(bf16[8,16,512]{2,1,0:T(8,128)(2,1)S(1)} %get-tuple-element.38), channel_id=1, source_target_pairs={{0,10},{2,8},{4,14},{6,12},{8,2},{10,0},{12,6},{14,4},{1,11},{3,9}... | collective-permute-start | bytes 393224 | tf_op jit(solution)/shard_map/ppermute | solution.py:405
  16.5 0.0 collective-permute-done.rest_1_.rest_5_
  16.5 3.6 %collective-permute-start.5 = (bf16[8,16,512]{2,1,0:T(8,128)(2,1)S(1)}, bf16[8,16,512]{2,1,0:T(8,128)(2,1)S(1)}, u32[]{:S(2)}, u32[]{:S(2)}) collective-permute-start(bf16[8,16,512]{2,1,0:T(8,128)(2,1)S(1)} %get-tuple-element.39), channel_id=1, source_target_pairs={{0,12},{2,14},{4,8},{6,10},{8,4},{10,6},{12,0},{14,2},{1,13},{3,15... | collective-permute-start | bytes 393224 | tf_op jit(solution)/shard_map/ppermute | solution.py:405
  20.1 1.3 %collective-permute-done.1.rest_2_ = bf16[8,16,512]{2,1,0:T(8,128)(2,1)S(1)} collective-permute-done((bf16[8,16,512]{2,1,0:T(8,128)(2,1)S(1)}, bf16[8,16,512]{2,1,0:T(8,128)(2,1)S(1)}, u32[]{:S(2)}, u32[]{:S(2)}) %collective-permute-start.1) | collective-permute-done | bytes 131104 | tf_op jit(solution)/shard_map/ppermute | solution.py:405
  21.4 0.7 collective-permute-start.6
  22.1 0.0 collective-permute-done.2.rest_3_
  22.1 2.5 %shard_map.47 = (bf16[512,1536]{1,0:T(8,128)(2,1)S(1)}, bf16[512,1536]{1,0:T(8,128)(2,1)S(1)}, bf16[512,512]{1,0:T(8,128)(2,1)S(1)}, f32[3,512]{1,0:T(4,128)S(1)}) custom-call(bf16[8,16,512]{2,1,0:T(8,128)(2,1)S(1)} %get-tuple-element.33.rest_0_.rest_4_, bf16[8,16,512]{2,1,0:T(8,128)(2,1)S(1)} %collective-permute-done.rest_1_.rest_5_, ...), custom_call_target="tpu_custom_call" | custom-call | tf_op jit(solution)/shard_map/pallas_call | solution.py:409
  24.7 0.0 collective-permute-done.3.rest_0_.rest_4_
  24.7 10.0 %collective-permute-done.4.rest_1_.rest_5_ = bf16[8,16,512]{2,1,0:T(8,128)(2,1)S(1)} collective-permute-done((bf16[8,16,512]{2,1,0:T(8,128)(2,1)S(1)}, bf16[8,16,512]{2,1,0:T(8,128)(2,1)S(1)}, u32[]{:S(2)}, u32[]{:S(2)}) %collective-permute-start.4) | collective-permute-done | bytes 131104 | tf_op jit(solution)/shard_map/ppermute | solution.py:405
  34.6 2.0 %shard_map.48 = (bf16[256,1536]{1,0:T(8,128)(2,1)S(1)}, bf16[512,1536]{1,0:T(8,128)(2,1)S(1)}, bf16[512,512]{1,0:T(8,128)(2,1)S(1)}) custom-call(bf16[8,16,512]{2,1,0:T(8,128)(2,1)S(1)} %collective-permute-done.3.rest_0_.rest_4_, bf16[8,16,512]{2,1,0:T(8,128)(2,1)S(1)} %collective-permute-done.4.rest_1_.rest_5_, ...), custom_call_target="tpu_custom_call" | custom-call | tf_op jit(solution)/shard_map/pallas_call | solution.py:420
  36.6 0.0 collective-permute-done.5.rest_6_.rest_0_
  36.6 0.0 collective-permute-done.6.rest_7_.rest_1_
  36.7 2.3 %shard_map.49 = (bf16[1024,512]{1,0:T(8,128)(2,1)S(1)}, bf16[1,8,16,512]{3,2,1,0:T(8,128)(2,1)S(1)}, bf16[1,8,16,512]{3,2,1,0:T(8,128)(2,1)S(1)}) custom-call(s32[1]{0:T(128)} %bitcast.6.core_ref, bf16[8,16,512]{2,1,0:T(8,128)(2,1)S(1)} %get-tuple-element.33.rest_0_.rest_4_, bf16[8,16,512]{2,1,0:T(8,128)(2,1)S(1)} %collective-permute-done.rest_1_.rest_5_, ...), custom_call_target="tpu_custom_call" | custom-call | tf_op jit(solution)/shard_map/pallas_call | solution.py:432
  39.0 1.2 %shard_map.50 = (bf16[3,8,16,512]{3,2,1,0:T(8,128)(2,1)S(1)}, bf16[3,8,16,512]{3,2,1,0:T(8,128)(2,1)S(1)}) custom-call(s32[1]{0:T(128)} %bitcast.6.core_ref, bf16[1024,512]{1,0:T(8,128)(2,1)S(1)} %get-tuple-element.46.mixed, bf16[512,512]{1,0:T(8,128)(2,1)S(1)} %get-tuple-element.45.rest_12_.wout, ...), custom_call_target="tpu_custom_call" | custom-call | tf_op jit(solution)/shard_map/pallas_call | solution.py:477
  40.2 0.1 collective-permute-start.7
  40.2 0.5 collective-permute-start.14
  40.7 0.5 shard_map.54.kept_packed
  41.2 0.9 %shard_map.51.kept_packed = bf16[384,1536]{1,0:T(8,128)(2,1)S(1)} custom-call(bf16[3,8,16,512]{3,2,1,0:T(8,128)(2,1)S(1)} %get-tuple-element.47.keep_ref, f32[3,512]{1,0:T(4,128)S(1)} %get-tuple-element.42.rest_2_.rest_10_.gain_ref, bf16[512,1536]{1,0:T(8,128)(2,1)S(1)} %get-tuple-element.49.win), custom_call_target="tpu_custom_call" | custom-call | tf_op jit(solution)/shard_map/pallas_call | solution.py:446
  42.1 0.1 collective-permute-done.14.got_ref
  42.1 1.1 %shard_map.55 = (bf16[8,16,512]{2,1,0:T(8,128)(2,1)S(1)}, bf16[8,16,512]{2,1,0:T(8,128)(2,1)S(1)}) custom-call(bf16[1,8,16,512]{3,2,1,0:T(8,128)(2,1)S(1)} %get-tuple-element.57.keep_ref, bf16[1,8,16,512]{3,2,1,0:T(8,128)(2,1)S(1)} %collective-permute-done.14.got_ref, bf16[128,1536]{1,0:T(8,128)(2,1)S(1)} %shard_map.54.kept_packed, ...), custom_call_target="tpu_custom_call" | custom-call | tf_op jit(solution)/shard_map/pallas_call | solution.py:455
  43.3 4.6 %collective-permute-start.15 = (bf16[8,16,512]{2,1,0:T(8,128)(2,1)S(1)}, bf16[8,16,512]{2,1,0:T(8,128)(2,1)S(1)}, u32[]{:S(2)}, u32[]{:S(2)}) collective-permute-start(bf16[8,16,512]{2,1,0:T(8,128)(2,1)S(1)} %get-tuple-element.59), channel_id=1, source_target_pairs={{0,8},{1,11},{2,10},{3,9},{4,12},{5,15},{6,14},{7,13},{8,0},{9,3},... | collective-permute-start | bytes 393224 | tf_op jit(solution)/shard_map/ppermute | solution.py:471
  47.9 0.0 collective-permute-start.16
  47.9 0.0 collective-permute-done.7.got_ref
  47.9 1.8 %shard_map.53 = (bf16[8,16,512]{2,1,0:T(8,128)(2,1)S(1)}, bf16[8,16,512]{2,1,0:T(8,128)(2,1)S(1)}, bf16[8,16,512]{2,1,0:T(8,128)(2,1)S(1)}, bf16[8,16,512]{2,1,0:T(8,128)(2,1)S(1)}) custom-call(bf16[3,8,16,512]{3,2,1,0:T(8,128)(2,1)S(1)} %get-tuple-element.47.keep_ref, bf16[3,8,16,512]{3,2,1,0:T(8,128)(2,1)S(1)} %collective-permute-done.7.got_ref, ...), custom_call_target="tpu_custom_call" | custom-call | tf_op jit(solution)/shard_map/pallas_call | solution.py:455
  49.7 0.7 collective-permute-start.10
  50.4 1.8 %collective-permute-start.11 = (bf16[8,16,512]{2,1,0:T(8,128)(2,1)S(1)}, bf16[8,16,512]{2,1,0:T(8,128)(2,1)S(1)}, u32[]{:S(2)}, u32[]{:S(2)}) collective-permute-start(bf16[8,16,512]{2,1,0:T(8,128)(2,1)S(1)} %get-tuple-element.54), channel_id=1, source_target_pairs={{0,5},{1,6},{2,7},{3,4},{4,1},{5,2},{6,3},{7,0},{8,13},{9,14},{10,... | collective-permute-start | bytes 393224 | tf_op jit(solution)/shard_map/ppermute | solution.py:471
  52.2 0.7 collective-permute-start.12
  52.8 1.1 %shard_map.52 = (bf16[8,16,512]{2,1,0:T(8,128)(2,1)S(1)}, bf16[8,16,512]{2,1,0:T(8,128)(2,1)S(1)}) custom-call(bf16[3,8,16,512]{3,2,1,0:T(8,128)(2,1)S(1)} %get-tuple-element.47.keep_ref, bf16[3,8,16,512]{3,2,1,0:T(8,128)(2,1)S(1)} %collective-permute-done.7.got_ref, bf16[384,1536]{1,0:T(8,128)(2,1)S(1)} %shard_map.51.kept_packed, ...), custom_call_target="tpu_custom_call" | custom-call | tf_op jit(solution)/shard_map/pallas_call | solution.py:455
  54.0 3.9 %collective-permute-done.15.rest_0_ = bf16[8,16,512]{2,1,0:T(8,128)(2,1)S(1)} collective-permute-done((bf16[8,16,512]{2,1,0:T(8,128)(2,1)S(1)}, bf16[8,16,512]{2,1,0:T(8,128)(2,1)S(1)}, u32[]{:S(2)}, u32[]{:S(2)}) %collective-permute-start.15) | collective-permute-done | bytes 131104 | tf_op jit(solution)/shard_map/ppermute | solution.py:471
  57.8 0.0 collective-permute-start.13
  57.8 1.8 %collective-permute-done.16.rest_1_ = bf16[8,16,512]{2,1,0:T(8,128)(2,1)S(1)} collective-permute-done((bf16[8,16,512]{2,1,0:T(8,128)(2,1)S(1)}, bf16[8,16,512]{2,1,0:T(8,128)(2,1)S(1)}, u32[]{:S(2)}, u32[]{:S(2)}) %collective-permute-start.16) | collective-permute-done | bytes 131104 | tf_op jit(solution)/shard_map/ppermute | solution.py:471
  59.7 2.3 %collective-permute-start.8 = (bf16[8,16,512]{2,1,0:T(8,128)(2,1)S(1)}, bf16[8,16,512]{2,1,0:T(8,128)(2,1)S(1)}, u32[]{:S(2)}, u32[]{:S(2)}) collective-permute-start(bf16[8,16,512]{2,1,0:T(8,128)(2,1)S(1)} %get-tuple-element.51), channel_id=1, source_target_pairs={{0,12},{1,15},{2,14},{3,13},{4,8},{5,11},{6,10},{7,9},{8,4},{9,7},... | collective-permute-start | bytes 393224 | tf_op jit(solution)/shard_map/ppermute | solution.py:471
  62.0 0.0 collective-permute-done.10.rest_2_
  62.0 1.4 %collective-permute-start.9 = (bf16[8,16,512]{2,1,0:T(8,128)(2,1)S(1)}, bf16[8,16,512]{2,1,0:T(8,128)(2,1)S(1)}, u32[]{:S(2)}, u32[]{:S(2)}) collective-permute-start(bf16[8,16,512]{2,1,0:T(8,128)(2,1)S(1)} %get-tuple-element.52), channel_id=1, source_target_pairs={{0,13},{1,14},{2,15},{3,12},{4,9},{5,10},{6,11},{7,8},{8,5},{9,6},... | collective-permute-start | bytes 393224 | tf_op jit(solution)/shard_map/ppermute | solution.py:471
  63.4 0.1 stack.36.starts_ref
  63.5 0.1 pad_add_fusion.starts_ref
  63.6 1.3 %join.2.rest_6_ = bf16[64,16,512]{2,1,0:T(8,128)(2,1)} custom-call(s32[2]{0:T(128)S(1)} %pad_add_fusion.starts_ref, bf16[8,16,512]{2,1,0:T(8,128)(2,1)S(1)} %collective-permute-done.15.rest_0_, bf16[8,16,512]{2,1,0:T(8,128)(2,1)S(1)} %collective-permute-done.16.rest_1_), custom_call_target="tpu_custom_call" | custom-call | tf_op jit(solution)/shard_map/join/pallas_call | solution.py:497
  64.9 0.0 collective-permute-done.11.rest_3_
  64.9 0.0 collective-permute-done.12.rest_4_
  64.9 0.0 collective-permute-done.13.rest_5_
  64.9 3.0 %collective-permute-done.8.rest_0_ = bf16[8,16,512]{2,1,0:T(8,128)(2,1)S(1)} collective-permute-done((bf16[8,16,512]{2,1,0:T(8,128)(2,1)S(1)}, bf16[8,16,512]{2,1,0:T(8,128)(2,1)S(1)}, u32[]{:S(2)}, u32[]{:S(2)}) %collective-permute-start.8) | collective-permute-done | bytes 131104 | tf_op jit(solution)/shard_map/ppermute | solution.py:471
  67.9 2.7 %collective-permute-done.9.rest_1_ = bf16[8,16,512]{2,1,0:T(8,128)(2,1)S(1)} collective-permute-done((bf16[8,16,512]{2,1,0:T(8,128)(2,1)S(1)}, bf16[8,16,512]{2,1,0:T(8,128)(2,1)S(1)}, u32[]{:S(2)}, u32[]{:S(2)}) %collective-permute-start.9) | collective-permute-done | bytes 131104 | tf_op jit(solution)/shard_map/ppermute | solution.py:471
  70.6 1.5 %join.3 = bf16[64,16,512]{2,1,0:T(8,128)(2,1)} custom-call(s32[6]{0:T(128)S(1)} %stack.36.starts_ref, bf16[8,16,512]{2,1,0:T(8,128)(2,1)S(1)} %collective-permute-done.8.rest_0_, bf16[8,16,512]{2,1,0:T(8,128)(2,1)S(1)} %collective-permute-done.9.rest_1_, bf16[8,16,512]{2,1,0:T(8,128)(2,1)S(1)} %collective-permute-done.10.rest_2_, ...), custom_call_target="tpu_custom_call", output_to_operand_aliasing={{}: (7, {})} | custom-call | tf_op jit(solution)/shard_map/join/pallas_call | solution.py:497
Async XLA Ops:
  7.6 8.9 %collective-permute-start = (bf16[8,16,512]{2,1,0:T(8,128)(2,1)S(1)}, bf16[8,16,512]{2,1,0:T(8,128)(2,1)S(1)}, u32[]{:S(2)}, u32[]{:S(2)}) collective-permute-start(bf16[8,16,512]{2,1,0:T(8,128)(2,1)S(1)} %get-tuple-element.34), channel_id=1, source_target_pairs={{0,2},{2,0},{4,6},{6,4},{8,10},{10,8},{12,14},{14,12},{1,3},{3,1},... | collective-permute-start | bytes 393224 | tf_op jit(solution)/shard_map/ppermute | solution.py:405
  10.6 10.8 %collective-permute-start.1 = (bf16[8,16,512]{2,1,0:T(8,128)(2,1)S(1)}, bf16[8,16,512]{2,1,0:T(8,128)(2,1)S(1)}, u32[]{:S(2)}, u32[]{:S(2)}) collective-permute-start(bf16[8,16,512]{2,1,0:T(8,128)(2,1)S(1)} %get-tuple-element.35), channel_id=1, source_target_pairs={{0,4},{2,6},{4,0},{6,2},{8,12},{10,14},{12,8},{14,10},{1,5},{3,7},... | collective-permute-start | bytes 393224 | tf_op jit(solution)/shard_map/ppermute | solution.py:405
  12.2 9.9 %collective-permute-start.2 = (bf16[8,16,512]{2,1,0:T(8,128)(2,1)S(1)}, bf16[8,16,512]{2,1,0:T(8,128)(2,1)S(1)}, u32[]{:S(2)}, u32[]{:S(2)}) collective-permute-start(bf16[8,16,512]{2,1,0:T(8,128)(2,1)S(1)} %get-tuple-element.36), channel_id=1, source_target_pairs={{0,6},{2,4},{4,2},{6,0},{8,14},{10,12},{12,10},{14,8},{1,7},{3,5},... | collective-permute-start | bytes 393224 | tf_op jit(solution)/shard_map/ppermute | solution.py:405
  12.2 12.4 %collective-permute-start.3 = (bf16[8,16,512]{2,1,0:T(8,128)(2,1)S(1)}, bf16[8,16,512]{2,1,0:T(8,128)(2,1)S(1)}, u32[]{:S(2)}, u32[]{:S(2)}) collective-permute-start(bf16[8,16,512]{2,1,0:T(8,128)(2,1)S(1)} %get-tuple-element.37), channel_id=1, source_target_pairs={{0,8},{2,10},{4,12},{6,14},{8,0},{10,2},{12,4},{14,6},{1,9},{3,11}... | collective-permute-start | bytes 393224 | tf_op jit(solution)/shard_map/ppermute | solution.py:405
  15.2 19.4 %collective-permute-start.4 = (bf16[8,16,512]{2,1,0:T(8,128)(2,1)S(1)}, bf16[8,16,512]{2,1,0:T(8,128)(2,1)S(1)}, u32[]{:S(2)}, u32[]{:S(2)}) collective-permute-start(bf16[8,16,512]{2,1,0:T(8,128)(2,1)S(1)} %get-tuple-element.38), channel_id=1, source_target_pairs={{0,10},{2,8},{4,14},{6,12},{8,2},{10,0},{12,6},{14,4},{1,11},{3,9}... | collective-permute-start | bytes 393224 | tf_op jit(solution)/shard_map/ppermute | solution.py:405
  16.5 20.1 %collective-permute-start.5 = (bf16[8,16,512]{2,1,0:T(8,128)(2,1)S(1)}, bf16[8,16,512]{2,1,0:T(8,128)(2,1)S(1)}, u32[]{:S(2)}, u32[]{:S(2)}) collective-permute-start(bf16[8,16,512]{2,1,0:T(8,128)(2,1)S(1)} %get-tuple-element.39), channel_id=1, source_target_pairs={{0,12},{2,14},{4,8},{6,10},{8,4},{10,6},{12,0},{14,2},{1,13},{3,15... | collective-permute-start | bytes 393224 | tf_op jit(solution)/shard_map/ppermute | solution.py:405
  21.4 15.2 %collective-permute-start.6 = (bf16[8,16,512]{2,1,0:T(8,128)(2,1)S(1)}, bf16[8,16,512]{2,1,0:T(8,128)(2,1)S(1)}, u32[]{:S(2)}, u32[]{:S(2)}) collective-permute-start(bf16[8,16,512]{2,1,0:T(8,128)(2,1)S(1)} %get-tuple-element.40), channel_id=1, source_target_pairs={{0,14},{2,12},{4,10},{6,8},{8,6},{10,4},{12,2},{14,0},{1,15},{3,13... | collective-permute-start | bytes 393224 | tf_op jit(solution)/shard_map/ppermute | solution.py:405
  40.2 7.8 %collective-permute-start.7 = (bf16[3,8,16,512]{3,2,1,0:T(8,128)(2,1)S(1)}, bf16[3,8,16,512]{3,2,1,0:T(8,128)(2,1)S(1)}, u32[]{:S(2)}, u32[]{:S(2)}) collective-permute-start(bf16[3,8,16,512]{3,2,1,0:T(8,128)(2,1)S(1)} %get-tuple-element.48), channel_id=1, source_target_pairs={{0,1},{1,0},{2,3},{3,2},{4,5},{5,4},{6,7},{7,6},{8,9},{9,8},{10,11... | collective-permute-start | bytes 1179656 | tf_op jit(solution)/shard_map/ppermute | solution.py:442
  40.2 1.9 %collective-permute-start.14 = (bf16[1,8,16,512]{3,2,1,0:T(8,128)(2,1)S(1)}, bf16[1,8,16,512]{3,2,1,0:T(8,128)(2,1)S(1)}, u32[]{:S(2)}, u32[]{:S(2)}) collective-permute-start(bf16[1,8,16,512]{3,2,1,0:T(8,128)(2,1)S(1)} %get-tuple-element.58), channel_id=1, source_target_pairs={{0,1},{1,0},{2,3},{3,2},{4,5},{5,4},{6,7},{7,6},{8,9},{9,8},{10,11... | collective-permute-start | bytes 393224 | tf_op jit(solution)/shard_map/ppermute | solution.py:442
  43.3 14.6 %collective-permute-start.15 = (bf16[8,16,512]{2,1,0:T(8,128)(2,1)S(1)}, bf16[8,16,512]{2,1,0:T(8,128)(2,1)S(1)}, u32[]{:S(2)}, u32[]{:S(2)}) collective-permute-start(bf16[8,16,512]{2,1,0:T(8,128)(2,1)S(1)} %get-tuple-element.59), channel_id=1, source_target_pairs={{0,8},{1,11},{2,10},{3,9},{4,12},{5,15},{6,14},{7,13},{8,0},{9,3},... | collective-permute-start | bytes 393224 | tf_op jit(solution)/shard_map/ppermute | solution.py:471
  47.9 11.8 %collective-permute-start.16 = (bf16[8,16,512]{2,1,0:T(8,128)(2,1)S(1)}, bf16[8,16,512]{2,1,0:T(8,128)(2,1)S(1)}, u32[]{:S(2)}, u32[]{:S(2)}) collective-permute-start(bf16[8,16,512]{2,1,0:T(8,128)(2,1)S(1)} %get-tuple-element.60), channel_id=1, source_target_pairs={{0,9},{1,10},{2,11},{3,8},{4,13},{5,14},{6,15},{7,12},{8,1},{9,2},... | collective-permute-start | bytes 393224 | tf_op jit(solution)/shard_map/ppermute | solution.py:471
  49.7 12.3 %collective-permute-start.10 = (bf16[8,16,512]{2,1,0:T(8,128)(2,1)S(1)}, bf16[8,16,512]{2,1,0:T(8,128)(2,1)S(1)}, u32[]{:S(2)}, u32[]{:S(2)}) collective-permute-start(bf16[8,16,512]{2,1,0:T(8,128)(2,1)S(1)} %get-tuple-element.53), channel_id=1, source_target_pairs={{0,4},{1,7},{2,6},{3,5},{4,0},{5,3},{6,2},{7,1},{8,12},{9,15},{10,... | collective-permute-start | bytes 393224 | tf_op jit(solution)/shard_map/ppermute | solution.py:471
  50.4 14.5 %collective-permute-start.11 = (bf16[8,16,512]{2,1,0:T(8,128)(2,1)S(1)}, bf16[8,16,512]{2,1,0:T(8,128)(2,1)S(1)}, u32[]{:S(2)}, u32[]{:S(2)}) collective-permute-start(bf16[8,16,512]{2,1,0:T(8,128)(2,1)S(1)} %get-tuple-element.54), channel_id=1, source_target_pairs={{0,5},{1,6},{2,7},{3,4},{4,1},{5,2},{6,3},{7,0},{8,13},{9,14},{10,... | collective-permute-start | bytes 393224 | tf_op jit(solution)/shard_map/ppermute | solution.py:471
  52.2 12.7 %collective-permute-start.12 = (bf16[8,16,512]{2,1,0:T(8,128)(2,1)S(1)}, bf16[8,16,512]{2,1,0:T(8,128)(2,1)S(1)}, u32[]{:S(2)}, u32[]{:S(2)}) collective-permute-start(bf16[8,16,512]{2,1,0:T(8,128)(2,1)S(1)} %get-tuple-element.55), channel_id=1, source_target_pairs={{0,0},{1,3},{2,2},{3,1},{4,4},{5,7},{6,6},{7,5},{8,8},{9,11},{10,1... | collective-permute-start | bytes 393224 | tf_op jit(solution)/shard_map/ppermute | solution.py:471
  57.8 7.0 %collective-permute-start.13 = (bf16[8,16,512]{2,1,0:T(8,128)(2,1)S(1)}, bf16[8,16,512]{2,1,0:T(8,128)(2,1)S(1)}, u32[]{:S(2)}, u32[]{:S(2)}) collective-permute-start(bf16[8,16,512]{2,1,0:T(8,128)(2,1)S(1)} %get-tuple-element.56), channel_id=1, source_target_pairs={{0,1},{1,2},{2,3},{3,0},{4,5},{5,6},{6,7},{7,4},{8,9},{9,10},{10,1... | collective-permute-start | bytes 393224 | tf_op jit(solution)/shard_map/ppermute | solution.py:471
  59.7 8.2 %collective-permute-start.8 = (bf16[8,16,512]{2,1,0:T(8,128)(2,1)S(1)}, bf16[8,16,512]{2,1,0:T(8,128)(2,1)S(1)}, u32[]{:S(2)}, u32[]{:S(2)}) collective-permute-start(bf16[8,16,512]{2,1,0:T(8,128)(2,1)S(1)} %get-tuple-element.51), channel_id=1, source_target_pairs={{0,12},{1,15},{2,14},{3,13},{4,8},{5,11},{6,10},{7,9},{8,4},{9,7},... | collective-permute-start | bytes 393224 | tf_op jit(solution)/shard_map/ppermute | solution.py:471
  62.0 8.6 %collective-permute-start.9 = (bf16[8,16,512]{2,1,0:T(8,128)(2,1)S(1)}, bf16[8,16,512]{2,1,0:T(8,128)(2,1)S(1)}, u32[]{:S(2)}, u32[]{:S(2)}) collective-permute-start(bf16[8,16,512]{2,1,0:T(8,128)(2,1)S(1)} %get-tuple-element.52), channel_id=1, source_target_pairs={{0,13},{1,14},{2,15},{3,12},{4,9},{5,10},{6,11},{7,8},{8,5},{9,6},... | collective-permute-start | bytes 393224 | tf_op jit(solution)/shard_map/ppermute | solution.py:471
where the time goes:
time: 72.4 us; the launch traced here: 72.2 us
  starting transfers between devices  25.3 us (35%)
  Pallas kernels  23.6 us (33%)
  waiting for transfers between devices  22.8 us (31%)
    ppermute x7, starting transfers between devices, fast_body(): came[k] = lax.ppermute(sent[k], 'aa', [(i, i ^ k) for i in range(n)])  13.2 us
    ppermute x8, starting transfers between devices, finish(): arrived.append(lax.ppermute(results[2 * index + flip], ('aa', 'ba'), route))  11.6 us
    ppermute x8, waiting for transfers between devices, finish(): arrived.append(lax.ppermute(results[2 * index + flip], ('aa', 'ba'), route))  11.4 us
    ppermute x7, waiting for transfers between devices, fast_body(): came[k] = lax.ppermute(sent[k], 'aa', [(i, i ^ k) for i in range(n)])  11.3 us
    pallas_call x1, Pallas kernels, fast_body(): call(functools.partial(first_kernel, 0), [message] * n, [SMEM, HBM, HBM,...  7.58 us
    pallas_call x3, Pallas kernels, finish(): call(functools.partial(last_kernel, 2, rows), [message] * (2 * len(rows))...  4.02 us
    pallas_call x2, Pallas kernels, join(): pl.pallas_call(functools.partial(join_kernel, count), out_shape=array((fr...  2.72 us
    pallas_call x1, Pallas kernels, fast_body(): call(functools.partial(early_kernel, 1, half), [array((half * per, 3 * wi...  2.54 us
  transfers between devices with their start and end apart: 17, of which 7 were waited for; matrix products, arithmetic and copies ran while one was open for 0% of the time, Pallas kernels for 15%

commit v1 on v0

--- a/solution.py
+++ b/solution.py
@@ -127,7 +127,7 @@
     )
 
 
-def first_kernel(block, me_ref, x_hbm, gain_hbm, win_hbm, wout_hbm, *rest):
+def first_kernel(block, x_hbm, gain_hbm, win_hbm, wout_hbm, *rest):
     n = len(rest) - 9
     outs = rest[:n]
     win, wout, natural, lined, packed, mixed, sems, x_ref, gain_ref = rest[n:]
@@ -172,8 +172,9 @@
         for index, lanes in enumerate(lanes_of(update)):
             lined[index, at : at + 256] += lanes
     piece = frames // n
+    spot = lax.axis_index("aa")
     for k in range(n):
-        start = jnp.bitwise_xor(me_ref[0], k) * piece
+        start = jnp.bitwise_xor(spot, k) * piece
         for frame in range(piece):
             outs[k][frame] = strided(lined, start + frame, columns, frames).astype(jnp.bfloat16)
 
@@ -200,32 +201,24 @@
             pieces, start, count = [], start + count, 0
 
 
-def early_kernel(block, count, *rest):
-    ins, (gain_hbm, win_hbm, wout_hbm) = rest[:count], rest[count : count + 3]
-    packed, win, wout, gain_ref, sems = rest[count + 3 :]
-    loads = load_all(
-        ((gain_hbm, gain_ref), (win_hbm.at[block], win), (wout_hbm.at[block], wout)), sems
-    )
-    loads[0].wait()
-    loads[1].wait()
+def weights_kernel(blocks, gain_hbm, win_hbm, wout_hbm, *rest):
+    gain, copies, sems = rest[0], rest[1:-1], rest[-1]
+    pairs = [(gain_hbm, gain)]
+    for index, block in enumerate(blocks):
+        pairs += [
+            (win_hbm.at[block], copies[2 * index]),
+            (wout_hbm.at[block], copies[2 * index + 1]),
+        ]
+    for load in load_all(pairs, sems):
+        load.wait()
+
+
+def group_kernel(block, count, *rest):
+    ins, (gain_ref, win, packed) = rest[:count], rest[count:]
     prepare(ins, gain_ref[block : block + 1], win, packed, 0)
-    loads[2].wait()
-
-
-def late_kernel(block, count, *rest):
-    ins, (gain_ref, win, win_hbm, wout_hbm, packed, next_win, next_wout, sems) = (
-        rest[:count],
-        rest[count:],
-    )
-    loads = load_all(
-        ((win_hbm.at[block + 1], next_win), (wout_hbm.at[block + 1], next_wout)), sems
-    )
-    prepare(ins, gain_ref[block : block + 1], win, packed, 0)
-    for load in loads:
-        load.wait()
-
-
-def share_rows(core_ref, update, ins, keep, give):
+
+
+def share_rows(update, ins, keep, give):
     frames, columns, width = ins[0].shape
     per = frames * columns
     totals = [
@@ -234,7 +227,7 @@
         .reshape(frames, columns, width)
         for each in range(2)
     ]
-    second = core_ref[0]
+    second = lax.axis_index("ba")
 
     @pl.when(second == 0)
     def _():
@@ -247,18 +240,18 @@
         give[...] = totals[0]
 
 
-def middle_kernel(block, counts, pair, core_ref, *rest):
-    n = sum(counts)
+def middle_kernel(block, groups, pair, *rest):
+    n = sum(map(len, groups))
     ins = rest[:n]
-    groups = rest[n : n + len(counts) - 1]
-    gain_ref, win, wout, mixed, keep_ref, give_ref, packed = rest[n + len(counts) - 1 :]
+    ready = rest[n : n + len(groups) - 1]
+    gain_ref, win, wout, mixed, keep_ref, give_ref, packed = rest[n + len(groups) - 1 :]
     frames, columns, _ = ins[0].shape
     per = columns * frames
-    last = n - counts[-1]
-    prepare(ins[last:], gain_ref[block : block + 1], win, packed, 0)
-    homes = []
-    for group, count in zip((*groups, packed), counts):
-        homes += [(group, index * per) for index in range(count)]
+    prepare([ins[k] for k in groups[-1]], gain_ref[block : block + 1], win, packed, 0)
+    homes = [None] * n
+    for group, ref in zip(groups, (*ready, packed)):
+        for index, k in enumerate(group):
+            homes[k] = (ref, index * per)
     share = LANES // n
     mask = line_mask(LANES, lambda i: i % share)
     halves = lane_halves(LANES)
@@ -271,10 +264,10 @@
             mixed[k * per + at : k * per + at + share] = result[k * share : (k + 1) * share]
     k = 2 * pair
     update = jnp.dot(mixed[k * per : (k + 2) * per], wout[...], preferred_element_type=jnp.float32)
-    share_rows(core_ref, update, ins[k : k + 2], keep_ref.at[0], give_ref.at[0])
-
-
-def middle_rest_kernel(pairs, core_ref, mixed, wout, *rest):
+    share_rows(update, ins[k : k + 2], keep_ref.at[0], give_ref.at[0])
+
+
+def middle_rest_kernel(pairs, mixed, wout, *rest):
     ins = rest[: 2 * len(pairs)]
     keep_ref, give_ref = rest[2 * len(pairs) :]
     frames, columns, _ = ins[0].shape
@@ -285,7 +278,6 @@
             mixed[k * per : (k + 2) * per], wout[...], preferred_element_type=jnp.float32
         )
         share_rows(
-            core_ref,
             update,
             ins[2 * index : 2 * index + 2],
             keep_ref.at[index],
@@ -335,24 +327,25 @@
             ).astype(jnp.bfloat16)
 
 
-def join_kernel(count, starts_ref, *rest):
-    pieces, out, sems = rest[:count], rest[-2], rest[-1]
+def join_kernel(senders, *rest):
+    pieces, out, sems = rest[: len(senders)], rest[-2], rest[-1]
     size = pieces[0].shape[0]
+    spot, core = lax.axis_index("aa"), lax.axis_index("ba")
     copies = []
-    for index, piece in enumerate(pieces):
-        where = pl.ds(starts_ref[index] * size, size)
+    for index, (piece, (row, flip)) in enumerate(zip(pieces, senders)):
+        sender = jnp.bitwise_xor(spot, 2 * row + jnp.bitwise_xor(core, flip))
+        where = pl.ds(sender * size, size)
         copies.append(pltpu.make_async_copy(piece, out.at[where], sems.at[index]))
         copies[-1].start()
     for copy in copies:
         copy.wait()
 
 
-SMEM = pl.BlockSpec(memory_space=pltpu.SMEM)
 VMEM = pl.BlockSpec(memory_space=pltpu.VMEM)
 HBM = pl.BlockSpec(memory_space=pltpu.HBM)
 
 
-def call(kernel, outs, in_specs, scratch_shapes, limit=24):
+def call(kernel, outs, in_specs, scratch_shapes, limit=8):
     return pl.pallas_call(
         kernel,
         out_shape=outs,
@@ -368,8 +361,6 @@
     piece = frames // n
     per = piece * columns
     tokens = frames * columns
-    spot = lax.axis_index("aa")
-    core = lax.axis_index("ba")
     bf16, f32 = jnp.bfloat16, jnp.float32
     array = jax.ShapeDtypeStruct
     message = array((piece, columns, width), bf16)
@@ -386,7 +377,7 @@
     sent = call(
         functools.partial(first_kernel, 0),
         [message] * n,
-        [SMEM, HBM, HBM, HBM, HBM],
+        [HBM] * 4,
         [
             pltpu.VMEM(win_shape, bf16),
             pltpu.VMEM(wout_shape, bf16),
@@ -398,31 +389,31 @@
             pltpu.VMEM((frames, columns, width), bf16),
             pltpu.VMEM(gain_shape, f32),
         ],
-    )(spot[None], local, *weights)
+        limit=24,
+    )(local, *weights)
 
     came = {0: sent[0]}
     for k in range(1, n):
         came[k] = lax.ppermute(sent[k], "aa", [(i, i ^ k) for i in range(n)])
 
-    half, quarter = n // 2, n // 4
-    final = n - half - quarter
-    packed_early, win, wout, gain = call(
-        functools.partial(early_kernel, 1, half),
-        [
-            array((half * per, 3 * width), bf16),
-            array(win_shape, bf16),
-            array(wout_shape, bf16),
-            array(gain_shape, f32),
-        ],
-        [VMEM] * half + [HBM, HBM, HBM],
-        [pltpu.SemaphoreType.DMA((3,))],
-    )(*[came[k] for k in range(half)], *weights)
-    packed_late, next_win, next_wout = call(
-        functools.partial(late_kernel, 1, quarter),
-        [array((quarter * per, 3 * width), bf16), array(win_shape, bf16), array(wout_shape, bf16)],
-        [VMEM] * (quarter + 2) + [HBM, HBM],
-        [pltpu.SemaphoreType.DMA((2,))],
-    )(*[came[k] for k in range(half, half + quarter)], gain, win, *weights[1:])
+    later = range(1, norm_gain.shape[0])
+    gain, *fetched = call(
+        functools.partial(weights_kernel, later),
+        [array(gain_shape, f32)] + [array(win_shape, bf16), array(wout_shape, bf16)] * len(later),
+        [HBM] * 3,
+        [pltpu.SemaphoreType.DMA((1 + 2 * len(later),))],
+    )(*weights)
+    win, wout, next_win, next_wout = fetched
+
+    *groups, final = arrival_groups(n)
+    ready = []
+    for group in groups:
+        ready += call(
+            functools.partial(group_kernel, 1, len(group)),
+            [array((len(group) * per, 3 * width), bf16)],
+            [VMEM] * (len(group) + 2),
+            [],
+        )(*[came[k] for k in group], gain, win)
 
     lead, *others = row_order(n)
 
@@ -430,11 +421,11 @@
         return array((count, piece, columns, width), bf16)
 
     mixed, keep, give = call(
-        functools.partial(middle_kernel, 1, (half, quarter, final), lead),
+        functools.partial(middle_kernel, 1, (*groups, final), lead),
         [array((tokens, width), bf16), kept(1), kept(1)],
-        [SMEM] + [VMEM] * (n + 5),
-        [pltpu.VMEM((final * per, 3 * width), bf16)],
-    )(core[None], *[came[k] for k in range(n)], packed_early, packed_late, gain, win, wout)
+        [VMEM] * (n + len(ready) + 3),
+        [pltpu.VMEM((len(final) * per, 3 * width), bf16)],
+    )(*[came[k] for k in range(n)], *ready, gain, win, wout)
 
     arrived, starts = [], []
 
@@ -469,7 +460,7 @@
                     for b in range(2)
                 ]
                 arrived.append(lax.ppermute(results[2 * index + flip], ("aa", "ba"), route))
-                starts.append(jnp.bitwise_xor(spot, 2 * row + jnp.bitwise_xor(core, flip)))
+                starts.append((row, flip))
 
     got = swap(give)
     finish([0], [lead], keep, got, project_kept(keep))
@@ -477,10 +468,9 @@
     keep, give = call(
         functools.partial(middle_rest_kernel, others),
         [kept(len(others)), kept(len(others))],
-        [SMEM] + [VMEM] * (2 + 2 * len(others)),
+        [VMEM] * (2 + 2 * len(others)),
         [],
     )(
-        core[None],
         mixed,
         wout,
         *[came[2 * pair + each] for pair in others for each in range(2)],
@@ -491,19 +481,19 @@
     for rows in ([*range(cut)], [*range(cut, len(others))]):
         finish(rows, [others[row] for row in rows], keep, got, packed)
 
-    def join(values, offsets, base=None):
+    def join(values, senders, base=None):
         count = len(values)
         given = [] if base is None else [base]
         return pl.pallas_call(
-            functools.partial(join_kernel, count),
+            functools.partial(join_kernel, senders),
             out_shape=array((frames, columns, width), bf16),
-            in_specs=[SMEM] + [VMEM] * count + [HBM] * len(given),
+            in_specs=[VMEM] * count + [HBM] * len(given),
             out_specs=HBM,
             scratch_shapes=[pltpu.SemaphoreType.DMA((count,))],
-            input_output_aliases={count + 1: 0} if given else {},
+            input_output_aliases={count: 0} if given else {},
             name="join",
             compiler_params=pltpu.CompilerParams(vmem_limit_bytes=4 << 20),
-        )(jnp.stack(offsets).astype(jnp.int32), *values, *given)
+        )(*values, *given)
 
     out = join(arrived[:2], starts[:2])
     out = join(arrived[2:], starts[2:], out)
@@ -539,6 +529,15 @@
     return [*range(n // 4, n // 2), *range(n // 4 - 1, -1, -1)]
 
 
+def arrival_groups(n):
+    half, quarter = n // 2, n // 4
+    return [
+        [0, 1, *range(half, half + quarter)],
+        [*range(2, half)],
+        [*range(half + quarter, n)],
+    ]
+
+
 def solution(mesh):
     n = mesh.shape["aa"]
     return jax.shard_map(

time: 72.4 us -> 74.9 us (1.035)
  starting transfers between devices: 25.3 us -> 28.5 us
  Pallas kernels: 23.6 us -> 21.6 us
  waiting for transfers between devices: 22.8 us -> 24.2 us
    ppermute x8, waiting for transfers between devices: 11.4 us -> 14.5 us  [finish(): arrived.append(lax.ppermute(results[2 * index + flip], ('aa', 'ba'), route))]
    pallas_call x6 -> x7, Pallas kernels: 17.1 us -> 15.3 us  [the longest x1 7.58 us: fast_body(): call(functools.partial(first_kernel, 0), [message] * n, [HBM] * 4, [pltpu...]
    ppermute x8, starting transfers between devices: 11.6 us -> 13.3 us  [finish(): arrived.append(lax.ppermute(results[2 * index + flip], ('aa', 'ba'), route))]
    ppermute x7, waiting for transfers between devices: 11.3 us -> 9.59 us  [fast_body(): came[k] = lax.ppermute(sent[k], 'aa', [(i, i ^ k) for i in range(n)])]
    ppermute x7, starting transfers between devices: 13.2 us -> 14.6 us  [fast_body(): came[k] = lax.ppermute(sent[k], 'aa', [(i, i ^ k) for i in range(n)])]
  transfers between devices with their start and end apart: 17 -> 17, of which waited for: 7 -> 7; matrix products, arithmetic and copies ran while one was open for 0% -> 0% of each run, Pallas kernels for 15% -> 13%
where the time goes in v1:
time: 74.9 us; the launch traced here: 74.7 us
  starting transfers between devices  28.5 us (38%)
  waiting for transfers between devices  24.2 us (32%)
  Pallas kernels  21.6 us (29%)
    ppermute x7, starting transfers between devices, fast_body(): came[k] = lax.ppermute(sent[k], 'aa', [(i, i ^ k) for i in range(n)])  14.6 us
    ppermute x8, waiting for transfers between devices, finish(): arrived.append(lax.ppermute(results[2 * index + flip], ('aa', 'ba'), route))  14.5 us
    ppermute x8, starting transfers between devices, finish(): arrived.append(lax.ppermute(results[2 * index + flip], ('aa', 'ba'), route))  13.3 us
    ppermute x7, waiting for transfers between devices, fast_body(): came[k] = lax.ppermute(sent[k], 'aa', [(i, i ^ k) for i in range(n)])  9.59 us
    pallas_call x1, Pallas kernels, fast_body(): call(functools.partial(first_kernel, 0), [message] * n, [HBM] * 4, [pltpu...  7.58 us
    pallas_call x3, Pallas kernels, finish(): call(functools.partial(last_kernel, 2, rows), [message] * (2 * len(rows))...  3.91 us
    pallas_call x1, Pallas kernels, fast_body(): call(functools.partial(middle_kernel, 1, (*groups, final), lead), [array(...  2.23 us
    pallas_call x1, Pallas kernels, fast_body(): call(functools.partial(weights_kernel, later), [array(gain_shape, f32)] +...  2.2 us
  transfers between devices with their start and end apart: 17, of which 7 were waited for; matrix products, arithmetic and copies ran while one was open for 0% of the time, Pallas kernels for 13%

profile of v1, /device:TPU:0, one launch (start us, length us, event | category | flops | bytes accessed | tf_op | source)
XLA Modules:
  0.0 74.7 jit_solution(6278130305018067971)
XLA Ops:
  0.0 7.6 %shard_map.46 = (bf16[8,16,512]{2,1,0:T(8,128)(2,1)S(1)}, bf16[8,16,512]{2,1,0:T(8,128)(2,1)S(1)}, bf16[8,16,512]{2,1,0:T(8,128)(2,1)S(1)}, bf16[8,16,512]{2,1,0...) custom-call(bf16[64,16,512]{2,1,0:T(8,128)(2,1)} %bitcast.4, ...), custom_call_target="tpu_custom_call" | custom-call | tf_op jit(solution)/shard_map/pallas_call | solution.py:377
  7.6 3.1 %collective-permute-start.1 = (bf16[8,16,512]{2,1,0:T(8,128)(2,1)S(1)}, bf16[8,16,512]{2,1,0:T(8,128)(2,1)S(1)}, u32[]{:S(2)}, u32[]{:S(2)}) collective-permute-start(bf16[8,16,512]{2,1,0:T(8,128)(2,1)S(1)} %get-tuple-element.33), channel_id=1, source_target_pairs={{0,4},{2,6},{4,0},{6,2},{8,12},{10,14},{12,8},{14,10},{1,5},{3,7},... | collective-permute-start | bytes 393224 | tf_op jit(solution)/shard_map/ppermute | solution.py:397
  10.7 1.4 %collective-permute-start.2 = (bf16[8,16,512]{2,1,0:T(8,128)(2,1)S(1)}, bf16[8,16,512]{2,1,0:T(8,128)(2,1)S(1)}, u32[]{:S(2)}, u32[]{:S(2)}) collective-permute-start(bf16[8,16,512]{2,1,0:T(8,128)(2,1)S(1)} %get-tuple-element.34), channel_id=1, source_target_pairs={{0,6},{2,4},{4,2},{6,0},{8,14},{10,12},{12,10},{14,8},{1,7},{3,5},... | collective-permute-start | bytes 393224 | tf_op jit(solution)/shard_map/ppermute | solution.py:397
  12.1 0.1 collective-permute-start
  12.2 3.0 %collective-permute-start.3 = (bf16[8,16,512]{2,1,0:T(8,128)(2,1)S(1)}, bf16[8,16,512]{2,1,0:T(8,128)(2,1)S(1)}, u32[]{:S(2)}, u32[]{:S(2)}) collective-permute-start(bf16[8,16,512]{2,1,0:T(8,128)(2,1)S(1)} %get-tuple-element.35), channel_id=1, source_target_pairs={{0,8},{2,10},{4,12},{6,14},{8,0},{10,2},{12,4},{14,6},{1,9},{3,11}... | collective-permute-start | bytes 393224 | tf_op jit(solution)/shard_map/ppermute | solution.py:397
  15.2 1.3 %collective-permute-start.4 = (bf16[8,16,512]{2,1,0:T(8,128)(2,1)S(1)}, bf16[8,16,512]{2,1,0:T(8,128)(2,1)S(1)}, u32[]{:S(2)}, u32[]{:S(2)}) collective-permute-start(bf16[8,16,512]{2,1,0:T(8,128)(2,1)S(1)} %get-tuple-element.36), channel_id=1, source_target_pairs={{0,10},{2,8},{4,14},{6,12},{8,2},{10,0},{12,6},{14,4},{1,11},{3,9}... | collective-permute-start | bytes 393224 | tf_op jit(solution)/shard_map/ppermute | solution.py:397
  16.5 0.0 collective-permute-done.1.rest_0_.rest_2_
  16.5 3.7 %collective-permute-start.5 = (bf16[8,16,512]{2,1,0:T(8,128)(2,1)S(1)}, bf16[8,16,512]{2,1,0:T(8,128)(2,1)S(1)}, u32[]{:S(2)}, u32[]{:S(2)}) collective-permute-start(bf16[8,16,512]{2,1,0:T(8,128)(2,1)S(1)} %get-tuple-element.37), channel_id=1, source_target_pairs={{0,12},{2,14},{4,8},{6,10},{8,4},{10,6},{12,0},{14,2},{1,13},{3,15... | collective-permute-start | bytes 393224 | tf_op jit(solution)/shard_map/ppermute | solution.py:397
  20.2 1.4 %collective-permute-done.2.rest_1_.rest_3_ = bf16[8,16,512]{2,1,0:T(8,128)(2,1)S(1)} collective-permute-done((bf16[8,16,512]{2,1,0:T(8,128)(2,1)S(1)}, bf16[8,16,512]{2,1,0:T(8,128)(2,1)S(1)}, u32[]{:S(2)}, u32[]{:S(2)}) %collective-permute-start.2) | collective-permute-done | bytes 131104 | tf_op jit(solution)/shard_map/ppermute | solution.py:397
  21.6 2.0 %collective-permute-start.6 = (bf16[8,16,512]{2,1,0:T(8,128)(2,1)S(1)}, bf16[8,16,512]{2,1,0:T(8,128)(2,1)S(1)}, u32[]{:S(2)}, u32[]{:S(2)}) collective-permute-start(bf16[8,16,512]{2,1,0:T(8,128)(2,1)S(1)} %get-tuple-element.38), channel_id=1, source_target_pairs={{0,14},{2,12},{4,10},{6,8},{8,6},{10,4},{12,2},{14,0},{1,15},{3,13... | collective-permute-start | bytes 393224 | tf_op jit(solution)/shard_map/ppermute | solution.py:397
  23.6 2.2 %shard_map.47 = (f32[3,512]{1,0:T(4,128)S(1)}, bf16[512,1536]{1,0:T(8,128)(2,1)S(1)}, bf16[512,512]{1,0:T(8,128)(2,1)S(1)}, bf16[512,1536]{1,0:T(8,128)(2,1)S(1)}, bf16[512,512]{1,0:T(8,128)(2,1)S(1)}) custom-call(f32[3,512]{1,0:T(4,128)} %gain_hbm.3, bf16[3,512,1536]{2,1,0:T(8,128)(2,1)} %win_hbm.3, bf16[3,512,512]{2,1,0:T(8,128)(2,1)} %wout_hbm.3), custom_call_target="tpu_custom_call" | custom-call | tf_op jit(solution)/shard_map/pallas_call | solution.py:400
  25.8 0.6 shard_map.49.rest_9_
  26.5 0.0 collective-permute-done.rest_1_.rest_5_
  26.5 0.0 collective-permute-done.3.rest_2_.rest_4_
  26.5 8.1 %collective-permute-done.4.rest_3_.rest_5_ = bf16[8,16,512]{2,1,0:T(8,128)(2,1)S(1)} collective-permute-done((bf16[8,16,512]{2,1,0:T(8,128)(2,1)S(1)}, bf16[8,16,512]{2,1,0:T(8,128)(2,1)S(1)}, u32[]{:S(2)}, u32[]{:S(2)}) %collective-permute-start.4) | collective-permute-done | bytes 131104 | tf_op jit(solution)/shard_map/ppermute | solution.py:397
  34.6 1.0 %shard_map.48.rest_8_ = bf16[512,1536]{1,0:T(8,128)(2,1)S(1)} custom-call(bf16[8,16,512]{2,1,0:T(8,128)(2,1)S(1)} %get-tuple-element.31.rest_0_.rest_4_, bf16[8,16,512]{2,1,0:T(8,128)(2,1)S(1)} %collective-permute-done.rest_1_.rest_5_, bf16[8,16,512]{2,1,0:T(8,128)(2,1)S(1)} %collective-permute-done.3.rest_2_.rest_4_, ...), custom_call_target="tpu_custom_call" | custom-call | tf_op jit(solution)/shard_map/pallas_call | solution.py:411
  35.7 0.0 collective-permute-done.5.rest_6_.rest_0_
  35.7 0.0 collective-permute-done.6.rest_7_.rest_1_
  35.7 2.2 %shard_map.50 = (bf16[1024,512]{1,0:T(8,128)(2,1)S(1)}, bf16[1,8,16,512]{3,2,1,0:T(8,128)(2,1)S(1)}, bf16[1,8,16,512]{3,2,1,0:T(8,128)(2,1)S(1)}) custom-call(bf16[8,16,512]{2,1,0:T(8,128)(2,1)S(1)} %get-tuple-element.31.rest_0_.rest_4_, bf16[8,16,512]{2,1,0:T(8,128)(2,1)S(1)} %collective-permute-done.rest_1_.rest_5_, ...), custom_call_target="tpu_custom_call" | custom-call | tf_op jit(solution)/shard_map/pallas_call | solution.py:423
  37.9 1.1 %shard_map.51 = (bf16[3,8,16,512]{3,2,1,0:T(8,128)(2,1)S(1)}, bf16[3,8,16,512]{3,2,1,0:T(8,128)(2,1)S(1)}) custom-call(bf16[1024,512]{1,0:T(8,128)(2,1)S(1)} %get-tuple-element.42.mixed, bf16[512,512]{1,0:T(8,128)(2,1)S(1)} %get-tuple-element.41.rest_12_.wout, bf16[8,16,512]{2,1,0:T(8,128)(2,1)S(1)} %collective-permute-done.5.rest_6_.rest_0_, ...), custom_call_target="tpu_custom_call" | custom-call | tf_op jit(solution)/shard_map/pallas_call | solution.py:468
  39.1 0.1 collective-permute-start.7
  39.2 0.5 collective-permute-start.14
  39.7 0.4 shard_map.55.kept_packed
  40.1 0.8 %shard_map.52.kept_packed = bf16[384,1536]{1,0:T(8,128)(2,1)S(1)} custom-call(bf16[3,8,16,512]{3,2,1,0:T(8,128)(2,1)S(1)} %get-tuple-element.43.keep_ref, f32[3,512]{1,0:T(4,128)S(1)} %get-tuple-element.39.rest_4_.rest_2_.rest_10_.gain_ref, bf16[512,1536]{1,0:T(8,128)(2,1)S(1)} %get-tuple-element.45.win), custom_call_target="tpu_custom_call" | custom-call | tf_op jit(solution)/shard_map/pallas_call | solution.py:437
  40.9 0.1 collective-permute-done.14.got_ref
  41.1 1.1 %shard_map.56 = (bf16[8,16,512]{2,1,0:T(8,128)(2,1)S(1)}, bf16[8,16,512]{2,1,0:T(8,128)(2,1)S(1)}) custom-call(bf16[1,8,16,512]{3,2,1,0:T(8,128)(2,1)S(1)} %get-tuple-element.53.keep_ref, bf16[1,8,16,512]{3,2,1,0:T(8,128)(2,1)S(1)} %collective-permute-done.14.got_ref, bf16[128,1536]{1,0:T(8,128)(2,1)S(1)} %shard_map.55.kept_packed, ...), custom_call_target="tpu_custom_call" | custom-call | tf_op jit(solution)/shard_map/pallas_call | solution.py:446
  42.2 5.6 %collective-permute-start.15 = (bf16[8,16,512]{2,1,0:T(8,128)(2,1)S(1)}, bf16[8,16,512]{2,1,0:T(8,128)(2,1)S(1)}, u32[]{:S(2)}, u32[]{:S(2)}) collective-permute-start(bf16[8,16,512]{2,1,0:T(8,128)(2,1)S(1)} %get-tuple-element.55), channel_id=1, source_target_pairs={{0,8},{1,11},{2,10},{3,9},{4,12},{5,15},{6,14},{7,13},{8,0},{9,3},... | collective-permute-start | bytes 393224 | tf_op jit(solution)/shard_map/ppermute | solution.py:462
  47.8 0.0 collective-permute-start.16
  47.8 0.0 collective-permute-done.7.got_ref
  47.8 1.1 %shard_map.53 = (bf16[8,16,512]{2,1,0:T(8,128)(2,1)S(1)}, bf16[8,16,512]{2,1,0:T(8,128)(2,1)S(1)}) custom-call(bf16[3,8,16,512]{3,2,1,0:T(8,128)(2,1)S(1)} %get-tuple-element.43.keep_ref, bf16[3,8,16,512]{3,2,1,0:T(8,128)(2,1)S(1)} %collective-permute-done.7.got_ref, bf16[384,1536]{1,0:T(8,128)(2,1)S(1)} %shard_map.52.kept_packed, ...), custom_call_target="tpu_custom_call" | custom-call | tf_op jit(solution)/shard_map/pallas_call | solution.py:446
  48.9 0.9 %collective-permute-start.8 = (bf16[8,16,512]{2,1,0:T(8,128)(2,1)S(1)}, bf16[8,16,512]{2,1,0:T(8,128)(2,1)S(1)}, u32[]{:S(2)}, u32[]{:S(2)}) collective-permute-start(bf16[8,16,512]{2,1,0:T(8,128)(2,1)S(1)} %get-tuple-element.47), channel_id=1, source_target_pairs={{0,12},{1,15},{2,14},{3,13},{4,8},{5,11},{6,10},{7,9},{8,4},{9,7},... | collective-permute-start | bytes 393224 | tf_op jit(solution)/shard_map/ppermute | solution.py:462
  49.8 3.4 %collective-permute-start.9 = (bf16[8,16,512]{2,1,0:T(8,128)(2,1)S(1)}, bf16[8,16,512]{2,1,0:T(8,128)(2,1)S(1)}, u32[]{:S(2)}, u32[]{:S(2)}) collective-permute-start(bf16[8,16,512]{2,1,0:T(8,128)(2,1)S(1)} %get-tuple-element.48), channel_id=1, source_target_pairs={{0,13},{1,14},{2,15},{3,12},{4,9},{5,10},{6,11},{7,8},{8,5},{9,6},... | collective-permute-start | bytes 393224 | tf_op jit(solution)/shard_map/ppermute | solution.py:462
  53.2 1.7 %shard_map.54 = (bf16[8,16,512]{2,1,0:T(8,128)(2,1)S(1)}, bf16[8,16,512]{2,1,0:T(8,128)(2,1)S(1)}, bf16[8,16,512]{2,1,0:T(8,128)(2,1)S(1)}, bf16[8,16,512]{2,1,0:T(8,128)(2,1)S(1)}) custom-call(bf16[3,8,16,512]{3,2,1,0:T(8,128)(2,1)S(1)} %get-tuple-element.43.keep_ref, bf16[3,8,16,512]{3,2,1,0:T(8,128)(2,1)S(1)} %collective-permute-done.7.got_ref, ...), custom_call_target="tpu_custom_call" | custom-call | tf_op jit(solution)/shard_map/pallas_call | solution.py:446
  54.9 0.1 collective-permute-start.10
  55.0 8.4 %collective-permute-done.15.rest_0_ = bf16[8,16,512]{2,1,0:T(8,128)(2,1)S(1)} collective-permute-done((bf16[8,16,512]{2,1,0:T(8,128)(2,1)S(1)}, bf16[8,16,512]{2,1,0:T(8,128)(2,1)S(1)}, u32[]{:S(2)}, u32[]{:S(2)}) %collective-permute-start.15) | collective-permute-done | bytes 131104 | tf_op jit(solution)/shard_map/ppermute | solution.py:462
  63.3 0.0 collective-permute-start.11
  63.3 1.8 %collective-permute-done.16.rest_1_ = bf16[8,16,512]{2,1,0:T(8,128)(2,1)S(1)} collective-permute-done((bf16[8,16,512]{2,1,0:T(8,128)(2,1)S(1)}, bf16[8,16,512]{2,1,0:T(8,128)(2,1)S(1)}, u32[]{:S(2)}, u32[]{:S(2)}) %collective-permute-start.16) | collective-permute-done | bytes 131104 | tf_op jit(solution)/shard_map/ppermute | solution.py:462
  65.1 0.7 collective-permute-start.12
  65.8 0.0 collective-permute-done.8.rest_0_
  65.8 2.7 %collective-permute-start.13 = (bf16[8,16,512]{2,1,0:T(8,128)(2,1)S(1)}, bf16[8,16,512]{2,1,0:T(8,128)(2,1)S(1)}, u32[]{:S(2)}, u32[]{:S(2)}) collective-permute-start(bf16[8,16,512]{2,1,0:T(8,128)(2,1)S(1)} %get-tuple-element.52), channel_id=1, source_target_pairs={{0,1},{1,2},{2,3},{3,0},{4,5},{5,6},{6,7},{7,4},{8,9},{9,10},{10,1... | collective-permute-start | bytes 393224 | tf_op jit(solution)/shard_map/ppermute | solution.py:462
  68.5 0.7 join.2.rest_6_
  69.2 0.0 collective-permute-done.9.rest_1_
  69.2 0.0 collective-permute-done.10.rest_2_
  69.2 1.9 %collective-permute-done.11.rest_3_ = bf16[8,16,512]{2,1,0:T(8,128)(2,1)S(1)} collective-permute-done((bf16[8,16,512]{2,1,0:T(8,128)(2,1)S(1)}, bf16[8,16,512]{2,1,0:T(8,128)(2,1)S(1)}, u32[]{:S(2)}, u32[]{:S(2)}) %collective-permute-start.11) | collective-permute-done | bytes 131104 | tf_op jit(solution)/shard_map/ppermute | solution.py:462
  71.2 0.0 collective-permute-done.12.rest_4_
  71.2 2.4 %collective-permute-done.13.rest_5_ = bf16[8,16,512]{2,1,0:T(8,128)(2,1)S(1)} collective-permute-done((bf16[8,16,512]{2,1,0:T(8,128)(2,1)S(1)}, bf16[8,16,512]{2,1,0:T(8,128)(2,1)S(1)}, u32[]{:S(2)}, u32[]{:S(2)}) %collective-permute-start.13) | collective-permute-done | bytes 131104 | tf_op jit(solution)/shard_map/ppermute | solution.py:462
  73.6 0.9 %join.3 = bf16[64,16,512]{2,1,0:T(8,128)(2,1)} custom-call(bf16[8,16,512]{2,1,0:T(8,128)(2,1)S(1)} %collective-permute-done.8.rest_0_, bf16[8,16,512]{2,1,0:T(8,128)(2,1)S(1)} %collective-permute-done.9.rest_1_, bf16[8,16,512]{2,1,0:T(8,128)(2,1)S(1)} %collective-permute-done.10.rest_2_, ...), custom_call_target="tpu_custom_call", output_to_operand_aliasing={{}: (6, {})} | custom-call | tf_op jit(solution)/shard_map/join/pallas_call | solution.py:487
Async XLA Ops:
  7.6 8.9 %collective-permute-start.1 = (bf16[8,16,512]{2,1,0:T(8,128)(2,1)S(1)}, bf16[8,16,512]{2,1,0:T(8,128)(2,1)S(1)}, u32[]{:S(2)}, u32[]{:S(2)}) collective-permute-start(bf16[8,16,512]{2,1,0:T(8,128)(2,1)S(1)} %get-tuple-element.33), channel_id=1, source_target_pairs={{0,4},{2,6},{4,0},{6,2},{8,12},{10,14},{12,8},{14,10},{1,5},{3,7},... | collective-permute-start | bytes 393224 | tf_op jit(solution)/shard_map/ppermute | solution.py:397
  10.7 10.9 %collective-permute-start.2 = (bf16[8,16,512]{2,1,0:T(8,128)(2,1)S(1)}, bf16[8,16,512]{2,1,0:T(8,128)(2,1)S(1)}, u32[]{:S(2)}, u32[]{:S(2)}) collective-permute-start(bf16[8,16,512]{2,1,0:T(8,128)(2,1)S(1)} %get-tuple-element.34), channel_id=1, source_target_pairs={{0,6},{2,4},{4,2},{6,0},{8,14},{10,12},{12,10},{14,8},{1,7},{3,5},... | collective-permute-start | bytes 393224 | tf_op jit(solution)/shard_map/ppermute | solution.py:397
  12.1 14.4 %collective-permute-start = (bf16[8,16,512]{2,1,0:T(8,128)(2,1)S(1)}, bf16[8,16,512]{2,1,0:T(8,128)(2,1)S(1)}, u32[]{:S(2)}, u32[]{:S(2)}) collective-permute-start(bf16[8,16,512]{2,1,0:T(8,128)(2,1)S(1)} %get-tuple-element.32), channel_id=1, source_target_pairs={{0,2},{2,0},{4,6},{6,4},{8,10},{10,8},{12,14},{14,12},{1,3},{3,1},... | collective-permute-start | bytes 393224 | tf_op jit(solution)/shard_map/ppermute | solution.py:397
  12.2 14.2 %collective-permute-start.3 = (bf16[8,16,512]{2,1,0:T(8,128)(2,1)S(1)}, bf16[8,16,512]{2,1,0:T(8,128)(2,1)S(1)}, u32[]{:S(2)}, u32[]{:S(2)}) collective-permute-start(bf16[8,16,512]{2,1,0:T(8,128)(2,1)S(1)} %get-tuple-element.35), channel_id=1, source_target_pairs={{0,8},{2,10},{4,12},{6,14},{8,0},{10,2},{12,4},{14,6},{1,9},{3,11}... | collective-permute-start | bytes 393224 | tf_op jit(solution)/shard_map/ppermute | solution.py:397
  15.2 19.4 %collective-permute-start.4 = (bf16[8,16,512]{2,1,0:T(8,128)(2,1)S(1)}, bf16[8,16,512]{2,1,0:T(8,128)(2,1)S(1)}, u32[]{:S(2)}, u32[]{:S(2)}) collective-permute-start(bf16[8,16,512]{2,1,0:T(8,128)(2,1)S(1)} %get-tuple-element.36), channel_id=1, source_target_pairs={{0,10},{2,8},{4,14},{6,12},{8,2},{10,0},{12,6},{14,4},{1,11},{3,9}... | collective-permute-start | bytes 393224 | tf_op jit(solution)/shard_map/ppermute | solution.py:397
  16.5 19.2 %collective-permute-start.5 = (bf16[8,16,512]{2,1,0:T(8,128)(2,1)S(1)}, bf16[8,16,512]{2,1,0:T(8,128)(2,1)S(1)}, u32[]{:S(2)}, u32[]{:S(2)}) collective-permute-start(bf16[8,16,512]{2,1,0:T(8,128)(2,1)S(1)} %get-tuple-element.37), channel_id=1, source_target_pairs={{0,12},{2,14},{4,8},{6,10},{8,4},{10,6},{12,0},{14,2},{1,13},{3,15... | collective-permute-start | bytes 393224 | tf_op jit(solution)/shard_map/ppermute | solution.py:397
  21.6 14.1 %collective-permute-start.6 = (bf16[8,16,512]{2,1,0:T(8,128)(2,1)S(1)}, bf16[8,16,512]{2,1,0:T(8,128)(2,1)S(1)}, u32[]{:S(2)}, u32[]{:S(2)}) collective-permute-start(bf16[8,16,512]{2,1,0:T(8,128)(2,1)S(1)} %get-tuple-element.38), channel_id=1, source_target_pairs={{0,14},{2,12},{4,10},{6,8},{8,6},{10,4},{12,2},{14,0},{1,15},{3,13... | collective-permute-start | bytes 393224 | tf_op jit(solution)/shard_map/ppermute | solution.py:397
  39.1 8.7 %collective-permute-start.7 = (bf16[3,8,16,512]{3,2,1,0:T(8,128)(2,1)S(1)}, bf16[3,8,16,512]{3,2,1,0:T(8,128)(2,1)S(1)}, u32[]{:S(2)}, u32[]{:S(2)}) collective-permute-start(bf16[3,8,16,512]{3,2,1,0:T(8,128)(2,1)S(1)} %get-tuple-element.44), channel_id=1, source_target_pairs={{0,1},{1,0},{2,3},{3,2},{4,5},{5,4},{6,7},{7,6},{8,9},{9,8},{10,11... | collective-permute-start | bytes 1179656 | tf_op jit(solution)/shard_map/ppermute | solution.py:433
  39.2 1.9 %collective-permute-start.14 = (bf16[1,8,16,512]{3,2,1,0:T(8,128)(2,1)S(1)}, bf16[1,8,16,512]{3,2,1,0:T(8,128)(2,1)S(1)}, u32[]{:S(2)}, u32[]{:S(2)}) collective-permute-start(bf16[1,8,16,512]{3,2,1,0:T(8,128)(2,1)S(1)} %get-tuple-element.54), channel_id=1, source_target_pairs={{0,1},{1,0},{2,3},{3,2},{4,5},{5,4},{6,7},{7,6},{8,9},{9,8},{10,11... | collective-permute-start | bytes 393224 | tf_op jit(solution)/shard_map/ppermute | solution.py:433
  42.2 21.2 %collective-permute-start.15 = (bf16[8,16,512]{2,1,0:T(8,128)(2,1)S(1)}, bf16[8,16,512]{2,1,0:T(8,128)(2,1)S(1)}, u32[]{:S(2)}, u32[]{:S(2)}) collective-permute-start(bf16[8,16,512]{2,1,0:T(8,128)(2,1)S(1)} %get-tuple-element.55), channel_id=1, source_target_pairs={{0,8},{1,11},{2,10},{3,9},{4,12},{5,15},{6,14},{7,13},{8,0},{9,3},... | collective-permute-start | bytes 393224 | tf_op jit(solution)/shard_map/ppermute | solution.py:462
  47.8 17.3 %collective-permute-start.16 = (bf16[8,16,512]{2,1,0:T(8,128)(2,1)S(1)}, bf16[8,16,512]{2,1,0:T(8,128)(2,1)S(1)}, u32[]{:S(2)}, u32[]{:S(2)}) collective-permute-start(bf16[8,16,512]{2,1,0:T(8,128)(2,1)S(1)} %get-tuple-element.56), channel_id=1, source_target_pairs={{0,9},{1,10},{2,11},{3,8},{4,13},{5,14},{6,15},{7,12},{8,1},{9,2},... | collective-permute-start | bytes 393224 | tf_op jit(solution)/shard_map/ppermute | solution.py:462
  48.9 16.9 %collective-permute-start.8 = (bf16[8,16,512]{2,1,0:T(8,128)(2,1)S(1)}, bf16[8,16,512]{2,1,0:T(8,128)(2,1)S(1)}, u32[]{:S(2)}, u32[]{:S(2)}) collective-permute-start(bf16[8,16,512]{2,1,0:T(8,128)(2,1)S(1)} %get-tuple-element.47), channel_id=1, source_target_pairs={{0,12},{1,15},{2,14},{3,13},{4,8},{5,11},{6,10},{7,9},{8,4},{9,7},... | collective-permute-start | bytes 393224 | tf_op jit(solution)/shard_map/ppermute | solution.py:462
  49.8 19.4 %collective-permute-start.9 = (bf16[8,16,512]{2,1,0:T(8,128)(2,1)S(1)}, bf16[8,16,512]{2,1,0:T(8,128)(2,1)S(1)}, u32[]{:S(2)}, u32[]{:S(2)}) collective-permute-start(bf16[8,16,512]{2,1,0:T(8,128)(2,1)S(1)} %get-tuple-element.48), channel_id=1, source_target_pairs={{0,13},{1,14},{2,15},{3,12},{4,9},{5,10},{6,11},{7,8},{8,5},{9,6},... | collective-permute-start | bytes 393224 | tf_op jit(solution)/shard_map/ppermute | solution.py:462
  54.9 14.3 %collective-permute-start.10 = (bf16[8,16,512]{2,1,0:T(8,128)(2,1)S(1)}, bf16[8,16,512]{2,1,0:T(8,128)(2,1)S(1)}, u32[]{:S(2)}, u32[]{:S(2)}) collective-permute-start(bf16[8,16,512]{2,1,0:T(8,128)(2,1)S(1)} %get-tuple-element.49), channel_id=1, source_target_pairs={{0,4},{1,7},{2,6},{3,5},{4,0},{5,3},{6,2},{7,1},{8,12},{9,15},{10,... | collective-permute-start | bytes 393224 | tf_op jit(solution)/shard_map/ppermute | solution.py:462
  63.3 7.8 %collective-permute-start.11 = (bf16[8,16,512]{2,1,0:T(8,128)(2,1)S(1)}, bf16[8,16,512]{2,1,0:T(8,128)(2,1)S(1)}, u32[]{:S(2)}, u32[]{:S(2)}) collective-permute-start(bf16[8,16,512]{2,1,0:T(8,128)(2,1)S(1)} %get-tuple-element.50), channel_id=1, source_target_pairs={{0,5},{1,6},{2,7},{3,4},{4,1},{5,2},{6,3},{7,0},{8,13},{9,14},{10,... | collective-permute-start | bytes 393224 | tf_op jit(solution)/shard_map/ppermute | solution.py:462
  65.1 6.0 %collective-permute-start.12 = (bf16[8,16,512]{2,1,0:T(8,128)(2,1)S(1)}, bf16[8,16,512]{2,1,0:T(8,128)(2,1)S(1)}, u32[]{:S(2)}, u32[]{:S(2)}) collective-permute-start(bf16[8,16,512]{2,1,0:T(8,128)(2,1)S(1)} %get-tuple-element.51), channel_id=1, source_target_pairs={{0,0},{1,3},{2,2},{3,1},{4,4},{5,7},{6,6},{7,5},{8,8},{9,11},{10,1... | collective-permute-start | bytes 393224 | tf_op jit(solution)/shard_map/ppermute | solution.py:462
  65.8 7.8 %collective-permute-start.13 = (bf16[8,16,512]{2,1,0:T(8,128)(2,1)S(1)}, bf16[8,16,512]{2,1,0:T(8,128)(2,1)S(1)}, u32[]{:S(2)}, u32[]{:S(2)}) collective-permute-start(bf16[8,16,512]{2,1,0:T(8,128)(2,1)S(1)} %get-tuple-element.52), channel_id=1, source_target_pairs={{0,1},{1,2},{2,3},{3,0},{4,5},{5,6},{6,7},{7,4},{8,9},{9,10},{10,1... | collective-permute-start | bytes 393224 | tf_op jit(solution)/shard_map/ppermute | solution.py:462

commit v2 on v1

--- a/solution.py
+++ b/solution.py
@@ -415,7 +415,7 @@
             [],
         )(*[came[k] for k in group], gain, win)
 
-    lead, *others = row_order(n)
+    lead, *others = (row for rows in row_plan(n) for row in rows)
 
     def kept(count):
         return array((count, piece, columns, width), bf16)
@@ -477,9 +477,8 @@
     )
     got = swap(give)
     packed = project_kept(keep)
-    cut = n // 4 - 1
-    for rows in ([*range(cut)], [*range(cut, len(others))]):
-        finish(rows, [others[row] for row in rows], keep, got, packed)
+    for rows in row_plan(n)[1:]:
+        finish([others.index(row) for row in rows], rows, keep, got, packed)
 
     def join(values, senders, base=None):
         count = len(values)
@@ -525,8 +524,9 @@
     return general_body(video, norm_gain, qkv_weight, out_weight)
 
 
-def row_order(n):
-    return [*range(n // 4, n // 2), *range(n // 4 - 1, -1, -1)]
+def row_plan(n):
+    half = n // 4
+    return [[2 * half - 1], [*range(2 * half - 2, half - 1, -1), *range(half - 1, 0, -1)], [0]]
 
 
 def arrival_groups(n):
@@ -534,7 +534,8 @@
     return [
         [0, 1, *range(half, half + quarter)],
         [*range(2, half)],
-        [*range(half + quarter, n)],
+        [*range(half + quarter, n - 1)],
+        [n - 1],
     ]
 
 

time: 74.9 us -> 76.4 us (1.020)
  starting transfers between devices: 28.5 us -> 35.1 us
  waiting for transfers between devices: 24.2 us -> 18.8 us
    ppermute x8, starting transfers between devices: 13.3 us -> 19.3 us  [finish(): arrived.append(lax.ppermute(results[2 * index + flip], ('aa', 'ba'), route))]
    ppermute x8, waiting for transfers between devices: 14.5 us -> 9.79 us  [finish(): arrived.append(lax.ppermute(results[2 * index + flip], ('aa', 'ba'), route))]
    pallas_call x2 -> x3, Pallas kernels: 1.67 us -> 2.11 us  [fast_body(): call(functools.partial(group_kernel, 1, len(group)), [array((len(group) *...]
  transfers between devices with their start and end apart: 17 -> 17, of which waited for: 7 -> 8; matrix products, arithmetic and copies ran while one was open for 0% -> 0% of each run, Pallas kernels for 13% -> 13%
where the time goes in v2:
time: 76.4 us; the launch traced here: 76.2 us
  starting transfers between devices  35.1 us (46%)
  Pallas kernels  21.9 us (29%)
  waiting for transfers between devices  18.8 us (25%)
    ppermute x8, starting transfers between devices, finish(): arrived.append(lax.ppermute(results[2 * index + flip], ('aa', 'ba'), route))  19.3 us
    ppermute x7, starting transfers between devices, fast_body(): came[k] = lax.ppermute(sent[k], 'aa', [(i, i ^ k) for i in range(n)])  15.2 us
    ppermute x8, waiting for transfers between devices, finish(): arrived.append(lax.ppermute(results[2 * index + flip], ('aa', 'ba'), route))  9.79 us
    ppermute x7, waiting for transfers between devices, fast_body(): came[k] = lax.ppermute(sent[k], 'aa', [(i, i ^ k) for i in range(n)])  8.92 us
    pallas_call x1, Pallas kernels, fast_body(): call(functools.partial(first_kernel, 0), [message] * n, [HBM] * 4, [pltpu...  7.58 us
    pallas_call x3, Pallas kernels, finish(): call(functools.partial(last_kernel, 2, rows), [message] * (2 * len(rows))...  3.92 us
    pallas_call x1, Pallas kernels, fast_body(): call(functools.partial(weights_kernel, later), [array(gain_shape, f32)] +...  2.2 us
    pallas_call x3, Pallas kernels, fast_body(): call(functools.partial(group_kernel, 1, len(group)), [array((len(group) *...  2.11 us
  transfers between devices with their start and end apart: 17, of which 8 were waited for; matrix products, arithmetic and copies ran while one was open for 0% of the time, Pallas kernels for 13%

profile of v2, /device:TPU:0, one launch (start us, length us, event | category | flops | bytes accessed | tf_op | source)
XLA Modules:
  0.0 76.2 jit_solution(1596018716902418423)
XLA Ops:
  0.0 7.6 %shard_map.46 = (bf16[8,16,512]{2,1,0:T(8,128)(2,1)S(1)}, bf16[8,16,512]{2,1,0:T(8,128)(2,1)S(1)}, bf16[8,16,512]{2,1,0:T(8,128)(2,1)S(1)}, bf16[8,16,512]{2,1,0...) custom-call(bf16[64,16,512]{2,1,0:T(8,128)(2,1)} %bitcast.4, ...), custom_call_target="tpu_custom_call" | custom-call | tf_op jit(solution)/shard_map/pallas_call | solution.py:377
  7.6 3.1 %collective-permute-start.1 = (bf16[8,16,512]{2,1,0:T(8,128)(2,1)S(1)}, bf16[8,16,512]{2,1,0:T(8,128)(2,1)S(1)}, u32[]{:S(2)}, u32[]{:S(2)}) collective-permute-start(bf16[8,16,512]{2,1,0:T(8,128)(2,1)S(1)} %get-tuple-element.33), channel_id=1, source_target_pairs={{0,4},{2,6},{4,0},{6,2},{8,12},{10,14},{12,8},{14,10},{1,5},{3,7},... | collective-permute-start | bytes 393224 | tf_op jit(solution)/shard_map/ppermute | solution.py:397
  10.7 2.5 %collective-permute-start.5 = (bf16[8,16,512]{2,1,0:T(8,128)(2,1)S(1)}, bf16[8,16,512]{2,1,0:T(8,128)(2,1)S(1)}, u32[]{:S(2)}, u32[]{:S(2)}) collective-permute-start(bf16[8,16,512]{2,1,0:T(8,128)(2,1)S(1)} %get-tuple-element.37), channel_id=1, source_target_pairs={{0,12},{2,14},{4,8},{6,10},{8,4},{10,6},{12,0},{14,2},{1,13},{3,15... | collective-permute-start | bytes 393224 | tf_op jit(solution)/shard_map/ppermute | solution.py:397
  13.2 1.5 %collective-permute-start = (bf16[8,16,512]{2,1,0:T(8,128)(2,1)S(1)}, bf16[8,16,512]{2,1,0:T(8,128)(2,1)S(1)}, u32[]{:S(2)}, u32[]{:S(2)}) collective-permute-start(bf16[8,16,512]{2,1,0:T(8,128)(2,1)S(1)} %get-tuple-element.32), channel_id=1, source_target_pairs={{0,2},{2,0},{4,6},{6,4},{8,10},{10,8},{12,14},{14,12},{1,3},{3,1},... | collective-permute-start | bytes 393224 | tf_op jit(solution)/shard_map/ppermute | solution.py:397
  14.7 0.6 collective-permute-start.2
  15.3 1.2 %collective-permute-start.3 = (bf16[8,16,512]{2,1,0:T(8,128)(2,1)S(1)}, bf16[8,16,512]{2,1,0:T(8,128)(2,1)S(1)}, u32[]{:S(2)}, u32[]{:S(2)}) collective-permute-start(bf16[8,16,512]{2,1,0:T(8,128)(2,1)S(1)} %get-tuple-element.35), channel_id=1, source_target_pairs={{0,8},{2,10},{4,12},{6,14},{8,0},{10,2},{12,4},{14,6},{1,9},{3,11}... | collective-permute-start | bytes 393224 | tf_op jit(solution)/shard_map/ppermute | solution.py:397
  16.6 0.0 collective-permute-done.1.rest_0_.rest_2_
  16.6 3.7 %collective-permute-start.4 = (bf16[8,16,512]{2,1,0:T(8,128)(2,1)S(1)}, bf16[8,16,512]{2,1,0:T(8,128)(2,1)S(1)}, u32[]{:S(2)}, u32[]{:S(2)}) collective-permute-start(bf16[8,16,512]{2,1,0:T(8,128)(2,1)S(1)} %get-tuple-element.36), channel_id=1, source_target_pairs={{0,10},{2,8},{4,14},{6,12},{8,2},{10,0},{12,6},{14,4},{1,11},{3,9}... | collective-permute-start | bytes 393224 | tf_op jit(solution)/shard_map/ppermute | solution.py:397
  20.3 0.1 collective-permute-done.5.rest_0_.rest_6_
  20.3 2.6 %collective-permute-start.6 = (bf16[8,16,512]{2,1,0:T(8,128)(2,1)S(1)}, bf16[8,16,512]{2,1,0:T(8,128)(2,1)S(1)}, u32[]{:S(2)}, u32[]{:S(2)}) collective-permute-start(bf16[8,16,512]{2,1,0:T(8,128)(2,1)S(1)} %get-tuple-element.38), channel_id=1, source_target_pairs={{0,14},{2,12},{4,10},{6,8},{8,6},{10,4},{12,2},{14,0},{1,15},{3,13... | collective-permute-start | bytes 393224 | tf_op jit(solution)/shard_map/ppermute | solution.py:397
  22.9 2.2 %shard_map.47 = (f32[3,512]{1,0:T(4,128)S(1)}, bf16[512,1536]{1,0:T(8,128)(2,1)S(1)}, bf16[512,512]{1,0:T(8,128)(2,1)S(1)}, bf16[512,1536]{1,0:T(8,128)(2,1)S(1)}, bf16[512,512]{1,0:T(8,128)(2,1)S(1)}) custom-call(f32[3,512]{1,0:T(4,128)} %gain_hbm.3, bf16[3,512,1536]{2,1,0:T(8,128)(2,1)} %win_hbm.3, bf16[3,512,512]{2,1,0:T(8,128)(2,1)} %wout_hbm.3), custom_call_target="tpu_custom_call" | custom-call | tf_op jit(solution)/shard_map/pallas_call | solution.py:400
  25.1 0.4 shard_map.50.rest_10_
  25.5 0.0 collective-permute-done.2.rest_1_.rest_3_
  25.6 0.6 shard_map.49.rest_9_
  26.2 0.0 collective-permute-done.rest_1_.rest_5_
  26.2 5.1 %collective-permute-done.3.rest_2_.rest_4_.rest_0_ = bf16[8,16,512]{2,1,0:T(8,128)(2,1)S(1)} collective-permute-done((bf16[8,16,512]{2,1,0:T(8,128)(2,1)S(1)}, bf16[8,16,512]{2,1,0:T(8,128)(2,1)S(1)}, u32[]{:S(2)}, u32[]{:S(2)}) %collective-permute-start.3) | collective-permute-done | bytes 131104 | tf_op jit(solution)/shard_map/ppermute | solution.py:397
  31.3 3.8 %collective-permute-done.4.rest_3_.rest_5_.rest_1_ = bf16[8,16,512]{2,1,0:T(8,128)(2,1)S(1)} collective-permute-done((bf16[8,16,512]{2,1,0:T(8,128)(2,1)S(1)}, bf16[8,16,512]{2,1,0:T(8,128)(2,1)S(1)}, u32[]{:S(2)}, u32[]{:S(2)}) %collective-permute-start.4) | collective-permute-done | bytes 131104 | tf_op jit(solution)/shard_map/ppermute | solution.py:397
  35.1 1.0 %shard_map.48.rest_8_ = bf16[512,1536]{1,0:T(8,128)(2,1)S(1)} custom-call(bf16[8,16,512]{2,1,0:T(8,128)(2,1)S(1)} %get-tuple-element.31.rest_0_.rest_4_, bf16[8,16,512]{2,1,0:T(8,128)(2,1)S(1)} %collective-permute-done.rest_1_.rest_5_, bf16[8,16,512]{2,1,0:T(8,128)(2,1)S(1)} %collective-permute-done.3.rest_2_.rest_4_.rest_0_, ...), custom_call_target="tpu_custom_call" | custom-call | tf_op jit(solution)/shard_map/pallas_call | solution.py:411
  36.1 0.0 collective-permute-done.6.rest_7_
  36.1 2.1 %shard_map.51 = (bf16[1024,512]{1,0:T(8,128)(2,1)S(1)}, bf16[1,8,16,512]{3,2,1,0:T(8,128)(2,1)S(1)}, bf16[1,8,16,512]{3,2,1,0:T(8,128)(2,1)S(1)}) custom-call(bf16[8,16,512]{2,1,0:T(8,128)(2,1)S(1)} %get-tuple-element.31.rest_0_.rest_4_, bf16[8,16,512]{2,1,0:T(8,128)(2,1)S(1)} %collective-permute-done.rest_1_.rest_5_, ...), custom_call_target="tpu_custom_call" | custom-call | tf_op jit(solution)/shard_map/pallas_call | solution.py:423
  38.2 1.1 %shard_map.52 = (bf16[3,8,16,512]{3,2,1,0:T(8,128)(2,1)S(1)}, bf16[3,8,16,512]{3,2,1,0:T(8,128)(2,1)S(1)}) custom-call(bf16[1024,512]{1,0:T(8,128)(2,1)S(1)} %get-tuple-element.42.mixed, bf16[512,512]{1,0:T(8,128)(2,1)S(1)} %get-tuple-element.41.rest_13_.wout, bf16[8,16,512]{2,1,0:T(8,128)(2,1)S(1)} %collective-permute-done.3.rest_2_.rest_4_.rest_0_, ...), custom_call_target="tpu_custom_call" | custom-call | tf_op jit(solution)/shard_map/pallas_call | solution.py:468
  39.3 0.1 collective-permute-start.7
  39.4 0.5 collective-permute-start.14
  39.9 0.4 shard_map.56.kept_packed
  40.4 0.8 %shard_map.53.kept_packed = bf16[384,1536]{1,0:T(8,128)(2,1)S(1)} custom-call(bf16[3,8,16,512]{3,2,1,0:T(8,128)(2,1)S(1)} %get-tuple-element.43.keep_ref, f32[3,512]{1,0:T(4,128)S(1)} %get-tuple-element.39.rest_4_.rest_2_.rest_1_.rest_11_.gain_ref, bf16[512,1536]{1,0:T(8,128)(2,1)S(1)} %get-tuple-element.45.win), custom_call_target="tpu_custom_call" | custom-call | tf_op jit(solution)/shard_map/pallas_call | solution.py:437
  41.2 0.1 collective-permute-done.14.got_ref
  41.3 1.1 %shard_map.57 = (bf16[8,16,512]{2,1,0:T(8,128)(2,1)S(1)}, bf16[8,16,512]{2,1,0:T(8,128)(2,1)S(1)}) custom-call(bf16[1,8,16,512]{3,2,1,0:T(8,128)(2,1)S(1)} %get-tuple-element.53.keep_ref, bf16[1,8,16,512]{3,2,1,0:T(8,128)(2,1)S(1)} %collective-permute-done.14.got_ref, bf16[128,1536]{1,0:T(8,128)(2,1)S(1)} %shard_map.56.kept_packed, ...), custom_call_target="tpu_custom_call" | custom-call | tf_op jit(solution)/shard_map/pallas_call | solution.py:446
  42.4 3.1 %collective-permute-start.15 = (bf16[8,16,512]{2,1,0:T(8,128)(2,1)S(1)}, bf16[8,16,512]{2,1,0:T(8,128)(2,1)S(1)}, u32[]{:S(2)}, u32[]{:S(2)}) collective-permute-start(bf16[8,16,512]{2,1,0:T(8,128)(2,1)S(1)} %get-tuple-element.55), channel_id=1, source_target_pairs={{0,12},{1,15},{2,14},{3,13},{4,8},{5,11},{6,10},{7,9},{8,4},{9,7},... | collective-permute-start | bytes 393224 | tf_op jit(solution)/shard_map/ppermute | solution.py:462
  45.5 0.2 collective-permute-start.16
  45.7 0.0 collective-permute-done.7.got_ref
  45.7 1.1 %shard_map.55 = (bf16[8,16,512]{2,1,0:T(8,128)(2,1)S(1)}, bf16[8,16,512]{2,1,0:T(8,128)(2,1)S(1)}) custom-call(bf16[3,8,16,512]{3,2,1,0:T(8,128)(2,1)S(1)} %get-tuple-element.43.keep_ref, bf16[3,8,16,512]{3,2,1,0:T(8,128)(2,1)S(1)} %collective-permute-done.7.got_ref, bf16[384,1536]{1,0:T(8,128)(2,1)S(1)} %shard_map.53.kept_packed, ...), custom_call_target="tpu_custom_call" | custom-call | tf_op jit(solution)/shard_map/pallas_call | solution.py:446
  46.9 0.7 collective-permute-start.12
  47.5 3.2 %collective-permute-start.13 = (bf16[8,16,512]{2,1,0:T(8,128)(2,1)S(1)}, bf16[8,16,512]{2,1,0:T(8,128)(2,1)S(1)}, u32[]{:S(2)}, u32[]{:S(2)}) collective-permute-start(bf16[8,16,512]{2,1,0:T(8,128)(2,1)S(1)} %get-tuple-element.52), channel_id=1, source_target_pairs={{0,1},{1,2},{2,3},{3,0},{4,5},{5,6},{6,7},{7,4},{8,9},{9,10},{10,1... | collective-permute-start | bytes 393224 | tf_op jit(solution)/shard_map/ppermute | solution.py:462
  50.7 1.7 %shard_map.54 = (bf16[8,16,512]{2,1,0:T(8,128)(2,1)S(1)}, bf16[8,16,512]{2,1,0:T(8,128)(2,1)S(1)}, bf16[8,16,512]{2,1,0:T(8,128)(2,1)S(1)}, bf16[8,16,512]{2,1,0:T(8,128)(2,1)S(1)}) custom-call(bf16[3,8,16,512]{3,2,1,0:T(8,128)(2,1)S(1)} %get-tuple-element.43.keep_ref, bf16[3,8,16,512]{3,2,1,0:T(8,128)(2,1)S(1)} %collective-permute-done.7.got_ref, ...), custom_call_target="tpu_custom_call" | custom-call | tf_op jit(solution)/shard_map/pallas_call | solution.py:446
  52.4 1.0 %collective-permute-start.8 = (bf16[8,16,512]{2,1,0:T(8,128)(2,1)S(1)}, bf16[8,16,512]{2,1,0:T(8,128)(2,1)S(1)}, u32[]{:S(2)}, u32[]{:S(2)}) collective-permute-start(bf16[8,16,512]{2,1,0:T(8,128)(2,1)S(1)} %get-tuple-element.47), channel_id=1, source_target_pairs={{0,8},{1,11},{2,10},{3,9},{4,12},{5,15},{6,14},{7,13},{8,0},{9,3},... | collective-permute-start | bytes 393224 | tf_op jit(solution)/shard_map/ppermute | solution.py:462
  53.4 0.0 collective-permute-done.15.rest_0_
  53.4 3.3 %collective-permute-start.9 = (bf16[8,16,512]{2,1,0:T(8,128)(2,1)S(1)}, bf16[8,16,512]{2,1,0:T(8,128)(2,1)S(1)}, u32[]{:S(2)}, u32[]{:S(2)}) collective-permute-start(bf16[8,16,512]{2,1,0:T(8,128)(2,1)S(1)} %get-tuple-element.48), channel_id=1, source_target_pairs={{0,9},{1,10},{2,11},{3,8},{4,13},{5,14},{6,15},{7,12},{8,1},{9,2},... | collective-permute-start | bytes 393224 | tf_op jit(solution)/shard_map/ppermute | solution.py:462
  56.7 0.0 collective-permute-done.16.rest_1_
  56.7 7.8 %collective-permute-start.10 = (bf16[8,16,512]{2,1,0:T(8,128)(2,1)S(1)}, bf16[8,16,512]{2,1,0:T(8,128)(2,1)S(1)}, u32[]{:S(2)}, u32[]{:S(2)}) collective-permute-start(bf16[8,16,512]{2,1,0:T(8,128)(2,1)S(1)} %get-tuple-element.49), channel_id=1, source_target_pairs={{0,4},{1,7},{2,6},{3,5},{4,0},{5,3},{6,2},{7,1},{8,12},{9,15},{10,... | collective-permute-start | bytes 393224 | tf_op jit(solution)/shard_map/ppermute | solution.py:462
  64.6 0.0 collective-permute-done.12.rest_4_
  64.6 0.0 collective-permute-start.11
  64.6 0.7 join.2.rest_6_
  65.3 0.0 collective-permute-done.13.rest_5_
  65.3 1.5 %collective-permute-done.8.rest_0_ = bf16[8,16,512]{2,1,0:T(8,128)(2,1)S(1)} collective-permute-done((bf16[8,16,512]{2,1,0:T(8,128)(2,1)S(1)}, bf16[8,16,512]{2,1,0:T(8,128)(2,1)S(1)}, u32[]{:S(2)}, u32[]{:S(2)}) %collective-permute-start.8) | collective-permute-done | bytes 131104 | tf_op jit(solution)/shard_map/ppermute | solution.py:462
  66.8 2.8 %collective-permute-done.9.rest_1_ = bf16[8,16,512]{2,1,0:T(8,128)(2,1)S(1)} collective-permute-done((bf16[8,16,512]{2,1,0:T(8,128)(2,1)S(1)}, bf16[8,16,512]{2,1,0:T(8,128)(2,1)S(1)}, u32[]{:S(2)}, u32[]{:S(2)}) %collective-permute-start.9) | collective-permute-done | bytes 131104 | tf_op jit(solution)/shard_map/ppermute | solution.py:462
  69.6 2.0 %collective-permute-done.10.rest_2_ = bf16[8,16,512]{2,1,0:T(8,128)(2,1)S(1)} collective-permute-done((bf16[8,16,512]{2,1,0:T(8,128)(2,1)S(1)}, bf16[8,16,512]{2,1,0:T(8,128)(2,1)S(1)}, u32[]{:S(2)}, u32[]{:S(2)}) %collective-permute-start.10) | collective-permute-done | bytes 131104 | tf_op jit(solution)/shard_map/ppermute | solution.py:462
  71.6 3.5 %collective-permute-done.11.rest_3_ = bf16[8,16,512]{2,1,0:T(8,128)(2,1)S(1)} collective-permute-done((bf16[8,16,512]{2,1,0:T(8,128)(2,1)S(1)}, bf16[8,16,512]{2,1,0:T(8,128)(2,1)S(1)}, u32[]{:S(2)}, u32[]{:S(2)}) %collective-permute-start.11) | collective-permute-done | bytes 131104 | tf_op jit(solution)/shard_map/ppermute | solution.py:462
  75.1 0.9 %join.3 = bf16[64,16,512]{2,1,0:T(8,128)(2,1)} custom-call(bf16[8,16,512]{2,1,0:T(8,128)(2,1)S(1)} %collective-permute-done.8.rest_0_, bf16[8,16,512]{2,1,0:T(8,128)(2,1)S(1)} %collective-permute-done.9.rest_1_, bf16[8,16,512]{2,1,0:T(8,128)(2,1)S(1)} %collective-permute-done.10.rest_2_, ...), custom_call_target="tpu_custom_call", output_to_operand_aliasing={{}: (6, {})} | custom-call | tf_op jit(solution)/shard_map/join/pallas_call | solution.py:486
Async XLA Ops:
  7.6 9.0 %collective-permute-start.1 = (bf16[8,16,512]{2,1,0:T(8,128)(2,1)S(1)}, bf16[8,16,512]{2,1,0:T(8,128)(2,1)S(1)}, u32[]{:S(2)}, u32[]{:S(2)}) collective-permute-start(bf16[8,16,512]{2,1,0:T(8,128)(2,1)S(1)} %get-tuple-element.33), channel_id=1, source_target_pairs={{0,4},{2,6},{4,0},{6,2},{8,12},{10,14},{12,8},{14,10},{1,5},{3,7},... | collective-permute-start | bytes 393224 | tf_op jit(solution)/shard_map/ppermute | solution.py:397
  10.7 9.6 %collective-permute-start.5 = (bf16[8,16,512]{2,1,0:T(8,128)(2,1)S(1)}, bf16[8,16,512]{2,1,0:T(8,128)(2,1)S(1)}, u32[]{:S(2)}, u32[]{:S(2)}) collective-permute-start(bf16[8,16,512]{2,1,0:T(8,128)(2,1)S(1)} %get-tuple-element.37), channel_id=1, source_target_pairs={{0,12},{2,14},{4,8},{6,10},{8,4},{10,6},{12,0},{14,2},{1,13},{3,15... | collective-permute-start | bytes 393224 | tf_op jit(solution)/shard_map/ppermute | solution.py:397
  13.2 13.0 %collective-permute-start = (bf16[8,16,512]{2,1,0:T(8,128)(2,1)S(1)}, bf16[8,16,512]{2,1,0:T(8,128)(2,1)S(1)}, u32[]{:S(2)}, u32[]{:S(2)}) collective-permute-start(bf16[8,16,512]{2,1,0:T(8,128)(2,1)S(1)} %get-tuple-element.32), channel_id=1, source_target_pairs={{0,2},{2,0},{4,6},{6,4},{8,10},{10,8},{12,14},{14,12},{1,3},{3,1},... | collective-permute-start | bytes 393224 | tf_op jit(solution)/shard_map/ppermute | solution.py:397
  14.7 10.8 %collective-permute-start.2 = (bf16[8,16,512]{2,1,0:T(8,128)(2,1)S(1)}, bf16[8,16,512]{2,1,0:T(8,128)(2,1)S(1)}, u32[]{:S(2)}, u32[]{:S(2)}) collective-permute-start(bf16[8,16,512]{2,1,0:T(8,128)(2,1)S(1)} %get-tuple-element.34), channel_id=1, source_target_pairs={{0,6},{2,4},{4,2},{6,0},{8,14},{10,12},{12,10},{14,8},{1,7},{3,5},... | collective-permute-start | bytes 393224 | tf_op jit(solution)/shard_map/ppermute | solution.py:397
  15.3 16.0 %collective-permute-start.3 = (bf16[8,16,512]{2,1,0:T(8,128)(2,1)S(1)}, bf16[8,16,512]{2,1,0:T(8,128)(2,1)S(1)}, u32[]{:S(2)}, u32[]{:S(2)}) collective-permute-start(bf16[8,16,512]{2,1,0:T(8,128)(2,1)S(1)} %get-tuple-element.35), channel_id=1, source_target_pairs={{0,8},{2,10},{4,12},{6,14},{8,0},{10,2},{12,4},{14,6},{1,9},{3,11}... | collective-permute-start | bytes 393224 | tf_op jit(solution)/shard_map/ppermute | solution.py:397
  16.6 18.5 %collective-permute-start.4 = (bf16[8,16,512]{2,1,0:T(8,128)(2,1)S(1)}, bf16[8,16,512]{2,1,0:T(8,128)(2,1)S(1)}, u32[]{:S(2)}, u32[]{:S(2)}) collective-permute-start(bf16[8,16,512]{2,1,0:T(8,128)(2,1)S(1)} %get-tuple-element.36), channel_id=1, source_target_pairs={{0,10},{2,8},{4,14},{6,12},{8,2},{10,0},{12,6},{14,4},{1,11},{3,9}... | collective-permute-start | bytes 393224 | tf_op jit(solution)/shard_map/ppermute | solution.py:397
  20.3 15.8 %collective-permute-start.6 = (bf16[8,16,512]{2,1,0:T(8,128)(2,1)S(1)}, bf16[8,16,512]{2,1,0:T(8,128)(2,1)S(1)}, u32[]{:S(2)}, u32[]{:S(2)}) collective-permute-start(bf16[8,16,512]{2,1,0:T(8,128)(2,1)S(1)} %get-tuple-element.38), channel_id=1, source_target_pairs={{0,14},{2,12},{4,10},{6,8},{8,6},{10,4},{12,2},{14,0},{1,15},{3,13... | collective-permute-start | bytes 393224 | tf_op jit(solution)/shard_map/ppermute | solution.py:397
  39.3 6.4 %collective-permute-start.7 = (bf16[3,8,16,512]{3,2,1,0:T(8,128)(2,1)S(1)}, bf16[3,8,16,512]{3,2,1,0:T(8,128)(2,1)S(1)}, u32[]{:S(2)}, u32[]{:S(2)}) collective-permute-start(bf16[3,8,16,512]{3,2,1,0:T(8,128)(2,1)S(1)} %get-tuple-element.44), channel_id=1, source_target_pairs={{0,1},{1,0},{2,3},{3,2},{4,5},{5,4},{6,7},{7,6},{8,9},{9,8},{10,11... | collective-permute-start | bytes 1179656 | tf_op jit(solution)/shard_map/ppermute | solution.py:433
  39.4 1.9 %collective-permute-start.14 = (bf16[1,8,16,512]{3,2,1,0:T(8,128)(2,1)S(1)}, bf16[1,8,16,512]{3,2,1,0:T(8,128)(2,1)S(1)}, u32[]{:S(2)}, u32[]{:S(2)}) collective-permute-start(bf16[1,8,16,512]{3,2,1,0:T(8,128)(2,1)S(1)} %get-tuple-element.54), channel_id=1, source_target_pairs={{0,1},{1,0},{2,3},{3,2},{4,5},{5,4},{6,7},{7,6},{8,9},{9,8},{10,11... | collective-permute-start | bytes 393224 | tf_op jit(solution)/shard_map/ppermute | solution.py:433
  42.4 11.0 %collective-permute-start.15 = (bf16[8,16,512]{2,1,0:T(8,128)(2,1)S(1)}, bf16[8,16,512]{2,1,0:T(8,128)(2,1)S(1)}, u32[]{:S(2)}, u32[]{:S(2)}) collective-permute-start(bf16[8,16,512]{2,1,0:T(8,128)(2,1)S(1)} %get-tuple-element.55), channel_id=1, source_target_pairs={{0,12},{1,15},{2,14},{3,13},{4,8},{5,11},{6,10},{7,9},{8,4},{9,7},... | collective-permute-start | bytes 393224 | tf_op jit(solution)/shard_map/ppermute | solution.py:462
  45.5 11.2 %collective-permute-start.16 = (bf16[8,16,512]{2,1,0:T(8,128)(2,1)S(1)}, bf16[8,16,512]{2,1,0:T(8,128)(2,1)S(1)}, u32[]{:S(2)}, u32[]{:S(2)}) collective-permute-start(bf16[8,16,512]{2,1,0:T(8,128)(2,1)S(1)} %get-tuple-element.56), channel_id=1, source_target_pairs={{0,13},{1,14},{2,15},{3,12},{4,9},{5,10},{6,11},{7,8},{8,5},{9,6},... | collective-permute-start | bytes 393224 | tf_op jit(solution)/shard_map/ppermute | solution.py:462
  46.9 17.7 %collective-permute-start.12 = (bf16[8,16,512]{2,1,0:T(8,128)(2,1)S(1)}, bf16[8,16,512]{2,1,0:T(8,128)(2,1)S(1)}, u32[]{:S(2)}, u32[]{:S(2)}) collective-permute-start(bf16[8,16,512]{2,1,0:T(8,128)(2,1)S(1)} %get-tuple-element.51), channel_id=1, source_target_pairs={{0,0},{1,3},{2,2},{3,1},{4,4},{5,7},{6,6},{7,5},{8,8},{9,11},{10,1... | collective-permute-start | bytes 393224 | tf_op jit(solution)/shard_map/ppermute | solution.py:462
  47.5 17.8 %collective-permute-start.13 = (bf16[8,16,512]{2,1,0:T(8,128)(2,1)S(1)}, bf16[8,16,512]{2,1,0:T(8,128)(2,1)S(1)}, u32[]{:S(2)}, u32[]{:S(2)}) collective-permute-start(bf16[8,16,512]{2,1,0:T(8,128)(2,1)S(1)} %get-tuple-element.52), channel_id=1, source_target_pairs={{0,1},{1,2},{2,3},{3,0},{4,5},{5,6},{6,7},{7,4},{8,9},{9,10},{10,1... | collective-permute-start | bytes 393224 | tf_op jit(solution)/shard_map/ppermute | solution.py:462
  52.4 14.4 %collective-permute-start.8 = (bf16[8,16,512]{2,1,0:T(8,128)(2,1)S(1)}, bf16[8,16,512]{2,1,0:T(8,128)(2,1)S(1)}, u32[]{:S(2)}, u32[]{:S(2)}) collective-permute-start(bf16[8,16,512]{2,1,0:T(8,128)(2,1)S(1)} %get-tuple-element.47), channel_id=1, source_target_pairs={{0,8},{1,11},{2,10},{3,9},{4,12},{5,15},{6,14},{7,13},{8,0},{9,3},... | collective-permute-start | bytes 393224 | tf_op jit(solution)/shard_map/ppermute | solution.py:462
  53.4 16.2 %collective-permute-start.9 = (bf16[8,16,512]{2,1,0:T(8,128)(2,1)S(1)}, bf16[8,16,512]{2,1,0:T(8,128)(2,1)S(1)}, u32[]{:S(2)}, u32[]{:S(2)}) collective-permute-start(bf16[8,16,512]{2,1,0:T(8,128)(2,1)S(1)} %get-tuple-element.48), channel_id=1, source_target_pairs={{0,9},{1,10},{2,11},{3,8},{4,13},{5,14},{6,15},{7,12},{8,1},{9,2},... | collective-permute-start | bytes 393224 | tf_op jit(solution)/shard_map/ppermute | solution.py:462
  56.7 14.8 %collective-permute-start.10 = (bf16[8,16,512]{2,1,0:T(8,128)(2,1)S(1)}, bf16[8,16,512]{2,1,0:T(8,128)(2,1)S(1)}, u32[]{:S(2)}, u32[]{:S(2)}) collective-permute-start(bf16[8,16,512]{2,1,0:T(8,128)(2,1)S(1)} %get-tuple-element.49), channel_id=1, source_target_pairs={{0,4},{1,7},{2,6},{3,5},{4,0},{5,3},{6,2},{7,1},{8,12},{9,15},{10,... | collective-permute-start | bytes 393224 | tf_op jit(solution)/shard_map/ppermute | solution.py:462
  64.6 10.5 %collective-permute-start.11 = (bf16[8,16,512]{2,1,0:T(8,128)(2,1)S(1)}, bf16[8,16,512]{2,1,0:T(8,128)(2,1)S(1)}, u32[]{:S(2)}, u32[]{:S(2)}) collective-permute-start(bf16[8,16,512]{2,1,0:T(8,128)(2,1)S(1)} %get-tuple-element.50), channel_id=1, source_target_pairs={{0,5},{1,6},{2,7},{3,4},{4,1},{5,2},{6,3},{7,0},{8,13},{9,14},{10,... | collective-permute-start | bytes 393224 | tf_op jit(solution)/shard_map/ppermute | solution.py:462

commit v3 on v2

--- a/solution.py
+++ b/solution.py
@@ -131,42 +131,47 @@
     n = len(rest) - 9
     outs = rest[:n]
     win, wout, natural, lined, packed, mixed, sems, x_ref, gain_ref = rest[n:]
-    frames, columns, width = x_ref.shape
+    parts, frames, cut, width = x_ref.shape
+    columns = parts * cut
     tokens = frames * columns
-    loads = [
-        pltpu.make_async_copy(source, target, sems.at[index])
-        for index, (source, target) in enumerate(
-            (
-                (x_hbm, x_ref),
-                (gain_hbm, gain_ref),
-                (win_hbm.at[block], win),
-                (wout_hbm.at[block], wout),
-            )
-        )
-    ]
-    for load in loads:
-        load.start()
-    loads[0].wait()
-    loads[1].wait()
-    for at, lanes in enumerate(lanes_of(x_ref[...].reshape(tokens, width).astype(jnp.float32))):
-        natural[at] = lanes
+    loads = load_all(
+        (
+            *((x_hbm.at[:, pl.ds(part * cut, cut)], x_ref.at[part]) for part in range(parts)),
+            (gain_hbm, gain_ref),
+            (win_hbm.at[block], win),
+            (wout_hbm.at[block], wout),
+        ),
+        sems,
+    )
+    loads[parts].wait()
     gain = gain_ref[block : block + 1]
     group = 256 // frames
-    for column in range(0, columns, group):
-        pieces = []
-        for each in range(column, column + group):
-            floats = strided(natural, each, frames, columns)
+    for part in range(parts):
+        loads[part].wait()
+        floats = x_ref[part].reshape(frames * cut, width).astype(jnp.float32)
+        for at, lanes in enumerate(lanes_of(floats)):
+            natural[part * (width // LANES) + at] = lanes
+        mine = natural.at[pl.ds(part * (width // LANES), width // LANES)]
+        normed = []
+        for column in range(part * cut, (part + 1) * cut):
+            floats = strided(mine, column % cut, frames, cut)
             for at, lanes in enumerate(lanes_of(floats)):
-                lined[at, each * frames : (each + 1) * frames] = lanes
-            pieces.append(normalise(floats, gain))
-        if column == 0:
-            loads[2].wait()
-        project(jnp.concatenate(pieces, axis=0), win, packed, column * frames)
+                lined[at, column * frames : (column + 1) * frames] = lanes
+            normed.append(normalise(floats, gain))
+        if part == 0:
+            loads[parts + 1].wait()
+        for at in range(0, cut, group):
+            project(
+                jnp.concatenate(normed[at : at + group], axis=0),
+                win,
+                packed,
+                (part * cut + at) * frames,
+            )
     mask = line_mask(LANES, lambda i: i // frames)
     halves = lane_halves(LANES)
     for at in range(0, tokens, LANES):
         mixed[at : at + LANES] = tile_attention(packed[at : at + LANES], mask, halves)
-    loads[3].wait()
+    loads[parts + 2].wait()
     for at in range(0, tokens, 256):
         update = jnp.dot(mixed[at : at + 256], wout[...], preferred_element_type=jnp.float32)
         for index, lanes in enumerate(lanes_of(update)):
@@ -381,12 +386,12 @@
         [
             pltpu.VMEM(win_shape, bf16),
             pltpu.VMEM(wout_shape, bf16),
-            pltpu.VMEM((width // LANES, tokens, LANES), f32),
+            pltpu.VMEM((2 * width // LANES, tokens // 2, LANES), f32),
             pltpu.VMEM((width // LANES, tokens, LANES), f32),
             pltpu.VMEM((tokens, 3 * width), bf16),
             pltpu.VMEM((tokens, width), bf16),
-            pltpu.SemaphoreType.DMA((4,)),
-            pltpu.VMEM((frames, columns, width), bf16),
+            pltpu.SemaphoreType.DMA((5,)),
+            pltpu.VMEM((2, frames, columns // 2, width), bf16),
             pltpu.VMEM(gain_shape, f32),
         ],
         limit=24,
@@ -494,8 +499,10 @@
             compiler_params=pltpu.CompilerParams(vmem_limit_bytes=4 << 20),
         )(*values, *given)
 
-    out = join(arrived[:2], starts[:2])
-    out = join(arrived[2:], starts[2:], out)
+    slow = [index for index, (row, _) in enumerate(starts) if row == others[0]]
+    soon = [index for index in range(n) if index not in slow]
+    out = join([arrived[index] for index in soon], [starts[index] for index in soon])
+    out = join([arrived[index] for index in slow], [starts[index] for index in slow], out)
     return out.reshape(video.shape)
 
 

time: 76.4 us -> 72.1 us (0.944)
  waiting for transfers between devices: 18.8 us -> 16.6 us
  starting transfers between devices: 35.1 us -> 33.2 us
    ppermute x8, waiting for transfers between devices: 9.79 us -> 7.66 us  [finish(): arrived.append(lax.ppermute(results[2 * index + flip], ('aa', 'ba'), route))]
    ppermute x8, starting transfers between devices: 19.3 us -> 17.3 us  [finish(): arrived.append(lax.ppermute(results[2 * index + flip], ('aa', 'ba'), route))]
  transfers between devices with their start and end apart: 17 -> 17, of which waited for: 8 -> 5; matrix products, arithmetic and copies ran while one was open for 0% -> 0% of each run, Pallas kernels for 13% -> 15%
where the time goes in v3:
time: 72.1 us; the launch traced here: 71.9 us
  starting transfers between devices  33.2 us (46%)
  Pallas kernels  21.7 us (30%)
  waiting for transfers between devices  16.6 us (23%)
    ppermute x8, starting transfers between devices, finish(): arrived.append(lax.ppermute(results[2 * index + flip], ('aa', 'ba'), route))  17.3 us
    ppermute x7, starting transfers between devices, fast_body(): came[k] = lax.ppermute(sent[k], 'aa', [(i, i ^ k) for i in range(n)])  15.3 us
    ppermute x7, waiting for transfers between devices, fast_body(): came[k] = lax.ppermute(sent[k], 'aa', [(i, i ^ k) for i in range(n)])  8.88 us
    ppermute x8, waiting for transfers between devices, finish(): arrived.append(lax.ppermute(results[2 * index + flip], ('aa', 'ba'), route))  7.66 us
    pallas_call x1, Pallas kernels, fast_body(): call(functools.partial(first_kernel, 0), [message] * n, [HBM] * 4, [pltpu...  7.37 us
    pallas_call x3, Pallas kernels, finish(): call(functools.partial(last_kernel, 2, rows), [message] * (2 * len(rows))...  3.92 us
    pallas_call x1, Pallas kernels, fast_body(): call(functools.partial(weights_kernel, later), [array(gain_shape, f32)] +...  2.2 us
    pallas_call x3, Pallas kernels, fast_body(): call(functools.partial(group_kernel, 1, len(group)), [array((len(group) *...  2.11 us
  transfers between devices with their start and end apart: 17, of which 5 were waited for; matrix products, arithmetic and copies ran while one was open for 0% of the time, Pallas kernels for 15%

profile of v3, /device:TPU:0, one launch (start us, length us, event | category | flops | bytes accessed | tf_op | source)
XLA Modules:
  0.0 71.9 jit_solution(6828804097577450049)
XLA Ops:
  0.0 7.4 %shard_map.46 = (bf16[8,16,512]{2,1,0:T(8,128)(2,1)S(1)}, bf16[8,16,512]{2,1,0:T(8,128)(2,1)S(1)}, bf16[8,16,512]{2,1,0:T(8,128)(2,1)S(1)}, bf16[8,16,512]{2,1,0...) custom-call(bf16[64,16,512]{2,1,0:T(8,128)(2,1)} %bitcast.4, ...), custom_call_target="tpu_custom_call" | custom-call | tf_op jit(solution)/shard_map/pallas_call | solution.py:382
  7.4 3.1 %collective-permute-start.1 = (bf16[8,16,512]{2,1,0:T(8,128)(2,1)S(1)}, bf16[8,16,512]{2,1,0:T(8,128)(2,1)S(1)}, u32[]{:S(2)}, u32[]{:S(2)}) collective-permute-start(bf16[8,16,512]{2,1,0:T(8,128)(2,1)S(1)} %get-tuple-element.33), channel_id=1, source_target_pairs={{0,4},{2,6},{4,0},{6,2},{8,12},{10,14},{12,8},{14,10},{1,5},{3,7},... | collective-permute-start | bytes 393224 | tf_op jit(solution)/shard_map/ppermute | solution.py:402
  10.5 2.5 %collective-permute-start.5 = (bf16[8,16,512]{2,1,0:T(8,128)(2,1)S(1)}, bf16[8,16,512]{2,1,0:T(8,128)(2,1)S(1)}, u32[]{:S(2)}, u32[]{:S(2)}) collective-permute-start(bf16[8,16,512]{2,1,0:T(8,128)(2,1)S(1)} %get-tuple-element.37), channel_id=1, source_target_pairs={{0,12},{2,14},{4,8},{6,10},{8,4},{10,6},{12,0},{14,2},{1,13},{3,15... | collective-permute-start | bytes 393224 | tf_op jit(solution)/shard_map/ppermute | solution.py:402
  13.0 1.5 %collective-permute-start = (bf16[8,16,512]{2,1,0:T(8,128)(2,1)S(1)}, bf16[8,16,512]{2,1,0:T(8,128)(2,1)S(1)}, u32[]{:S(2)}, u32[]{:S(2)}) collective-permute-start(bf16[8,16,512]{2,1,0:T(8,128)(2,1)S(1)} %get-tuple-element.32), channel_id=1, source_target_pairs={{0,2},{2,0},{4,6},{6,4},{8,10},{10,8},{12,14},{14,12},{1,3},{3,1},... | collective-permute-start | bytes 393224 | tf_op jit(solution)/shard_map/ppermute | solution.py:402
  14.5 0.6 collective-permute-start.2
  15.1 1.2 %collective-permute-start.3 = (bf16[8,16,512]{2,1,0:T(8,128)(2,1)S(1)}, bf16[8,16,512]{2,1,0:T(8,128)(2,1)S(1)}, u32[]{:S(2)}, u32[]{:S(2)}) collective-permute-start(bf16[8,16,512]{2,1,0:T(8,128)(2,1)S(1)} %get-tuple-element.35), channel_id=1, source_target_pairs={{0,8},{2,10},{4,12},{6,14},{8,0},{10,2},{12,4},{14,6},{1,9},{3,11}... | collective-permute-start | bytes 393224 | tf_op jit(solution)/shard_map/ppermute | solution.py:402
  16.4 0.0 collective-permute-done.1.rest_0_.rest_2_
  16.4 3.7 %collective-permute-start.4 = (bf16[8,16,512]{2,1,0:T(8,128)(2,1)S(1)}, bf16[8,16,512]{2,1,0:T(8,128)(2,1)S(1)}, u32[]{:S(2)}, u32[]{:S(2)}) collective-permute-start(bf16[8,16,512]{2,1,0:T(8,128)(2,1)S(1)} %get-tuple-element.36), channel_id=1, source_target_pairs={{0,10},{2,8},{4,14},{6,12},{8,2},{10,0},{12,6},{14,4},{1,11},{3,9}... | collective-permute-start | bytes 393224 | tf_op jit(solution)/shard_map/ppermute | solution.py:402
  20.1 0.0 collective-permute-done.5.rest_0_.rest_6_
  20.1 2.6 %collective-permute-start.6 = (bf16[8,16,512]{2,1,0:T(8,128)(2,1)S(1)}, bf16[8,16,512]{2,1,0:T(8,128)(2,1)S(1)}, u32[]{:S(2)}, u32[]{:S(2)}) collective-permute-start(bf16[8,16,512]{2,1,0:T(8,128)(2,1)S(1)} %get-tuple-element.38), channel_id=1, source_target_pairs={{0,14},{2,12},{4,10},{6,8},{8,6},{10,4},{12,2},{14,0},{1,15},{3,13... | collective-permute-start | bytes 393224 | tf_op jit(solution)/shard_map/ppermute | solution.py:402
  22.7 2.2 %shard_map.47 = (f32[3,512]{1,0:T(4,128)S(1)}, bf16[512,1536]{1,0:T(8,128)(2,1)S(1)}, bf16[512,512]{1,0:T(8,128)(2,1)S(1)}, bf16[512,1536]{1,0:T(8,128)(2,1)S(1)}, bf16[512,512]{1,0:T(8,128)(2,1)S(1)}) custom-call(f32[3,512]{1,0:T(4,128)} %gain_hbm.3, bf16[3,512,1536]{2,1,0:T(8,128)(2,1)} %win_hbm.3, bf16[3,512,512]{2,1,0:T(8,128)(2,1)} %wout_hbm.3), custom_call_target="tpu_custom_call" | custom-call | tf_op jit(solution)/shard_map/pallas_call | solution.py:405
  24.9 0.4 shard_map.50.rest_10_
  25.3 0.0 collective-permute-done.2.rest_1_.rest_3_
  25.4 0.6 shard_map.49.rest_9_
  26.0 0.0 collective-permute-done.rest_1_.rest_5_
  26.0 5.1 %collective-permute-done.3.rest_2_.rest_4_.rest_0_ = bf16[8,16,512]{2,1,0:T(8,128)(2,1)S(1)} collective-permute-done((bf16[8,16,512]{2,1,0:T(8,128)(2,1)S(1)}, bf16[8,16,512]{2,1,0:T(8,128)(2,1)S(1)}, u32[]{:S(2)}, u32[]{:S(2)}) %collective-permute-start.3) | collective-permute-done | bytes 131104 | tf_op jit(solution)/shard_map/ppermute | solution.py:402
  31.1 3.8 %collective-permute-done.4.rest_3_.rest_5_.rest_1_ = bf16[8,16,512]{2,1,0:T(8,128)(2,1)S(1)} collective-permute-done((bf16[8,16,512]{2,1,0:T(8,128)(2,1)S(1)}, bf16[8,16,512]{2,1,0:T(8,128)(2,1)S(1)}, u32[]{:S(2)}, u32[]{:S(2)}) %collective-permute-start.4) | collective-permute-done | bytes 131104 | tf_op jit(solution)/shard_map/ppermute | solution.py:402
  34.8 1.0 %shard_map.48.rest_8_ = bf16[512,1536]{1,0:T(8,128)(2,1)S(1)} custom-call(bf16[8,16,512]{2,1,0:T(8,128)(2,1)S(1)} %get-tuple-element.31.rest_0_.rest_4_, bf16[8,16,512]{2,1,0:T(8,128)(2,1)S(1)} %collective-permute-done.rest_1_.rest_5_, bf16[8,16,512]{2,1,0:T(8,128)(2,1)S(1)} %collective-permute-done.3.rest_2_.rest_4_.rest_0_, ...), custom_call_target="tpu_custom_call" | custom-call | tf_op jit(solution)/shard_map/pallas_call | solution.py:416
  35.9 0.0 collective-permute-done.6.rest_7_
  35.9 2.1 %shard_map.51 = (bf16[1024,512]{1,0:T(8,128)(2,1)S(1)}, bf16[1,8,16,512]{3,2,1,0:T(8,128)(2,1)S(1)}, bf16[1,8,16,512]{3,2,1,0:T(8,128)(2,1)S(1)}) custom-call(bf16[8,16,512]{2,1,0:T(8,128)(2,1)S(1)} %get-tuple-element.31.rest_0_.rest_4_, bf16[8,16,512]{2,1,0:T(8,128)(2,1)S(1)} %collective-permute-done.rest_1_.rest_5_, ...), custom_call_target="tpu_custom_call" | custom-call | tf_op jit(solution)/shard_map/pallas_call | solution.py:428
  38.0 1.1 %shard_map.52 = (bf16[3,8,16,512]{3,2,1,0:T(8,128)(2,1)S(1)}, bf16[3,8,16,512]{3,2,1,0:T(8,128)(2,1)S(1)}) custom-call(bf16[1024,512]{1,0:T(8,128)(2,1)S(1)} %get-tuple-element.42.mixed, bf16[512,512]{1,0:T(8,128)(2,1)S(1)} %get-tuple-element.41.rest_13_.wout, bf16[8,16,512]{2,1,0:T(8,128)(2,1)S(1)} %collective-permute-done.3.rest_2_.rest_4_.rest_0_, ...), custom_call_target="tpu_custom_call" | custom-call | tf_op jit(solution)/shard_map/pallas_call | solution.py:473
  39.1 0.1 collective-permute-start.7
  39.2 0.5 collective-permute-start.10
  39.7 0.4 shard_map.55.kept_packed
  40.2 0.9 %shard_map.53.kept_packed = bf16[384,1536]{1,0:T(8,128)(2,1)S(1)} custom-call(bf16[3,8,16,512]{3,2,1,0:T(8,128)(2,1)S(1)} %get-tuple-element.43.keep_ref, f32[3,512]{1,0:T(4,128)S(1)} %get-tuple-element.39.rest_4_.rest_2_.rest_1_.rest_11_.gain_ref, bf16[512,1536]{1,0:T(8,128)(2,1)S(1)} %get-tuple-element.45.win), custom_call_target="tpu_custom_call" | custom-call | tf_op jit(solution)/shard_map/pallas_call | solution.py:442
  41.0 0.1 collective-permute-done.10.got_ref
  41.1 1.1 %shard_map.56 = (bf16[8,16,512]{2,1,0:T(8,128)(2,1)S(1)}, bf16[8,16,512]{2,1,0:T(8,128)(2,1)S(1)}) custom-call(bf16[1,8,16,512]{3,2,1,0:T(8,128)(2,1)S(1)} %get-tuple-element.49.keep_ref, bf16[1,8,16,512]{3,2,1,0:T(8,128)(2,1)S(1)} %collective-permute-done.10.got_ref, bf16[128,1536]{1,0:T(8,128)(2,1)S(1)} %shard_map.55.kept_packed, ...), custom_call_target="tpu_custom_call" | custom-call | tf_op jit(solution)/shard_map/pallas_call | solution.py:451
  42.2 3.1 %collective-permute-start.11 = (bf16[8,16,512]{2,1,0:T(8,128)(2,1)S(1)}, bf16[8,16,512]{2,1,0:T(8,128)(2,1)S(1)}, u32[]{:S(2)}, u32[]{:S(2)}) collective-permute-start(bf16[8,16,512]{2,1,0:T(8,128)(2,1)S(1)} %get-tuple-element.51), channel_id=1, source_target_pairs={{0,12},{1,15},{2,14},{3,13},{4,8},{5,11},{6,10},{7,9},{8,4},{9,7},... | collective-permute-start | bytes 393224 | tf_op jit(solution)/shard_map/ppermute | solution.py:467
  45.3 0.2 collective-permute-start.12
  45.5 0.0 collective-permute-done.7.got_ref
  45.5 1.1 %shard_map.57 = (bf16[8,16,512]{2,1,0:T(8,128)(2,1)S(1)}, bf16[8,16,512]{2,1,0:T(8,128)(2,1)S(1)}) custom-call(bf16[3,8,16,512]{3,2,1,0:T(8,128)(2,1)S(1)} %get-tuple-element.43.keep_ref, bf16[3,8,16,512]{3,2,1,0:T(8,128)(2,1)S(1)} %collective-permute-done.7.got_ref, bf16[384,1536]{1,0:T(8,128)(2,1)S(1)} %shard_map.53.kept_packed, ...), custom_call_target="tpu_custom_call" | custom-call | tf_op jit(solution)/shard_map/pallas_call | solution.py:451
  46.6 0.7 collective-permute-start.15
  47.3 3.2 %collective-permute-start.16 = (bf16[8,16,512]{2,1,0:T(8,128)(2,1)S(1)}, bf16[8,16,512]{2,1,0:T(8,128)(2,1)S(1)}, u32[]{:S(2)}, u32[]{:S(2)}) collective-permute-start(bf16[8,16,512]{2,1,0:T(8,128)(2,1)S(1)} %get-tuple-element.56), channel_id=1, source_target_pairs={{0,1},{1,2},{2,3},{3,0},{4,5},{5,6},{6,7},{7,4},{8,9},{9,10},{10,1... | collective-permute-start | bytes 393224 | tf_op jit(solution)/shard_map/ppermute | solution.py:467
  50.5 1.7 %shard_map.54 = (bf16[8,16,512]{2,1,0:T(8,128)(2,1)S(1)}, bf16[8,16,512]{2,1,0:T(8,128)(2,1)S(1)}, bf16[8,16,512]{2,1,0:T(8,128)(2,1)S(1)}, bf16[8,16,512]{2,1,0:T(8,128)(2,1)S(1)}) custom-call(bf16[3,8,16,512]{3,2,1,0:T(8,128)(2,1)S(1)} %get-tuple-element.43.keep_ref, bf16[3,8,16,512]{3,2,1,0:T(8,128)(2,1)S(1)} %collective-permute-done.7.got_ref, ...), custom_call_target="tpu_custom_call" | custom-call | tf_op jit(solution)/shard_map/pallas_call | solution.py:451
  52.2 1.0 %collective-permute-start.8 = (bf16[8,16,512]{2,1,0:T(8,128)(2,1)S(1)}, bf16[8,16,512]{2,1,0:T(8,128)(2,1)S(1)}, u32[]{:S(2)}, u32[]{:S(2)}) collective-permute-start(bf16[8,16,512]{2,1,0:T(8,128)(2,1)S(1)} %get-tuple-element.47), channel_id=1, source_target_pairs={{0,8},{1,11},{2,10},{3,9},{4,12},{5,15},{6,14},{7,13},{8,0},{9,3},... | collective-permute-start | bytes 393224 | tf_op jit(solution)/shard_map/ppermute | solution.py:467
  53.2 0.0 collective-permute-done.11.rest_0_
  53.2 2.6 %collective-permute-start.13 = (bf16[8,16,512]{2,1,0:T(8,128)(2,1)S(1)}, bf16[8,16,512]{2,1,0:T(8,128)(2,1)S(1)}, u32[]{:S(2)}, u32[]{:S(2)}) collective-permute-start(bf16[8,16,512]{2,1,0:T(8,128)(2,1)S(1)} %get-tuple-element.53), channel_id=1, source_target_pairs={{0,4},{1,7},{2,6},{3,5},{4,0},{5,3},{6,2},{7,1},{8,12},{9,15},{10,... | collective-permute-start | bytes 393224 | tf_op jit(solution)/shard_map/ppermute | solution.py:467
  55.9 0.0 collective-permute-done.12.rest_1_
  55.9 5.3 %collective-permute-start.14 = (bf16[8,16,512]{2,1,0:T(8,128)(2,1)S(1)}, bf16[8,16,512]{2,1,0:T(8,128)(2,1)S(1)}, u32[]{:S(2)}, u32[]{:S(2)}) collective-permute-start(bf16[8,16,512]{2,1,0:T(8,128)(2,1)S(1)} %get-tuple-element.54), channel_id=1, source_target_pairs={{0,5},{1,6},{2,7},{3,4},{4,1},{5,2},{6,3},{7,0},{8,13},{9,14},{10,... | collective-permute-start | bytes 393224 | tf_op jit(solution)/shard_map/ppermute | solution.py:467
  61.2 0.0 collective-permute-done.15.rest_4_
  61.2 1.2 %collective-permute-start.9 = (bf16[8,16,512]{2,1,0:T(8,128)(2,1)S(1)}, bf16[8,16,512]{2,1,0:T(8,128)(2,1)S(1)}, u32[]{:S(2)}, u32[]{:S(2)}) collective-permute-start(bf16[8,16,512]{2,1,0:T(8,128)(2,1)S(1)} %get-tuple-element.48), channel_id=1, source_target_pairs={{0,9},{1,10},{2,11},{3,8},{4,13},{5,14},{6,15},{7,12},{8,1},{9,2},... | collective-permute-start | bytes 393224 | tf_op jit(solution)/shard_map/ppermute | solution.py:467
  62.4 0.0 collective-permute-done.16.rest_5_
  62.4 0.0 collective-permute-done.13.rest_2_
  62.4 5.6 %collective-permute-done.14.rest_3_ = bf16[8,16,512]{2,1,0:T(8,128)(2,1)S(1)} collective-permute-done((bf16[8,16,512]{2,1,0:T(8,128)(2,1)S(1)}, bf16[8,16,512]{2,1,0:T(8,128)(2,1)S(1)}, u32[]{:S(2)}, u32[]{:S(2)}) %collective-permute-start.14) | collective-permute-done | bytes 131104 | tf_op jit(solution)/shard_map/ppermute | solution.py:467
  68.0 0.9 %join.2.rest_2_ = bf16[64,16,512]{2,1,0:T(8,128)(2,1)} custom-call(bf16[8,16,512]{2,1,0:T(8,128)(2,1)S(1)} %collective-permute-done.11.rest_0_, bf16[8,16,512]{2,1,0:T(8,128)(2,1)S(1)} %collective-permute-done.12.rest_1_, bf16[8,16,512]{2,1,0:T(8,128)(2,1)S(1)} %collective-permute-done.13.rest_2_, bf16[8,16,512]{2,1,0:T(8,128)(2,1)S(1)} %collective-permute-done.14.rest_3_, ...), custom_call_target="tpu_custom_call" | custom-call | tf_op jit(solution)/shard_map/join/pallas_call | solution.py:491
  69.0 0.0 collective-permute-done.8.rest_0_
  69.0 2.0 %collective-permute-done.9.rest_1_ = bf16[8,16,512]{2,1,0:T(8,128)(2,1)S(1)} collective-permute-done((bf16[8,16,512]{2,1,0:T(8,128)(2,1)S(1)}, bf16[8,16,512]{2,1,0:T(8,128)(2,1)S(1)}, u32[]{:S(2)}, u32[]{:S(2)}) %collective-permute-start.9) | collective-permute-done | bytes 131104 | tf_op jit(solution)/shard_map/ppermute | solution.py:467
  71.0 0.7 join.3
Async XLA Ops:
  7.4 9.0 %collective-permute-start.1 = (bf16[8,16,512]{2,1,0:T(8,128)(2,1)S(1)}, bf16[8,16,512]{2,1,0:T(8,128)(2,1)S(1)}, u32[]{:S(2)}, u32[]{:S(2)}) collective-permute-start(bf16[8,16,512]{2,1,0:T(8,128)(2,1)S(1)} %get-tuple-element.33), channel_id=1, source_target_pairs={{0,4},{2,6},{4,0},{6,2},{8,12},{10,14},{12,8},{14,10},{1,5},{3,7},... | collective-permute-start | bytes 393224 | tf_op jit(solution)/shard_map/ppermute | solution.py:402
  10.5 9.6 %collective-permute-start.5 = (bf16[8,16,512]{2,1,0:T(8,128)(2,1)S(1)}, bf16[8,16,512]{2,1,0:T(8,128)(2,1)S(1)}, u32[]{:S(2)}, u32[]{:S(2)}) collective-permute-start(bf16[8,16,512]{2,1,0:T(8,128)(2,1)S(1)} %get-tuple-element.37), channel_id=1, source_target_pairs={{0,12},{2,14},{4,8},{6,10},{8,4},{10,6},{12,0},{14,2},{1,13},{3,15... | collective-permute-start | bytes 393224 | tf_op jit(solution)/shard_map/ppermute | solution.py:402
  13.0 13.0 %collective-permute-start = (bf16[8,16,512]{2,1,0:T(8,128)(2,1)S(1)}, bf16[8,16,512]{2,1,0:T(8,128)(2,1)S(1)}, u32[]{:S(2)}, u32[]{:S(2)}) collective-permute-start(bf16[8,16,512]{2,1,0:T(8,128)(2,1)S(1)} %get-tuple-element.32), channel_id=1, source_target_pairs={{0,2},{2,0},{4,6},{6,4},{8,10},{10,8},{12,14},{14,12},{1,3},{3,1},... | collective-permute-start | bytes 393224 | tf_op jit(solution)/shard_map/ppermute | solution.py:402
  14.5 10.9 %collective-permute-start.2 = (bf16[8,16,512]{2,1,0:T(8,128)(2,1)S(1)}, bf16[8,16,512]{2,1,0:T(8,128)(2,1)S(1)}, u32[]{:S(2)}, u32[]{:S(2)}) collective-permute-start(bf16[8,16,512]{2,1,0:T(8,128)(2,1)S(1)} %get-tuple-element.34), channel_id=1, source_target_pairs={{0,6},{2,4},{4,2},{6,0},{8,14},{10,12},{12,10},{14,8},{1,7},{3,5},... | collective-permute-start | bytes 393224 | tf_op jit(solution)/shard_map/ppermute | solution.py:402
  15.1 16.0 %collective-permute-start.3 = (bf16[8,16,512]{2,1,0:T(8,128)(2,1)S(1)}, bf16[8,16,512]{2,1,0:T(8,128)(2,1)S(1)}, u32[]{:S(2)}, u32[]{:S(2)}) collective-permute-start(bf16[8,16,512]{2,1,0:T(8,128)(2,1)S(1)} %get-tuple-element.35), channel_id=1, source_target_pairs={{0,8},{2,10},{4,12},{6,14},{8,0},{10,2},{12,4},{14,6},{1,9},{3,11}... | collective-permute-start | bytes 393224 | tf_op jit(solution)/shard_map/ppermute | solution.py:402
  16.4 18.5 %collective-permute-start.4 = (bf16[8,16,512]{2,1,0:T(8,128)(2,1)S(1)}, bf16[8,16,512]{2,1,0:T(8,128)(2,1)S(1)}, u32[]{:S(2)}, u32[]{:S(2)}) collective-permute-start(bf16[8,16,512]{2,1,0:T(8,128)(2,1)S(1)} %get-tuple-element.36), channel_id=1, source_target_pairs={{0,10},{2,8},{4,14},{6,12},{8,2},{10,0},{12,6},{14,4},{1,11},{3,9}... | collective-permute-start | bytes 393224 | tf_op jit(solution)/shard_map/ppermute | solution.py:402
  20.1 15.8 %collective-permute-start.6 = (bf16[8,16,512]{2,1,0:T(8,128)(2,1)S(1)}, bf16[8,16,512]{2,1,0:T(8,128)(2,1)S(1)}, u32[]{:S(2)}, u32[]{:S(2)}) collective-permute-start(bf16[8,16,512]{2,1,0:T(8,128)(2,1)S(1)} %get-tuple-element.38), channel_id=1, source_target_pairs={{0,14},{2,12},{4,10},{6,8},{8,6},{10,4},{12,2},{14,0},{1,15},{3,13... | collective-permute-start | bytes 393224 | tf_op jit(solution)/shard_map/ppermute | solution.py:402
  39.1 6.4 %collective-permute-start.7 = (bf16[3,8,16,512]{3,2,1,0:T(8,128)(2,1)S(1)}, bf16[3,8,16,512]{3,2,1,0:T(8,128)(2,1)S(1)}, u32[]{:S(2)}, u32[]{:S(2)}) collective-permute-start(bf16[3,8,16,512]{3,2,1,0:T(8,128)(2,1)S(1)} %get-tuple-element.44), channel_id=1, source_target_pairs={{0,1},{1,0},{2,3},{3,2},{4,5},{5,4},{6,7},{7,6},{8,9},{9,8},{10,11... | collective-permute-start | bytes 1179656 | tf_op jit(solution)/shard_map/ppermute | solution.py:438
  39.2 1.9 %collective-permute-start.10 = (bf16[1,8,16,512]{3,2,1,0:T(8,128)(2,1)S(1)}, bf16[1,8,16,512]{3,2,1,0:T(8,128)(2,1)S(1)}, u32[]{:S(2)}, u32[]{:S(2)}) collective-permute-start(bf16[1,8,16,512]{3,2,1,0:T(8,128)(2,1)S(1)} %get-tuple-element.50), channel_id=1, source_target_pairs={{0,1},{1,0},{2,3},{3,2},{4,5},{5,4},{6,7},{7,6},{8,9},{9,8},{10,11... | collective-permute-start | bytes 393224 | tf_op jit(solution)/shard_map/ppermute | solution.py:438
  42.2 11.0 %collective-permute-start.11 = (bf16[8,16,512]{2,1,0:T(8,128)(2,1)S(1)}, bf16[8,16,512]{2,1,0:T(8,128)(2,1)S(1)}, u32[]{:S(2)}, u32[]{:S(2)}) collective-permute-start(bf16[8,16,512]{2,1,0:T(8,128)(2,1)S(1)} %get-tuple-element.51), channel_id=1, source_target_pairs={{0,12},{1,15},{2,14},{3,13},{4,8},{5,11},{6,10},{7,9},{8,4},{9,7},... | collective-permute-start | bytes 393224 | tf_op jit(solution)/shard_map/ppermute | solution.py:467
  45.3 10.6 %collective-permute-start.12 = (bf16[8,16,512]{2,1,0:T(8,128)(2,1)S(1)}, bf16[8,16,512]{2,1,0:T(8,128)(2,1)S(1)}, u32[]{:S(2)}, u32[]{:S(2)}) collective-permute-start(bf16[8,16,512]{2,1,0:T(8,128)(2,1)S(1)} %get-tuple-element.52), channel_id=1, source_target_pairs={{0,13},{1,14},{2,15},{3,12},{4,9},{5,10},{6,11},{7,8},{8,5},{9,6},... | collective-permute-start | bytes 393224 | tf_op jit(solution)/shard_map/ppermute | solution.py:467
  46.6 14.6 %collective-permute-start.15 = (bf16[8,16,512]{2,1,0:T(8,128)(2,1)S(1)}, bf16[8,16,512]{2,1,0:T(8,128)(2,1)S(1)}, u32[]{:S(2)}, u32[]{:S(2)}) collective-permute-start(bf16[8,16,512]{2,1,0:T(8,128)(2,1)S(1)} %get-tuple-element.55), channel_id=1, source_target_pairs={{0,0},{1,3},{2,2},{3,1},{4,4},{5,7},{6,6},{7,5},{8,8},{9,11},{10,1... | collective-permute-start | bytes 393224 | tf_op jit(solution)/shard_map/ppermute | solution.py:467
  47.3 15.1 %collective-permute-start.16 = (bf16[8,16,512]{2,1,0:T(8,128)(2,1)S(1)}, bf16[8,16,512]{2,1,0:T(8,128)(2,1)S(1)}, u32[]{:S(2)}, u32[]{:S(2)}) collective-permute-start(bf16[8,16,512]{2,1,0:T(8,128)(2,1)S(1)} %get-tuple-element.56), channel_id=1, source_target_pairs={{0,1},{1,2},{2,3},{3,0},{4,5},{5,6},{6,7},{7,4},{8,9},{9,10},{10,1... | collective-permute-start | bytes 393224 | tf_op jit(solution)/shard_map/ppermute | solution.py:467
  52.2 16.8 %collective-permute-start.8 = (bf16[8,16,512]{2,1,0:T(8,128)(2,1)S(1)}, bf16[8,16,512]{2,1,0:T(8,128)(2,1)S(1)}, u32[]{:S(2)}, u32[]{:S(2)}) collective-permute-start(bf16[8,16,512]{2,1,0:T(8,128)(2,1)S(1)} %get-tuple-element.47), channel_id=1, source_target_pairs={{0,8},{1,11},{2,10},{3,9},{4,12},{5,15},{6,14},{7,13},{8,0},{9,3},... | collective-permute-start | bytes 393224 | tf_op jit(solution)/shard_map/ppermute | solution.py:467
  53.2 9.2 %collective-permute-start.13 = (bf16[8,16,512]{2,1,0:T(8,128)(2,1)S(1)}, bf16[8,16,512]{2,1,0:T(8,128)(2,1)S(1)}, u32[]{:S(2)}, u32[]{:S(2)}) collective-permute-start(bf16[8,16,512]{2,1,0:T(8,128)(2,1)S(1)} %get-tuple-element.53), channel_id=1, source_target_pairs={{0,4},{1,7},{2,6},{3,5},{4,0},{5,3},{6,2},{7,1},{8,12},{9,15},{10,... | collective-permute-start | bytes 393224 | tf_op jit(solution)/shard_map/ppermute | solution.py:467
  55.9 12.2 %collective-permute-start.14 = (bf16[8,16,512]{2,1,0:T(8,128)(2,1)S(1)}, bf16[8,16,512]{2,1,0:T(8,128)(2,1)S(1)}, u32[]{:S(2)}, u32[]{:S(2)}) collective-permute-start(bf16[8,16,512]{2,1,0:T(8,128)(2,1)S(1)} %get-tuple-element.54), channel_id=1, source_target_pairs={{0,5},{1,6},{2,7},{3,4},{4,1},{5,2},{6,3},{7,0},{8,13},{9,14},{10,... | collective-permute-start | bytes 393224 | tf_op jit(solution)/shard_map/ppermute | solution.py:467
  61.2 9.8 %collective-permute-start.9 = (bf16[8,16,512]{2,1,0:T(8,128)(2,1)S(1)}, bf16[8,16,512]{2,1,0:T(8,128)(2,1)S(1)}, u32[]{:S(2)}, u32[]{:S(2)}) collective-permute-start(bf16[8,16,512]{2,1,0:T(8,128)(2,1)S(1)} %get-tuple-element.48), channel_id=1, source_target_pairs={{0,9},{1,10},{2,11},{3,8},{4,13},{5,14},{6,15},{7,12},{8,1},{9,2},... | collective-permute-start | bytes 393224 | tf_op jit(solution)/shard_map/ppermute | solution.py:467

commit v4 on v3

--- a/solution.py
+++ b/solution.py
@@ -73,6 +73,7 @@
 def tile_attention(packed, same_line, halves):
     tokens, width = packed.shape[0], packed.shape[1] // 3
     left, right = halves
+    scale = math.log2(math.e) / math.sqrt(HEAD_DIM)
     pieces = []
     for at in range(0, width, LANES):
         q = packed[:, at : at + LANES]
@@ -88,7 +89,7 @@
         for head in range(2):
             own = jnp.where(same_line, scores[:, head * tokens : (head + 1) * tokens], HIDDEN)
             top = jnp.max(own, axis=-1, keepdims=True)
-            weights.append(jnp.exp2(own - top).astype(jnp.bfloat16))
+            weights.append(jnp.exp2((own - top) * scale).astype(jnp.bfloat16))
         values = jnp.concatenate(
             [
                 jnp.concatenate([v * left, left], axis=1),
@@ -110,11 +111,9 @@
 
 
 def project(normed, weight_ref, packed_ref, at):
-    rows, width = normed.shape
-    result = jnp.dot(normed, weight_ref[...], preferred_element_type=jnp.float32)
-    scale = math.log2(math.e) / math.sqrt(HEAD_DIM)
-    packed_ref[at : at + rows, :width] = (result[:, :width] * scale).astype(jnp.bfloat16)
-    packed_ref[at : at + rows, width:] = result[:, width:].astype(jnp.bfloat16)
+    packed_ref[at : at + normed.shape[0]] = jnp.dot(
+        normed, weight_ref[...], preferred_element_type=jnp.float32
+    ).astype(jnp.bfloat16)
 
 
 def lanes_of(value):

time: 72.1 us -> 72.1 us (level)
  transfers between devices with their start and end apart: 17 -> 17, of which waited for: 5 -> 5; matrix products, arithmetic and copies ran while one was open for 0% -> 0% of each run, Pallas kernels for 15% -> 14%
where the time goes in v4:
time: 72.1 us; the launch traced here: 71.9 us
  starting transfers between devices  33.1 us (46%)
  Pallas kernels  21.7 us (30%)
  waiting for transfers between devices  16.7 us (23%)
    ppermute x8, starting transfers between devices, finish(): arrived.append(lax.ppermute(results[2 * index + flip], ('aa', 'ba'), route))  17.3 us
    ppermute x7, starting transfers between devices, fast_body(): came[k] = lax.ppermute(sent[k], 'aa', [(i, i ^ k) for i in range(n)])  15.2 us
    ppermute x7, waiting for transfers between devices, fast_body(): came[k] = lax.ppermute(sent[k], 'aa', [(i, i ^ k) for i in range(n)])  8.92 us
    ppermute x8, waiting for transfers between devices, finish(): arrived.append(lax.ppermute(results[2 * index + flip], ('aa', 'ba'), route))  7.68 us
    pallas_call x1, Pallas kernels, fast_body(): call(functools.partial(first_kernel, 0), [message] * n, [HBM] * 4, [pltpu...  7.39 us
    pallas_call x3, Pallas kernels, finish(): call(functools.partial(last_kernel, 2, rows), [message] * (2 * len(rows))...  3.92 us
    pallas_call x1, Pallas kernels, fast_body(): call(functools.partial(weights_kernel, later), [array(gain_shape, f32)] +...  2.2 us
    pallas_call x3, Pallas kernels, fast_body(): call(functools.partial(group_kernel, 1, len(group)), [array((len(group) *...  2.1 us
  transfers between devices with their start and end apart: 17, of which 5 were waited for; matrix products, arithmetic and copies ran while one was open for 0% of the time, Pallas kernels for 14%

profile of v4, /device:TPU:0, one launch (start us, length us, event | category | flops | bytes accessed | tf_op | source)
XLA Modules:
  0.0 71.9 jit_solution(5557993819544944523)
XLA Ops:
  0.0 7.4 %shard_map.46 = (bf16[8,16,512]{2,1,0:T(8,128)(2,1)S(1)}, bf16[8,16,512]{2,1,0:T(8,128)(2,1)S(1)}, bf16[8,16,512]{2,1,0:T(8,128)(2,1)S(1)}, bf16[8,16,512]{2,1,0...) custom-call(bf16[64,16,512]{2,1,0:T(8,128)(2,1)} %bitcast.4, ...), custom_call_target="tpu_custom_call" | custom-call | tf_op jit(solution)/shard_map/pallas_call | solution.py:381
  7.4 3.1 %collective-permute-start.1 = (bf16[8,16,512]{2,1,0:T(8,128)(2,1)S(1)}, bf16[8,16,512]{2,1,0:T(8,128)(2,1)S(1)}, u32[]{:S(2)}, u32[]{:S(2)}) collective-permute-start(bf16[8,16,512]{2,1,0:T(8,128)(2,1)S(1)} %get-tuple-element.33), channel_id=1, source_target_pairs={{0,4},{2,6},{4,0},{6,2},{8,12},{10,14},{12,8},{14,10},{1,5},{3,7},... | collective-permute-start | bytes 393224 | tf_op jit(solution)/shard_map/ppermute | solution.py:401
  10.5 2.5 %collective-permute-start.5 = (bf16[8,16,512]{2,1,0:T(8,128)(2,1)S(1)}, bf16[8,16,512]{2,1,0:T(8,128)(2,1)S(1)}, u32[]{:S(2)}, u32[]{:S(2)}) collective-permute-start(bf16[8,16,512]{2,1,0:T(8,128)(2,1)S(1)} %get-tuple-element.37), channel_id=1, source_target_pairs={{0,12},{2,14},{4,8},{6,10},{8,4},{10,6},{12,0},{14,2},{1,13},{3,15... | collective-permute-start | bytes 393224 | tf_op jit(solution)/shard_map/ppermute | solution.py:401
  13.0 1.5 %collective-permute-start = (bf16[8,16,512]{2,1,0:T(8,128)(2,1)S(1)}, bf16[8,16,512]{2,1,0:T(8,128)(2,1)S(1)}, u32[]{:S(2)}, u32[]{:S(2)}) collective-permute-start(bf16[8,16,512]{2,1,0:T(8,128)(2,1)S(1)} %get-tuple-element.32), channel_id=1, source_target_pairs={{0,2},{2,0},{4,6},{6,4},{8,10},{10,8},{12,14},{14,12},{1,3},{3,1},... | collective-permute-start | bytes 393224 | tf_op jit(solution)/shard_map/ppermute | solution.py:401
  14.5 0.6 collective-permute-start.2
  15.1 1.2 %collective-permute-start.3 = (bf16[8,16,512]{2,1,0:T(8,128)(2,1)S(1)}, bf16[8,16,512]{2,1,0:T(8,128)(2,1)S(1)}, u32[]{:S(2)}, u32[]{:S(2)}) collective-permute-start(bf16[8,16,512]{2,1,0:T(8,128)(2,1)S(1)} %get-tuple-element.35), channel_id=1, source_target_pairs={{0,8},{2,10},{4,12},{6,14},{8,0},{10,2},{12,4},{14,6},{1,9},{3,11}... | collective-permute-start | bytes 393224 | tf_op jit(solution)/shard_map/ppermute | solution.py:401
  16.4 0.0 collective-permute-done.1.rest_0_.rest_2_
  16.4 3.7 %collective-permute-start.4 = (bf16[8,16,512]{2,1,0:T(8,128)(2,1)S(1)}, bf16[8,16,512]{2,1,0:T(8,128)(2,1)S(1)}, u32[]{:S(2)}, u32[]{:S(2)}) collective-permute-start(bf16[8,16,512]{2,1,0:T(8,128)(2,1)S(1)} %get-tuple-element.36), channel_id=1, source_target_pairs={{0,10},{2,8},{4,14},{6,12},{8,2},{10,0},{12,6},{14,4},{1,11},{3,9}... | collective-permute-start | bytes 393224 | tf_op jit(solution)/shard_map/ppermute | solution.py:401
  20.1 0.0 collective-permute-done.5.rest_0_.rest_6_
  20.1 2.6 %collective-permute-start.6 = (bf16[8,16,512]{2,1,0:T(8,128)(2,1)S(1)}, bf16[8,16,512]{2,1,0:T(8,128)(2,1)S(1)}, u32[]{:S(2)}, u32[]{:S(2)}) collective-permute-start(bf16[8,16,512]{2,1,0:T(8,128)(2,1)S(1)} %get-tuple-element.38), channel_id=1, source_target_pairs={{0,14},{2,12},{4,10},{6,8},{8,6},{10,4},{12,2},{14,0},{1,15},{3,13... | collective-permute-start | bytes 393224 | tf_op jit(solution)/shard_map/ppermute | solution.py:401
  22.7 2.2 %shard_map.47 = (f32[3,512]{1,0:T(4,128)S(1)}, bf16[512,1536]{1,0:T(8,128)(2,1)S(1)}, bf16[512,512]{1,0:T(8,128)(2,1)S(1)}, bf16[512,1536]{1,0:T(8,128)(2,1)S(1)}, bf16[512,512]{1,0:T(8,128)(2,1)S(1)}) custom-call(f32[3,512]{1,0:T(4,128)} %gain_hbm.3, bf16[3,512,1536]{2,1,0:T(8,128)(2,1)} %win_hbm.3, bf16[3,512,512]{2,1,0:T(8,128)(2,1)} %wout_hbm.3), custom_call_target="tpu_custom_call" | custom-call | tf_op jit(solution)/shard_map/pallas_call | solution.py:404
  24.9 0.4 shard_map.50.rest_10_
  25.3 0.0 collective-permute-done.2.rest_1_.rest_3_
  25.4 0.6 shard_map.49.rest_9_
  26.0 0.0 collective-permute-done.rest_1_.rest_5_
  26.0 5.1 %collective-permute-done.3.rest_2_.rest_4_.rest_0_ = bf16[8,16,512]{2,1,0:T(8,128)(2,1)S(1)} collective-permute-done((bf16[8,16,512]{2,1,0:T(8,128)(2,1)S(1)}, bf16[8,16,512]{2,1,0:T(8,128)(2,1)S(1)}, u32[]{:S(2)}, u32[]{:S(2)}) %collective-permute-start.3) | collective-permute-done | bytes 131104 | tf_op jit(solution)/shard_map/ppermute | solution.py:401
  31.1 3.8 %collective-permute-done.4.rest_3_.rest_5_.rest_1_ = bf16[8,16,512]{2,1,0:T(8,128)(2,1)S(1)} collective-permute-done((bf16[8,16,512]{2,1,0:T(8,128)(2,1)S(1)}, bf16[8,16,512]{2,1,0:T(8,128)(2,1)S(1)}, u32[]{:S(2)}, u32[]{:S(2)}) %collective-permute-start.4) | collective-permute-done | bytes 131104 | tf_op jit(solution)/shard_map/ppermute | solution.py:401
  34.9 1.0 %shard_map.48.rest_8_ = bf16[512,1536]{1,0:T(8,128)(2,1)S(1)} custom-call(bf16[8,16,512]{2,1,0:T(8,128)(2,1)S(1)} %get-tuple-element.31.rest_0_.rest_4_, bf16[8,16,512]{2,1,0:T(8,128)(2,1)S(1)} %collective-permute-done.rest_1_.rest_5_, bf16[8,16,512]{2,1,0:T(8,128)(2,1)S(1)} %collective-permute-done.3.rest_2_.rest_4_.rest_0_, ...), custom_call_target="tpu_custom_call" | custom-call | tf_op jit(solution)/shard_map/pallas_call | solution.py:415
  35.9 0.0 collective-permute-done.6.rest_7_
  35.9 2.1 %shard_map.51 = (bf16[1024,512]{1,0:T(8,128)(2,1)S(1)}, bf16[1,8,16,512]{3,2,1,0:T(8,128)(2,1)S(1)}, bf16[1,8,16,512]{3,2,1,0:T(8,128)(2,1)S(1)}) custom-call(bf16[8,16,512]{2,1,0:T(8,128)(2,1)S(1)} %get-tuple-element.31.rest_0_.rest_4_, bf16[8,16,512]{2,1,0:T(8,128)(2,1)S(1)} %collective-permute-done.rest_1_.rest_5_, ...), custom_call_target="tpu_custom_call" | custom-call | tf_op jit(solution)/shard_map/pallas_call | solution.py:427
  38.0 1.1 %shard_map.52 = (bf16[3,8,16,512]{3,2,1,0:T(8,128)(2,1)S(1)}, bf16[3,8,16,512]{3,2,1,0:T(8,128)(2,1)S(1)}) custom-call(bf16[1024,512]{1,0:T(8,128)(2,1)S(1)} %get-tuple-element.42.mixed, bf16[512,512]{1,0:T(8,128)(2,1)S(1)} %get-tuple-element.41.rest_13_.wout, bf16[8,16,512]{2,1,0:T(8,128)(2,1)S(1)} %collective-permute-done.3.rest_2_.rest_4_.rest_0_, ...), custom_call_target="tpu_custom_call" | custom-call | tf_op jit(solution)/shard_map/pallas_call | solution.py:472
  39.2 0.1 collective-permute-start.7
  39.2 0.5 collective-permute-start.10
  39.7 0.4 shard_map.55.kept_packed
  40.2 0.8 %shard_map.53.kept_packed = bf16[384,1536]{1,0:T(8,128)(2,1)S(1)} custom-call(bf16[3,8,16,512]{3,2,1,0:T(8,128)(2,1)S(1)} %get-tuple-element.43.keep_ref, f32[3,512]{1,0:T(4,128)S(1)} %get-tuple-element.39.rest_4_.rest_2_.rest_1_.rest_11_.gain_ref, bf16[512,1536]{1,0:T(8,128)(2,1)S(1)} %get-tuple-element.45.win), custom_call_target="tpu_custom_call" | custom-call | tf_op jit(solution)/shard_map/pallas_call | solution.py:441
  41.0 0.1 collective-permute-done.10.got_ref
  41.1 1.1 %shard_map.56 = (bf16[8,16,512]{2,1,0:T(8,128)(2,1)S(1)}, bf16[8,16,512]{2,1,0:T(8,128)(2,1)S(1)}) custom-call(bf16[1,8,16,512]{3,2,1,0:T(8,128)(2,1)S(1)} %get-tuple-element.49.keep_ref, bf16[1,8,16,512]{3,2,1,0:T(8,128)(2,1)S(1)} %collective-permute-done.10.got_ref, bf16[128,1536]{1,0:T(8,128)(2,1)S(1)} %shard_map.55.kept_packed, ...), custom_call_target="tpu_custom_call" | custom-call | tf_op jit(solution)/shard_map/pallas_call | solution.py:450
  42.2 3.1 %collective-permute-start.11 = (bf16[8,16,512]{2,1,0:T(8,128)(2,1)S(1)}, bf16[8,16,512]{2,1,0:T(8,128)(2,1)S(1)}, u32[]{:S(2)}, u32[]{:S(2)}) collective-permute-start(bf16[8,16,512]{2,1,0:T(8,128)(2,1)S(1)} %get-tuple-element.51), channel_id=1, source_target_pairs={{0,12},{1,15},{2,14},{3,13},{4,8},{5,11},{6,10},{7,9},{8,4},{9,7},... | collective-permute-start | bytes 393224 | tf_op jit(solution)/shard_map/ppermute | solution.py:466
  45.3 0.2 collective-permute-start.12
  45.5 0.0 collective-permute-done.7.got_ref
  45.5 1.1 %shard_map.57 = (bf16[8,16,512]{2,1,0:T(8,128)(2,1)S(1)}, bf16[8,16,512]{2,1,0:T(8,128)(2,1)S(1)}) custom-call(bf16[3,8,16,512]{3,2,1,0:T(8,128)(2,1)S(1)} %get-tuple-element.43.keep_ref, bf16[3,8,16,512]{3,2,1,0:T(8,128)(2,1)S(1)} %collective-permute-done.7.got_ref, bf16[384,1536]{1,0:T(8,128)(2,1)S(1)} %shard_map.53.kept_packed, ...), custom_call_target="tpu_custom_call" | custom-call | tf_op jit(solution)/shard_map/pallas_call | solution.py:450
  46.7 0.7 collective-permute-start.15
  47.3 3.2 %collective-permute-start.16 = (bf16[8,16,512]{2,1,0:T(8,128)(2,1)S(1)}, bf16[8,16,512]{2,1,0:T(8,128)(2,1)S(1)}, u32[]{:S(2)}, u32[]{:S(2)}) collective-permute-start(bf16[8,16,512]{2,1,0:T(8,128)(2,1)S(1)} %get-tuple-element.56), channel_id=1, source_target_pairs={{0,1},{1,2},{2,3},{3,0},{4,5},{5,6},{6,7},{7,4},{8,9},{9,10},{10,1... | collective-permute-start | bytes 393224 | tf_op jit(solution)/shard_map/ppermute | solution.py:466
  50.5 1.7 %shard_map.54 = (bf16[8,16,512]{2,1,0:T(8,128)(2,1)S(1)}, bf16[8,16,512]{2,1,0:T(8,128)(2,1)S(1)}, bf16[8,16,512]{2,1,0:T(8,128)(2,1)S(1)}, bf16[8,16,512]{2,1,0:T(8,128)(2,1)S(1)}) custom-call(bf16[3,8,16,512]{3,2,1,0:T(8,128)(2,1)S(1)} %get-tuple-element.43.keep_ref, bf16[3,8,16,512]{3,2,1,0:T(8,128)(2,1)S(1)} %collective-permute-done.7.got_ref, ...), custom_call_target="tpu_custom_call" | custom-call | tf_op jit(solution)/shard_map/pallas_call | solution.py:450
  52.2 1.0 %collective-permute-start.8 = (bf16[8,16,512]{2,1,0:T(8,128)(2,1)S(1)}, bf16[8,16,512]{2,1,0:T(8,128)(2,1)S(1)}, u32[]{:S(2)}, u32[]{:S(2)}) collective-permute-start(bf16[8,16,512]{2,1,0:T(8,128)(2,1)S(1)} %get-tuple-element.47), channel_id=1, source_target_pairs={{0,8},{1,11},{2,10},{3,9},{4,12},{5,15},{6,14},{7,13},{8,0},{9,3},... | collective-permute-start | bytes 393224 | tf_op jit(solution)/shard_map/ppermute | solution.py:466
  53.3 0.0 collective-permute-done.11.rest_0_
  53.3 2.6 %collective-permute-start.13 = (bf16[8,16,512]{2,1,0:T(8,128)(2,1)S(1)}, bf16[8,16,512]{2,1,0:T(8,128)(2,1)S(1)}, u32[]{:S(2)}, u32[]{:S(2)}) collective-permute-start(bf16[8,16,512]{2,1,0:T(8,128)(2,1)S(1)} %get-tuple-element.53), channel_id=1, source_target_pairs={{0,4},{1,7},{2,6},{3,5},{4,0},{5,3},{6,2},{7,1},{8,12},{9,15},{10,... | collective-permute-start | bytes 393224 | tf_op jit(solution)/shard_map/ppermute | solution.py:466
  55.9 0.0 collective-permute-done.12.rest_1_
  55.9 5.3 %collective-permute-start.14 = (bf16[8,16,512]{2,1,0:T(8,128)(2,1)S(1)}, bf16[8,16,512]{2,1,0:T(8,128)(2,1)S(1)}, u32[]{:S(2)}, u32[]{:S(2)}) collective-permute-start(bf16[8,16,512]{2,1,0:T(8,128)(2,1)S(1)} %get-tuple-element.54), channel_id=1, source_target_pairs={{0,5},{1,6},{2,7},{3,4},{4,1},{5,2},{6,3},{7,0},{8,13},{9,14},{10,... | collective-permute-start | bytes 393224 | tf_op jit(solution)/shard_map/ppermute | solution.py:466
  61.2 0.0 collective-permute-done.15.rest_4_
  61.2 1.2 %collective-permute-start.9 = (bf16[8,16,512]{2,1,0:T(8,128)(2,1)S(1)}, bf16[8,16,512]{2,1,0:T(8,128)(2,1)S(1)}, u32[]{:S(2)}, u32[]{:S(2)}) collective-permute-start(bf16[8,16,512]{2,1,0:T(8,128)(2,1)S(1)} %get-tuple-element.48), channel_id=1, source_target_pairs={{0,9},{1,10},{2,11},{3,8},{4,13},{5,14},{6,15},{7,12},{8,1},{9,2},... | collective-permute-start | bytes 393224 | tf_op jit(solution)/shard_map/ppermute | solution.py:466
  62.4 0.0 collective-permute-done.16.rest_5_
  62.4 0.0 collective-permute-done.13.rest_2_
  62.4 5.7 %collective-permute-done.14.rest_3_ = bf16[8,16,512]{2,1,0:T(8,128)(2,1)S(1)} collective-permute-done((bf16[8,16,512]{2,1,0:T(8,128)(2,1)S(1)}, bf16[8,16,512]{2,1,0:T(8,128)(2,1)S(1)}, u32[]{:S(2)}, u32[]{:S(2)}) %collective-permute-start.14) | collective-permute-done | bytes 131104 | tf_op jit(solution)/shard_map/ppermute | solution.py:466
  68.1 0.9 %join.2.rest_2_ = bf16[64,16,512]{2,1,0:T(8,128)(2,1)} custom-call(bf16[8,16,512]{2,1,0:T(8,128)(2,1)S(1)} %collective-permute-done.11.rest_0_, bf16[8,16,512]{2,1,0:T(8,128)(2,1)S(1)} %collective-permute-done.12.rest_1_, bf16[8,16,512]{2,1,0:T(8,128)(2,1)S(1)} %collective-permute-done.13.rest_2_, bf16[8,16,512]{2,1,0:T(8,128)(2,1)S(1)} %collective-permute-done.14.rest_3_, ...), custom_call_target="tpu_custom_call" | custom-call | tf_op jit(solution)/shard_map/join/pallas_call | solution.py:490
  69.0 0.0 collective-permute-done.8.rest_0_
  69.0 2.0 %collective-permute-done.9.rest_1_ = bf16[8,16,512]{2,1,0:T(8,128)(2,1)S(1)} collective-permute-done((bf16[8,16,512]{2,1,0:T(8,128)(2,1)S(1)}, bf16[8,16,512]{2,1,0:T(8,128)(2,1)S(1)}, u32[]{:S(2)}, u32[]{:S(2)}) %collective-permute-start.9) | collective-permute-done | bytes 131104 | tf_op jit(solution)/shard_map/ppermute | solution.py:466
  71.0 0.7 join.3
Async XLA Ops:
  7.4 9.0 %collective-permute-start.1 = (bf16[8,16,512]{2,1,0:T(8,128)(2,1)S(1)}, bf16[8,16,512]{2,1,0:T(8,128)(2,1)S(1)}, u32[]{:S(2)}, u32[]{:S(2)}) collective-permute-start(bf16[8,16,512]{2,1,0:T(8,128)(2,1)S(1)} %get-tuple-element.33), channel_id=1, source_target_pairs={{0,4},{2,6},{4,0},{6,2},{8,12},{10,14},{12,8},{14,10},{1,5},{3,7},... | collective-permute-start | bytes 393224 | tf_op jit(solution)/shard_map/ppermute | solution.py:401
  10.5 9.6 %collective-permute-start.5 = (bf16[8,16,512]{2,1,0:T(8,128)(2,1)S(1)}, bf16[8,16,512]{2,1,0:T(8,128)(2,1)S(1)}, u32[]{:S(2)}, u32[]{:S(2)}) collective-permute-start(bf16[8,16,512]{2,1,0:T(8,128)(2,1)S(1)} %get-tuple-element.37), channel_id=1, source_target_pairs={{0,12},{2,14},{4,8},{6,10},{8,4},{10,6},{12,0},{14,2},{1,13},{3,15... | collective-permute-start | bytes 393224 | tf_op jit(solution)/shard_map/ppermute | solution.py:401
  13.0 13.0 %collective-permute-start = (bf16[8,16,512]{2,1,0:T(8,128)(2,1)S(1)}, bf16[8,16,512]{2,1,0:T(8,128)(2,1)S(1)}, u32[]{:S(2)}, u32[]{:S(2)}) collective-permute-start(bf16[8,16,512]{2,1,0:T(8,128)(2,1)S(1)} %get-tuple-element.32), channel_id=1, source_target_pairs={{0,2},{2,0},{4,6},{6,4},{8,10},{10,8},{12,14},{14,12},{1,3},{3,1},... | collective-permute-start | bytes 393224 | tf_op jit(solution)/shard_map/ppermute | solution.py:401
  14.5 10.8 %collective-permute-start.2 = (bf16[8,16,512]{2,1,0:T(8,128)(2,1)S(1)}, bf16[8,16,512]{2,1,0:T(8,128)(2,1)S(1)}, u32[]{:S(2)}, u32[]{:S(2)}) collective-permute-start(bf16[8,16,512]{2,1,0:T(8,128)(2,1)S(1)} %get-tuple-element.34), channel_id=1, source_target_pairs={{0,6},{2,4},{4,2},{6,0},{8,14},{10,12},{12,10},{14,8},{1,7},{3,5},... | collective-permute-start | bytes 393224 | tf_op jit(solution)/shard_map/ppermute | solution.py:401
  15.1 16.0 %collective-permute-start.3 = (bf16[8,16,512]{2,1,0:T(8,128)(2,1)S(1)}, bf16[8,16,512]{2,1,0:T(8,128)(2,1)S(1)}, u32[]{:S(2)}, u32[]{:S(2)}) collective-permute-start(bf16[8,16,512]{2,1,0:T(8,128)(2,1)S(1)} %get-tuple-element.35), channel_id=1, source_target_pairs={{0,8},{2,10},{4,12},{6,14},{8,0},{10,2},{12,4},{14,6},{1,9},{3,11}... | collective-permute-start | bytes 393224 | tf_op jit(solution)/shard_map/ppermute | solution.py:401
  16.4 18.5 %collective-permute-start.4 = (bf16[8,16,512]{2,1,0:T(8,128)(2,1)S(1)}, bf16[8,16,512]{2,1,0:T(8,128)(2,1)S(1)}, u32[]{:S(2)}, u32[]{:S(2)}) collective-permute-start(bf16[8,16,512]{2,1,0:T(8,128)(2,1)S(1)} %get-tuple-element.36), channel_id=1, source_target_pairs={{0,10},{2,8},{4,14},{6,12},{8,2},{10,0},{12,6},{14,4},{1,11},{3,9}... | collective-permute-start | bytes 393224 | tf_op jit(solution)/shard_map/ppermute | solution.py:401
  20.1 15.8 %collective-permute-start.6 = (bf16[8,16,512]{2,1,0:T(8,128)(2,1)S(1)}, bf16[8,16,512]{2,1,0:T(8,128)(2,1)S(1)}, u32[]{:S(2)}, u32[]{:S(2)}) collective-permute-start(bf16[8,16,512]{2,1,0:T(8,128)(2,1)S(1)} %get-tuple-element.38), channel_id=1, source_target_pairs={{0,14},{2,12},{4,10},{6,8},{8,6},{10,4},{12,2},{14,0},{1,15},{3,13... | collective-permute-start | bytes 393224 | tf_op jit(solution)/shard_map/ppermute | solution.py:401
  39.2 6.4 %collective-permute-start.7 = (bf16[3,8,16,512]{3,2,1,0:T(8,128)(2,1)S(1)}, bf16[3,8,16,512]{3,2,1,0:T(8,128)(2,1)S(1)}, u32[]{:S(2)}, u32[]{:S(2)}) collective-permute-start(bf16[3,8,16,512]{3,2,1,0:T(8,128)(2,1)S(1)} %get-tuple-element.44), channel_id=1, source_target_pairs={{0,1},{1,0},{2,3},{3,2},{4,5},{5,4},{6,7},{7,6},{8,9},{9,8},{10,11... | collective-permute-start | bytes 1179656 | tf_op jit(solution)/shard_map/ppermute | solution.py:437
  39.2 1.9 %collective-permute-start.10 = (bf16[1,8,16,512]{3,2,1,0:T(8,128)(2,1)S(1)}, bf16[1,8,16,512]{3,2,1,0:T(8,128)(2,1)S(1)}, u32[]{:S(2)}, u32[]{:S(2)}) collective-permute-start(bf16[1,8,16,512]{3,2,1,0:T(8,128)(2,1)S(1)} %get-tuple-element.50), channel_id=1, source_target_pairs={{0,1},{1,0},{2,3},{3,2},{4,5},{5,4},{6,7},{7,6},{8,9},{9,8},{10,11... | collective-permute-start | bytes 393224 | tf_op jit(solution)/shard_map/ppermute | solution.py:437
  42.2 11.0 %collective-permute-start.11 = (bf16[8,16,512]{2,1,0:T(8,128)(2,1)S(1)}, bf16[8,16,512]{2,1,0:T(8,128)(2,1)S(1)}, u32[]{:S(2)}, u32[]{:S(2)}) collective-permute-start(bf16[8,16,512]{2,1,0:T(8,128)(2,1)S(1)} %get-tuple-element.51), channel_id=1, source_target_pairs={{0,12},{1,15},{2,14},{3,13},{4,8},{5,11},{6,10},{7,9},{8,4},{9,7},... | collective-permute-start | bytes 393224 | tf_op jit(solution)/shard_map/ppermute | solution.py:466
  45.3 10.6 %collective-permute-start.12 = (bf16[8,16,512]{2,1,0:T(8,128)(2,1)S(1)}, bf16[8,16,512]{2,1,0:T(8,128)(2,1)S(1)}, u32[]{:S(2)}, u32[]{:S(2)}) collective-permute-start(bf16[8,16,512]{2,1,0:T(8,128)(2,1)S(1)} %get-tuple-element.52), channel_id=1, source_target_pairs={{0,13},{1,14},{2,15},{3,12},{4,9},{5,10},{6,11},{7,8},{8,5},{9,6},... | collective-permute-start | bytes 393224 | tf_op jit(solution)/shard_map/ppermute | solution.py:466
  46.7 14.5 %collective-permute-start.15 = (bf16[8,16,512]{2,1,0:T(8,128)(2,1)S(1)}, bf16[8,16,512]{2,1,0:T(8,128)(2,1)S(1)}, u32[]{:S(2)}, u32[]{:S(2)}) collective-permute-start(bf16[8,16,512]{2,1,0:T(8,128)(2,1)S(1)} %get-tuple-element.55), channel_id=1, source_target_pairs={{0,0},{1,3},{2,2},{3,1},{4,4},{5,7},{6,6},{7,5},{8,8},{9,11},{10,1... | collective-permute-start | bytes 393224 | tf_op jit(solution)/shard_map/ppermute | solution.py:466
  47.3 15.1 %collective-permute-start.16 = (bf16[8,16,512]{2,1,0:T(8,128)(2,1)S(1)}, bf16[8,16,512]{2,1,0:T(8,128)(2,1)S(1)}, u32[]{:S(2)}, u32[]{:S(2)}) collective-permute-start(bf16[8,16,512]{2,1,0:T(8,128)(2,1)S(1)} %get-tuple-element.56), channel_id=1, source_target_pairs={{0,1},{1,2},{2,3},{3,0},{4,5},{5,6},{6,7},{7,4},{8,9},{9,10},{10,1... | collective-permute-start | bytes 393224 | tf_op jit(solution)/shard_map/ppermute | solution.py:466
  52.2 16.8 %collective-permute-start.8 = (bf16[8,16,512]{2,1,0:T(8,128)(2,1)S(1)}, bf16[8,16,512]{2,1,0:T(8,128)(2,1)S(1)}, u32[]{:S(2)}, u32[]{:S(2)}) collective-permute-start(bf16[8,16,512]{2,1,0:T(8,128)(2,1)S(1)} %get-tuple-element.47), channel_id=1, source_target_pairs={{0,8},{1,11},{2,10},{3,9},{4,12},{5,15},{6,14},{7,13},{8,0},{9,3},... | collective-permute-start | bytes 393224 | tf_op jit(solution)/shard_map/ppermute | solution.py:466
  53.3 9.2 %collective-permute-start.13 = (bf16[8,16,512]{2,1,0:T(8,128)(2,1)S(1)}, bf16[8,16,512]{2,1,0:T(8,128)(2,1)S(1)}, u32[]{:S(2)}, u32[]{:S(2)}) collective-permute-start(bf16[8,16,512]{2,1,0:T(8,128)(2,1)S(1)} %get-tuple-element.53), channel_id=1, source_target_pairs={{0,4},{1,7},{2,6},{3,5},{4,0},{5,3},{6,2},{7,1},{8,12},{9,15},{10,... | collective-permute-start | bytes 393224 | tf_op jit(solution)/shard_map/ppermute | solution.py:466
  55.9 12.2 %collective-permute-start.14 = (bf16[8,16,512]{2,1,0:T(8,128)(2,1)S(1)}, bf16[8,16,512]{2,1,0:T(8,128)(2,1)S(1)}, u32[]{:S(2)}, u32[]{:S(2)}) collective-permute-start(bf16[8,16,512]{2,1,0:T(8,128)(2,1)S(1)} %get-tuple-element.54), channel_id=1, source_target_pairs={{0,5},{1,6},{2,7},{3,4},{4,1},{5,2},{6,3},{7,0},{8,13},{9,14},{10,... | collective-permute-start | bytes 393224 | tf_op jit(solution)/shard_map/ppermute | solution.py:466
  61.2 9.8 %collective-permute-start.9 = (bf16[8,16,512]{2,1,0:T(8,128)(2,1)S(1)}, bf16[8,16,512]{2,1,0:T(8,128)(2,1)S(1)}, u32[]{:S(2)}, u32[]{:S(2)}) collective-permute-start(bf16[8,16,512]{2,1,0:T(8,128)(2,1)S(1)} %get-tuple-element.48), channel_id=1, source_target_pairs={{0,9},{1,10},{2,11},{3,8},{4,13},{5,14},{6,15},{7,12},{8,1},{9,2},... | collective-permute-start | bytes 393224 | tf_op jit(solution)/shard_map/ppermute | solution.py:466
